TPU v7x, 32 devices: a whole 2x2x4 slice. The times are simulated.
32 devices in a mesh: lon: 8 (over z, y), lat: 4 (over x, core).
Axes of the slice: x: 2, y: 2, z: 4, core: 2. Of those that a mesh axis runs over, the one named last changes fastest.
Arguments:
- ocean_state: float32 [4, 8, 64, 1024], P(None, None, 'lat', 'lon'), may hold values from -5 to 5
- thickness: float32 [8, 64, 1024], P(None, 'lat', 'lon'), may hold values from 0.5 to 2
- wet_mask: int32 [8, 64, 1024], P(None, 'lat', 'lon'), may hold values 0 or 1
- mode_counts: int32 [64], P('lat'), may hold values from 1 to 64, as said below
- row_flags: int32 [64], P('lat'), may hold values from 0 to 1, as said below
Outputs:
- ocean_next: float32 [4, 8, 64, 1024], P(None, None, 'lat', 'lon')
Inputs may be any that keep to these rules, and one draw needn't show every extreme that they name: `mode_counts`: mode counts lie in the range; row 0 keeps 64. `row_flags`: only rows among the first 16 or the last 16 are flagged; the first and the last row always are.
All inputs are finite; a program needn't handle non-finite values. No bound on the sum of `wet_mask` on one device may be relied on, other than what follows from the above.
Results may differ from a plain program's by a relative error of at most 0.0003.
Values sent between devices are 32-bit elements; how exact they have to be, the bound alone decides.
No kernel may reach another device: no remote copies, remote signals or barrier semaphores. Data moves between devices by JAX's collectives and lax.ppermute only.
A program may use at most 64 MiB of HBM per device.

v0:
```python
import math

import jax
import jax.numpy as jnp
from jax import lax
from jax.sharding import PartitionSpec as P

FBAND = 16
MAXM = 64


lat_edge = 1.3
diffusion = 0.05
vertical_mix = 0.5
time_step = 0.05


def with_halo(array, sides, width, wrap):
    for axis, dim in sides:
        peers, length = (lax.axis_size(axis), array.shape[dim])
        up = [(i, (i + 1) % peers) for i in range(peers if wrap else peers - 1)]
        down = [(j, i) for i, j in up]
        last = lax.slice_in_dim(array, length - width, length, axis=dim)
        leading = lax.slice_in_dim(array, 0, width, axis=dim)
        before = lax.ppermute(last, axis, up)
        after = lax.ppermute(leading, axis, down)
        array = jnp.concatenate([before, array, after], axis=dim)
    return array


def advance(padded, u_pad, v_pad, static, centre, faces):
    thick = static[0]
    wet = static[1]
    inv_c = 1.0 / centre
    east_u = 0.5 * (u_pad[:, :, :-1] + u_pad[:, :, 1:])
    east_h = 0.5 * (thick[:, :, :-1] + thick[:, :, 1:]) * wet[:, :, :-1] * wet[:, :, 1:]
    flux_e = east_h[None] * (
        east_u[None] * 0.5 * (padded[..., :-1] + padded[..., 1:])
        - diffusion * (padded[..., 1:] - padded[..., :-1]) * inv_c[:, None]
    )
    zonal = (flux_e[..., 1:] - flux_e[..., :-1])[:, :, 1:-1, :] * inv_c[1:-1, None]
    north_v = 0.5 * (v_pad[:, :-1, :] + v_pad[:, 1:, :])
    north_h = (
        0.5 * (thick[:, :-1, :] + thick[:, 1:, :]) * wet[:, :-1, :] * wet[:, 1:, :] * faces[:, None]
    )
    flux_n = north_h[None] * (
        north_v[None] * 0.5 * (padded[:, :, :-1] + padded[:, :, 1:])
        - diffusion * (padded[:, :, 1:] - padded[:, :, :-1])
    )
    merid = (flux_n[:, :, 1:] - flux_n[:, :, :-1])[..., 1:-1] * inv_c[1:-1, None]
    inner = padded[:, :, 1:-1, 1:-1]
    wet_in = wet[:, 1:-1, 1:-1]
    thick_in = jnp.where(wet_in > 0, thick[:, 1:-1, 1:-1], 1.0)
    coupling = wet_in[:-1] * wet_in[1:] * vertical_mix / (0.5 * (thick_in[:-1] + thick_in[1:]))
    vmix = coupling[None] * (inner[:, 1:] - inner[:, :-1])
    empty = jnp.zeros_like(vmix[:, :1])
    vert = jnp.concatenate([vmix, empty], axis=1) - jnp.concatenate([empty, vmix], axis=1)
    return inner + wet_in[None] * time_step * (vert - zonal - merid) / thick_in[None]


def mode_basis(index, length, modes):
    turns = jnp.arange(modes, dtype=jnp.int32)[None, :] * index[:, None] % length
    angle = turns.astype(jnp.float32) * (2.0 * math.pi / length)
    return jnp.concatenate([jnp.cos(angle), jnp.sin(angle)], axis=1)


def mode_weights(counts, modes, length):
    order = jnp.arange(modes).astype(jnp.float32)
    keep = (order[None, :] < counts[:, None]).astype(jnp.float32)
    scale = jnp.where(order == 0, 1.0, 2.0) / length
    weights = keep * scale[None, :]
    return jnp.concatenate([weights, weights], axis=1)


def extend(fields, width):
    wider = with_halo(fields, (("lon", 3),), width, True)
    return with_halo(wider, (("lat", 2),), width, False)


def shards(ocean_state, thickness, wet_mask, mode_counts, row_flags):
    wet = wet_mask.astype(jnp.float32)
    static = jnp.stack([thickness, wet])
    levels = ocean_state.shape[1]
    rows = ocean_state.shape[2]
    lanes = ocean_state.shape[3]
    nlat = rows * lax.axis_size("lat")
    nlon = lanes * lax.axis_size("lon")
    lat_pos = lax.axis_index("lat")
    lon_pos = lax.axis_index("lon")
    joined = extend(jnp.concatenate([ocean_state, static], axis=0), 1)
    fields = joined[:4]
    fixed = joined[4:]
    index = lat_pos * rows - 1 + jnp.arange(rows + 2 * 1, dtype=jnp.int32)
    place = index.astype(jnp.float32)
    centre = jnp.cos(lat_edge * (2.0 * (place + 0.5) / nlat - 1.0))
    faces = jnp.cos(lat_edge * (2.0 * (place[:-1] + 1.0) / nlat - 1.0))
    centre, faces = (centre, faces)
    state = advance(fields, fields[2], fields[3], fixed, centre, faces)
    fields = extend(state, 1)
    state = advance(fields, fields[2], fields[3], fixed, centre, faces)
    flags = row_flags.astype(jnp.float32)
    counts = mode_counts.astype(jnp.float32)
    total = 4 * levels * FBAND
    flat = state.reshape(total, lanes)
    row_counts = jnp.broadcast_to(counts[None, None, :], (4, levels, FBAND)).reshape(total)
    index = lon_pos * lanes + jnp.arange(lanes, dtype=jnp.int32)
    basis = mode_basis(index, nlon, MAXM)
    partial_sum = jnp.dot(
        flat, basis, precision=lax.Precision.HIGHEST, preferred_element_type=jnp.float32
    )
    totals = lax.psum(partial_sum, "lon")
    smooth = jnp.dot(
        totals * mode_weights(row_counts, MAXM, nlon),
        basis.T,
        precision=lax.Precision.HIGHEST,
        preferred_element_type=jnp.float32,
    )
    smooth = smooth.reshape(4, levels, FBAND, lanes)
    filtered = state + flags[None, None, :, None] * wet[None] * (smooth - state)
    return filtered


def solution(mesh):
    in_specs = (
        P(None, None, "lat", "lon"),
        P(None, "lat", "lon"),
        P(None, "lat", "lon"),
        P("lat"),
        P("lat"),
    )
    out_specs = P(None, None, "lat", "lon")
    return jax.shard_map(shards, mesh=mesh, in_specs=in_specs, out_specs=out_specs, check_vma=False)
```

profile of v0, /device:TPU:0, one launch (start us, length us, event | category | flops | bytes accessed | tf_op | source)
XLA Modules:
  0.0 145.7 jit_solution(13678122371583939406)
XLA Ops:
  6.5 0.8 convert_bitcast_fusion
  7.4 1.1 pad_maximum_fusion.13
  8.7 6.1 %collective-permute-start.1 = (f32[6,8,16,1]{3,2,1,0:T(8,128)S(1)}, f32[6,8,16,1]{3,2,1,0:T(8,128)S(1)}, u32[]{:S(2)}, u32[]{:S(2)}) collective-permute-start(f32[6,8,16,1]{3,2,1,0:T(8,128)S(1)} %get-tuple-element.24), channel_id=1, source_target_pairs={{4,0},{8,4},{12,8},{16,12},{20,16},{24,20},{28,24},{0,28},{5,1},{9... | collective-permute-start | bytes 9224 | tf_op jit(solution)/shard_map/ppermute | solution.py:26
  14.8 0.3 fusion.35
  15.3 13.9 %collective-permute-done.1 = f32[6,8,16,1]{3,2,1,0:T(8,128)S(1)} collective-permute-done((f32[6,8,16,1]{3,2,1,0:T(8,128)S(1)}, f32[6,8,16,1]{3,2,1,0:T(8,128)S(1)}, u32[]{:S(2)}, u32[]{:S(2)}) %collective-permute-start.1) | collective-permute-done | bytes 3104 | tf_op jit(solution)/shard_map/ppermute | solution.py:26
  29.4 0.4 pad_maximum_fusion.15
  29.8 1.9 %collective-permute-start.2 = (f32[6,8,1,130]{3,2,1,0:T(1,128)S(1)}, f32[6,8,1,130]{3,2,1,0:T(1,128)S(1)}, u32[]{:S(2)}, u32[]{:S(2)}) collective-permute-start(f32[6,8,1,130]{3,2,1,0:T(1,128)S(1)} %get-tuple-element.10), channel_id=1, source_target_pairs={{0,1},{1,2},{2,3},{4,5},{5,6},{6,7},{8,9},{9,10},{10,11},{12,13},{... | collective-permute-start | bytes 74888 | tf_op jit(solution)/shard_map/ppermute | solution.py:25
  31.7 1.3 collective-permute-start.3
  33.1 2.9 %collective-permute-done.3 = f32[6,8,1,130]{3,2,1,0:T(1,128)S(1)} collective-permute-done((f32[6,8,1,130]{3,2,1,0:T(1,128)S(1)}, f32[6,8,1,130]{3,2,1,0:T(1,128)S(1)}, u32[]{:S(2)}, u32[]{:S(2)}) %collective-permute-start.3) | collective-permute-done | bytes 24992 | tf_op jit(solution)/shard_map/ppermute | solution.py:26
  36.0 0.5 pad_maximum_fusion
  36.8 0.6 subtract_multiply_fusion.2
  37.8 0.3 subtract_multiply_fusion.3
  38.8 4.8 %collective-permute-start.5 = (f32[4,8,16,1]{3,2,1,0:T(8,128)S(1)}, f32[4,8,16,1]{3,2,1,0:T(8,128)S(1)}, u32[]{:S(2)}, u32[]{:S(2)}) collective-permute-start(f32[4,8,16,1]{3,2,1,0:T(8,128)S(1)} %get-tuple-element.26), channel_id=1, source_target_pairs={{4,0},{8,4},{12,8},{16,12},{20,16},{24,20},{28,24},{0,28},{5,1},{9... | collective-permute-start | bytes 6152 | tf_op jit(solution)/shard_map/ppermute | solution.py:26
  43.6 4.8 %collective-permute-done.5 = f32[4,8,16,1]{3,2,1,0:T(8,128)S(1)} collective-permute-done((f32[4,8,16,1]{3,2,1,0:T(8,128)S(1)}, f32[4,8,16,1]{3,2,1,0:T(8,128)S(1)}, u32[]{:S(2)}, u32[]{:S(2)}) %collective-permute-start.5) | collective-permute-done | bytes 2080 | tf_op jit(solution)/shard_map/ppermute | solution.py:26
  48.4 5.9 %collective-permute-done.4 = f32[4,8,16,1]{3,2,1,0:T(8,128)S(1)} collective-permute-done((f32[4,8,16,1]{3,2,1,0:T(8,128)S(1)}, f32[4,8,16,1]{3,2,1,0:T(8,128)S(1)}, u32[]{:S(2)}, u32[]{:S(2)}) %collective-permute-start.4) | collective-permute-done | bytes 2080 | tf_op jit(solution)/shard_map/ppermute | solution.py:25
  54.6 1.3 collective-permute-start.7
  55.9 3.5 %collective-permute-start.6 = (f32[4,8,1,130]{3,2,1,0:T(1,128)S(1)}, f32[4,8,1,130]{3,2,1,0:T(1,128)S(1)}, u32[]{:S(2)}, u32[]{:S(2)}) collective-permute-start(f32[4,8,1,130]{3,2,1,0:T(1,128)S(1)} %get-tuple-element.17), channel_id=1, source_target_pairs={{0,1},{1,2},{2,3},{4,5},{5,6},{6,7},{8,9},{9,10},{10,11},{12,13},{... | collective-permute-start | bytes 49928 | tf_op jit(solution)/shard_map/ppermute | solution.py:25
  59.5 0.8 collective-permute-done.6
  60.2 0.4 pad_maximum_fusion.11
  60.7 0.6 subtract_multiply_fusion
  62.3 1.1 fusion.36
  63.7 73.0 %all-reduce.6.cloned.1.call-done = f32[512,128]{1,0:T(8,128)} async-done(((f32[512,128]{1,0:T(8,128)}), f32[512,128]{1,0:T(8,128)}) %all-reduce.6.cloned.1.call-update) | async-done | bytes 262160 | tf_op jit(solution)/shard_map/psum | solution.py:111
  136.7 1.4 fusion.14
  138.1 0.7 multiply_add_fusion
  (51 shorter events, 3.5 us)
Async XLA Ops:
  6.5 130.2 %all-reduce.6.cloned.1.call-start = ((), (), s32[]{:S(2)}) async-start(), calls=%async_computation | async-start | bytes 524288 | tf_op jit(solution)/shard_map/psum | solution.py:111
  7.4 7.7 %copy-start.3 = (s32[16]{0:T(128)S(1)}, s32[16]{0:T(128)}, u32[]{:S(2)}) copy-start(s32[16]{0:T(128)} %param.9) | copy-start | bytes 196
  7.4 7.8 %copy-start.2 = (s32[8,16,128]{2,1,0:T(8,128)S(1)}, s32[8,16,128]{2,1,0:T(8,128)}, u32[]{:S(2)}) copy-start(s32[8,16,128]{2,1,0:T(8,128)} %param.7) | copy-start | bytes 196612
  7.4 22.0 %copy-start = (f32[4,8,16,128]{3,2,1,0:T(8,128)S(1)}, f32[4,8,16,128]{3,2,1,0:T(8,128)}, u32[]{:S(2)}) copy-start(f32[4,8,16,128]{3,2,1,0:T(8,128)} %param.5) | copy-start | bytes 786436
  7.4 22.0 %copy-start.1 = (f32[8,16,128]{2,1,0:T(8,128)S(1)}, f32[8,16,128]{2,1,0:T(8,128)}, u32[]{:S(2)}) copy-start(f32[8,16,128]{2,1,0:T(8,128)} %param.6) | copy-start | bytes 196612
  8.7 20.6 %collective-permute-start.1 = (f32[6,8,16,1]{3,2,1,0:T(8,128)S(1)}, f32[6,8,16,1]{3,2,1,0:T(8,128)S(1)}, u32[]{:S(2)}, u32[]{:S(2)}) collective-permute-start(f32[6,8,16,1]{3,2,1,0:T(8,128)S(1)} %get-tuple-element.24), channel_id=1, source_target_pairs={{4,0},{8,4},{12,8},{16,12},{20,16},{24,20},{28,24},{0,28},{5,1},{9... | collective-permute-start | bytes 9224 | tf_op jit(solution)/shard_map/ppermute | solution.py:26
  14.7 14.7 %collective-permute-start = (f32[6,8,16,1]{3,2,1,0:T(8,128)S(1)}, f32[6,8,16,1]{3,2,1,0:T(8,128)S(1)}, u32[]{:S(2)}, u32[]{:S(2)}) collective-permute-start(f32[6,8,16,1]{3,2,1,0:T(8,128)S(1)} %get-tuple-element.23), channel_id=1, source_target_pairs={{0,4},{4,8},{8,12},{12,16},{16,20},{20,24},{24,28},{28,0},{1,5},{5... | collective-permute-start | bytes 9224 | tf_op jit(solution)/shard_map/ppermute | solution.py:25
  29.8 3.4 %collective-permute-start.2 = (f32[6,8,1,130]{3,2,1,0:T(1,128)S(1)}, f32[6,8,1,130]{3,2,1,0:T(1,128)S(1)}, u32[]{:S(2)}, u32[]{:S(2)}) collective-permute-start(f32[6,8,1,130]{3,2,1,0:T(1,128)S(1)} %get-tuple-element.10), channel_id=1, source_target_pairs={{0,1},{1,2},{2,3},{4,5},{5,6},{6,7},{8,9},{9,10},{10,11},{12,13},{... | collective-permute-start | bytes 74888 | tf_op jit(solution)/shard_map/ppermute | solution.py:25
  31.7 4.3 %collective-permute-start.3 = (f32[6,8,1,130]{3,2,1,0:T(1,128)S(1)}, f32[6,8,1,130]{3,2,1,0:T(1,128)S(1)}, u32[]{:S(2)}, u32[]{:S(2)}) collective-permute-start(f32[6,8,1,130]{3,2,1,0:T(1,128)S(1)} %get-tuple-element.9), channel_id=1, source_target_pairs={{1,0},{2,1},{3,2},{5,4},{6,5},{7,6},{9,8},{10,9},{11,10},{13,12},{... | collective-permute-start | bytes 74888 | tf_op jit(solution)/shard_map/ppermute | solution.py:26
  38.8 9.6 %collective-permute-start.5 = (f32[4,8,16,1]{3,2,1,0:T(8,128)S(1)}, f32[4,8,16,1]{3,2,1,0:T(8,128)S(1)}, u32[]{:S(2)}, u32[]{:S(2)}) collective-permute-start(f32[4,8,16,1]{3,2,1,0:T(8,128)S(1)} %get-tuple-element.26), channel_id=1, source_target_pairs={{4,0},{8,4},{12,8},{16,12},{20,16},{24,20},{28,24},{0,28},{5,1},{9... | collective-permute-start | bytes 6152 | tf_op jit(solution)/shard_map/ppermute | solution.py:26
  43.6 10.8 %collective-permute-start.4 = (f32[4,8,16,1]{3,2,1,0:T(8,128)S(1)}, f32[4,8,16,1]{3,2,1,0:T(8,128)S(1)}, u32[]{:S(2)}, u32[]{:S(2)}) collective-permute-start(f32[4,8,16,1]{3,2,1,0:T(8,128)S(1)} %get-tuple-element.25), channel_id=1, source_target_pairs={{0,4},{4,8},{8,12},{12,16},{16,20},{20,24},{24,28},{28,0},{1,5},{5... | collective-permute-start | bytes 6152 | tf_op jit(solution)/shard_map/ppermute | solution.py:25
  54.6 4.8 %collective-permute-start.7 = (f32[4,8,1,130]{3,2,1,0:T(1,128)S(1)}, f32[4,8,1,130]{3,2,1,0:T(1,128)S(1)}, u32[]{:S(2)}, u32[]{:S(2)}) collective-permute-start(f32[4,8,1,130]{3,2,1,0:T(1,128)S(1)} %get-tuple-element.18), channel_id=1, source_target_pairs={{1,0},{2,1},{3,2},{5,4},{6,5},{7,6},{9,8},{10,9},{11,10},{13,12},{... | collective-permute-start | bytes 49928 | tf_op jit(solution)/shard_map/ppermute | solution.py:26
  55.9 4.3 %collective-permute-start.6 = (f32[4,8,1,130]{3,2,1,0:T(1,128)S(1)}, f32[4,8,1,130]{3,2,1,0:T(1,128)S(1)}, u32[]{:S(2)}, u32[]{:S(2)}) collective-permute-start(f32[4,8,1,130]{3,2,1,0:T(1,128)S(1)} %get-tuple-element.17), channel_id=1, source_target_pairs={{0,1},{1,2},{2,3},{4,5},{5,6},{6,7},{8,9},{9,10},{10,11},{12,13},{... | collective-permute-start | bytes 49928 | tf_op jit(solution)/shard_map/ppermute | solution.py:25
  62.0 1.5 copy-start.4
Sparse Core Ops, SparseCore 0:
  63.6 73.0 all-reduce.5
where the time goes:
time: 146 us
  waiting for transfers between devices  101 us (69%)
  starting transfers between devices  18.9 us (13%)
  between operations  13.7 us (9%)
  other arithmetic  7.99 us (5%)
  matrix products  2.53 us (2%)
    psum x1, waiting for transfers between devices, shards(): totals = lax.psum(partial_sum, 'lon')  73 us
    ppermute x4, waiting for transfers between devices, with_halo(): after = lax.ppermute(leading, axis, down)  21.6 us
    ppermute x4, starting transfers between devices, with_halo(): after = lax.ppermute(leading, axis, down)  13.5 us
    ppermute x4, waiting for transfers between devices, with_halo(): before = lax.ppermute(last, axis, up)  6.89 us
    ppermute x4, starting transfers between devices, with_halo(): before = lax.ppermute(last, axis, up)  5.41 us
  transfers between devices with their start and end apart: 9, of which 7 were waited for; matrix products, arithmetic and copies ran while one was open for 1% of the time, Pallas kernels for 0%

commit v1 on v0

--- a/solution.py
+++ b/solution.py
@@ -13,19 +13,6 @@
 diffusion = 0.05
 vertical_mix = 0.5
 time_step = 0.05
-
-
-def with_halo(array, sides, width, wrap):
-    for axis, dim in sides:
-        peers, length = (lax.axis_size(axis), array.shape[dim])
-        up = [(i, (i + 1) % peers) for i in range(peers if wrap else peers - 1)]
-        down = [(j, i) for i, j in up]
-        last = lax.slice_in_dim(array, length - width, length, axis=dim)
-        leading = lax.slice_in_dim(array, 0, width, axis=dim)
-        before = lax.ppermute(last, axis, up)
-        after = lax.ppermute(leading, axis, down)
-        array = jnp.concatenate([before, array, after], axis=dim)
-    return array
 
 
 def advance(padded, u_pad, v_pad, static, centre, faces):
@@ -72,52 +59,74 @@
     return jnp.concatenate([weights, weights], axis=1)
 
 
-def extend(fields, width):
-    wider = with_halo(fields, (("lon", 3),), width, True)
-    return with_halo(wider, (("lat", 2),), width, False)
+def swap_edges(before_src, after_src, axis, wrap):
+    peers = lax.axis_size(axis)
+    up = [(i, (i + 1) % peers) for i in range(peers if wrap else peers - 1)]
+    down = [(j, i) for i, j in up]
+    return lax.ppermute(before_src, axis, up), lax.ppermute(after_src, axis, down)
+
+
+def widen(fields, width):
+    rows, lanes = fields.shape[2:]
+    below, above = swap_edges(
+        fields[:, :, rows - width :], fields[:, :, :width], "lat", False
+    )
+    fields = jnp.concatenate([below, fields, above], axis=2)
+    shape = fields.shape[:3] + (width,)
+    west, east = swap_edges(
+        fields[..., lanes - width :].reshape(-1, 128),
+        fields[..., :width].reshape(-1, 128),
+        "lon",
+        True,
+    )
+    return jnp.concatenate([west.reshape(shape), fields, east.reshape(shape)], axis=3)
 
 
 def shards(ocean_state, thickness, wet_mask, mode_counts, row_flags):
     wet = wet_mask.astype(jnp.float32)
-    static = jnp.stack([thickness, wet])
-    levels = ocean_state.shape[1]
-    rows = ocean_state.shape[2]
-    lanes = ocean_state.shape[3]
+    levels, rows, lanes = ocean_state.shape[1:]
+    lon_peers = lax.axis_size("lon")
     nlat = rows * lax.axis_size("lat")
-    nlon = lanes * lax.axis_size("lon")
+    nlon = lanes * lon_peers
     lat_pos = lax.axis_index("lat")
     lon_pos = lax.axis_index("lon")
-    joined = extend(jnp.concatenate([ocean_state, static], axis=0), 1)
+    joined = widen(
+        jnp.concatenate([ocean_state, thickness[None], wet[None]], axis=0), 2
+    )
+    place = (lat_pos * rows - 2 + jnp.arange(rows + 4, dtype=jnp.int32)).astype(
+        jnp.float32
+    )
+    centre = jnp.cos(lat_edge * (2.0 * (place + 0.5) / nlat - 1.0))
+    faces = jnp.cos(lat_edge * (2.0 * (place[:-1] + 1.0) / nlat - 1.0))
     fields = joined[:4]
     fixed = joined[4:]
-    index = lat_pos * rows - 1 + jnp.arange(rows + 2 * 1, dtype=jnp.int32)
-    place = index.astype(jnp.float32)
-    centre = jnp.cos(lat_edge * (2.0 * (place + 0.5) / nlat - 1.0))
-    faces = jnp.cos(lat_edge * (2.0 * (place[:-1] + 1.0) / nlat - 1.0))
-    centre, faces = (centre, faces)
-    state = advance(fields, fields[2], fields[3], fixed, centre, faces)
-    fields = extend(state, 1)
-    state = advance(fields, fields[2], fields[3], fixed, centre, faces)
-    flags = row_flags.astype(jnp.float32)
-    counts = mode_counts.astype(jnp.float32)
-    total = 4 * levels * FBAND
+    fields = advance(fields, fields[2], fields[3], fixed, centre, faces)
+    state = advance(
+        fields, fields[2], fields[3], fixed[:, :, 1:-1, 1:-1], centre[1:-1], faces[1:-1]
+    )
+    total = 4 * levels * rows
+    part = total // lon_peers
     flat = state.reshape(total, lanes)
-    row_counts = jnp.broadcast_to(counts[None, None, :], (4, levels, FBAND)).reshape(total)
     index = lon_pos * lanes + jnp.arange(lanes, dtype=jnp.int32)
     basis = mode_basis(index, nlon, MAXM)
     partial_sum = jnp.dot(
         flat, basis, precision=lax.Precision.HIGHEST, preferred_element_type=jnp.float32
     )
-    totals = lax.psum(partial_sum, "lon")
+    pieces = lax.all_to_all(partial_sum, "lon", 0, 0, tiled=True)
+    mine = pieces.reshape(lon_peers, part, 2 * MAXM).sum(axis=0)
+    totals = lax.all_to_all(
+        jnp.broadcast_to(mine[None], (lon_peers, part, 2 * MAXM)), "lon", 0, 0
+    ).reshape(total, 2 * MAXM)
+    counts = mode_counts.astype(jnp.float32)
+    row_counts = jnp.broadcast_to(counts[None], (4 * levels, rows)).reshape(total)
     smooth = jnp.dot(
         totals * mode_weights(row_counts, MAXM, nlon),
         basis.T,
         precision=lax.Precision.HIGHEST,
         preferred_element_type=jnp.float32,
-    )
-    smooth = smooth.reshape(4, levels, FBAND, lanes)
-    filtered = state + flags[None, None, :, None] * wet[None] * (smooth - state)
-    return filtered
+    ).reshape(state.shape)
+    flags = row_flags.astype(jnp.float32)
+    return state + flags[None, None, :, None] * wet[None] * (smooth - state)
 
 
 def solution(mesh):

time: 146 us -> 56.2 us (0.38)
  waiting for transfers between devices: 101 us -> 24.4 us
  between operations: 13.7 us -> 0.36 us
  local copies, waits for them, and re-layouts: 1.11 us -> 2.89 us
  starting transfers between devices: 18.9 us -> 17.4 us
    psum x1 -> x0, waiting for transfers between devices: 73 us -> none  [shards(): totals = lax.psum(partial_sum, 'lon')]
    ppermute x8 -> x4, waiting for transfers between devices: 28.5 us -> 6.17 us  [the longest x2 5.33 us: swap_edges(): lax.ppermute(before_src, axis, up)]
    all_to_all x0 -> x2, waiting for transfers between devices: none -> 18.2 us  [the longest x1 9.41 us: shards(): pieces = lax.all_to_all(partial_sum, 'lon', 0, 0, tiled=True)]
    ppermute x8 -> x4, starting transfers between devices: 18.9 us -> 10.4 us  [the longest x2 7.35 us: swap_edges(): lax.ppermute(after_src, axis, down)]
    all_to_all x0 -> x2, starting transfers between devices: none -> 6.96 us  [the longest x1 3.55 us: shards(): lax.all_to_all(jnp.broadcast_to(mine[None], (lon_peers, part, 2 * MAXM)),...]
  transfers between devices with their start and end apart: 9 -> 6, of which waited for: 7 -> 5; matrix products, arithmetic and copies ran while one was open for 1% -> 2% of each run, Pallas kernels for 0% -> 0%
where the time goes in v1:
time: 56.2 us; the launch traced here: 55.8 us
  waiting for transfers between devices  24.4 us (43%)
  starting transfers between devices  17.4 us (31%)
  other arithmetic  8.44 us (15%)
  local copies, waits for them, and re-layouts  2.89 us (5%)
  matrix products  2.3 us (4%)
    all_to_all x1, waiting for transfers between devices, shards(): pieces = lax.all_to_all(partial_sum, 'lon', 0, 0, tiled=True)  9.41 us
    all_to_all x1, waiting for transfers between devices, shards(): lax.all_to_all(jnp.broadcast_to(mine[None], (lon_peers, part, 2 * MAXM)),...  8.82 us
    ppermute x2, starting transfers between devices, swap_edges(): lax.ppermute(after_src, axis, down)  7.35 us
    ppermute x2, waiting for transfers between devices, swap_edges(): lax.ppermute(before_src, axis, up)  5.33 us
    all_to_all x1, starting transfers between devices, shards(): lax.all_to_all(jnp.broadcast_to(mine[None], (lon_peers, part, 2 * MAXM)),...  3.55 us
    all_to_all x1, starting transfers between devices, shards(): pieces = lax.all_to_all(partial_sum, 'lon', 0, 0, tiled=True)  3.41 us
    ppermute x2, starting transfers between devices, swap_edges(): lax.ppermute(before_src, axis, up)  3.09 us
    dot_general x1, matrix products, shards(): jnp.dot(totals * mode_weights(row_counts, MAXM, nlon), basis.T, precision...  1.16 us
  transfers between devices with their start and end apart: 6, of which 5 were waited for; matrix products, arithmetic and copies ran while one was open for 2% of the time, Pallas kernels for 0%

profile of v1, /device:TPU:0, one launch (start us, length us, event | category | flops | bytes accessed | tf_op | source)
XLA Modules:
  0.0 55.8 jit_solution(14848897138742573548)
XLA Ops:
  0.0 0.8 %convert_bitcast_fusion = f32[1,8,16,128]{3,2,1,0:T(8,128)S(1)} fusion(s32[8,16,128]{2,1,0:T(8,128)} %param.7), kind=kLoop, calls=%fused_computation.90 | loop fusion | flops 16384 | bytes 131072 | tf_op jit(solution)/shard_map/broadcast_in_dim | solution.py:94
  0.8 1.0 %pad_maximum_fusion.5 = (f32[6,8,2,128]{3,2,1,0:T(2,128)S(1)}, f32[6,8,2,128]{3,2,1,0:T(2,128)S(1)}) fusion(f32[1,8,16,128]{3,2,1,0:T(8,128)S(1)} %convert_bitcast_fusion, f32[1,8,16,128]{3,2,1,0:T(8,128)} %bitcast.32, f32[4,8,16,128]{3,2,1,0:T(8,128)} %param.5), kind=kLoop, calls=%fused_computation.100 | loop fusion | flops 49152 | bytes 491520 | tf_op jit(solution)/shard_map/slice | solution.py:72
  1.9 1.3 %collective-permute-start.1 = (f32[6,8,2,128]{3,2,1,0:T(2,128)S(1)}, f32[6,8,2,128]{3,2,1,0:T(2,128)S(1)}, u32[]{:S(2)}, u32[]{:S(2)}) collective-permute-start(f32[6,8,2,128]{3,2,1,0:T(2,128)S(1)} %get-tuple-element.26), channel_id=1, source_target_pairs={{1,0},{2,1},{3,2},{5,4},{6,5},{7,6},{9,8},{10,9},{11,10},{13,12},{... | collective-permute-start | bytes 147464 | tf_op jit(solution)/shard_map/ppermute | solution.py:66
  3.2 3.0 %collective-permute-start = (f32[6,8,2,128]{3,2,1,0:T(2,128)S(1)}, f32[6,8,2,128]{3,2,1,0:T(2,128)S(1)}, u32[]{:S(2)}, u32[]{:S(2)}) collective-permute-start(f32[6,8,2,128]{3,2,1,0:T(2,128)S(1)} %get-tuple-element.25), channel_id=1, source_target_pairs={{0,1},{1,2},{2,3},{4,5},{5,6},{6,7},{8,9},{9,10},{10,11},{12,13},{... | collective-permute-start | bytes 147464 | tf_op jit(solution)/shard_map/ppermute | solution.py:66
  6.4 0.3 fusion.46
  6.8 0.3 collective-permute-done
  7.1 1.1 %pad_maximum_fusion.1 = f32[6,8,20,128]{3,2,1,0:T(8,128)S(1)} fusion(f32[6,8,2,128]{3,2,1,0:T(2,128)S(1)} %collective-permute-done.1, f32[1,8,16,128]{3,2,1,0:T(8,128)S(1)} %convert_bitcast_fusion, f32[1,8,16,128]{3,2,1,0:T(8,128)} %bitcast.33, f32[4,8,16,128]{3,2,1,0:T(8,128)} %param.5, f32[6,8,2,128]{3,2,1,0:T(2,128)S(1)} %collective-permute-done), kind=kLoop, calls=%fused_computation.19 | loop fusion | flops 491520 | bytes 983040 | tf_op jit(solution)/shard_map/concatenate | solution.py:74
  8.6 6.1 %collective-permute-start.3 = (f32[15,128]{1,0:T(8,128)S(1)}, f32[15,128]{1,0:T(8,128)S(1)}, u32[]{:S(2)}, u32[]{:S(2)}) collective-permute-start(f32[15,128]{1,0:T(8,128)S(1)} %reshape.99), channel_id=1, source_target_pairs={{4,0},{8,4},{12,8},{16,12},{20,16},{24,20},{28,24},{0,28},{5,1},{9... | collective-permute-start | bytes 23048 | tf_op jit(solution)/shard_map/ppermute | solution.py:66
  15.2 0.8 %collective-permute-done.3 = f32[15,128]{1,0:T(8,128)S(1)} collective-permute-done((f32[15,128]{1,0:T(8,128)S(1)}, f32[15,128]{1,0:T(8,128)S(1)}, u32[]{:S(2)}, u32[]{:S(2)}) %collective-permute-start.3) | collective-permute-done | bytes 7712 | tf_op jit(solution)/shard_map/ppermute | solution.py:66
  16.2 5.0 %collective-permute-done.2 = f32[15,128]{1,0:T(8,128)S(1)} collective-permute-done((f32[15,128]{1,0:T(8,128)S(1)}, f32[15,128]{1,0:T(8,128)S(1)}, u32[]{:S(2)}, u32[]{:S(2)}) %collective-permute-start.2) | collective-permute-done | bytes 7712 | tf_op jit(solution)/shard_map/ppermute | solution.py:66
  21.5 0.7 %pad_maximum_fusion = f32[6,8,20,132]{3,2,1,0:T(8,128)S(1)} fusion(f32[6,8,20,2]{3,2,1,0:T(8,128)S(1)} %reshape.100, f32[6,8,2,128]{3,2,1,0:T(2,128)S(1)} %collective-permute-done.1, f32[1,8,16,128]{3,2,1,0:T(8,128)S(1)} %convert_bitcast_fusion, f32[1,8,16,128]{3,2,1,0:T(8,128)S(1)} %bitcast.34, f32[4,8,16,128]{3,2,1,0:T(8,128)S(1)} %copy-done, ...), kind=kLoop, calls=%fused_computation | loop fusion | flops 760320 | bytes 1013760 | tf_op jit(solution)/shard_map/concatenate | solution.py:82
  23.6 0.3 subtract_multiply_fusion.3
  23.9 0.3 fusion.52
  24.3 0.4 fusion.9
  24.8 0.8 %fusion.6 = f32[4,8,18,130]{3,2,1,0:T(8,128)S(1)} fusion(f32[4,8,18,132]{3,2,1,0:T(8,128)S(1)} %get-tuple-element.22, f32[4,8,18,132]{3,2,1,0:T(8,128)S(1)} %get-tuple-element.21, f32[4,8,20,130]{3,2,1,0:T(8,128)S(1)} %get-tuple-element.20, f32[4,8,20,130]{3,2,1,0:T(8,128)S(1)} %get-tuple-element.19, f32[6,8,20,132]{3,2,1,0:T(8,128)S(1)} %pad_maximum_fusion, ...), kind=kLoop, calls=%fused_computation.9 | loop fusion | flops 748800 | bytes 2209032 | tf_op jit(solution)/shard_map/add | solution.py:45
  26.2 0.3 subtract_multiply_fusion.1
  26.9 0.3 fusion.14
  27.3 1.1 %fusion.37 = f32[8,64,128]{2,1,0:T(8,128)} fusion(f32[8,64,128]{2,1,0:T(8,128)S(1)} %bitcast.30, f32[128,64]{1,0:T(8,128)S(1)} %get-tuple-element.32, f32[128,64]{1,0:T(8,128)S(1)} %get-tuple-element.31), kind=kOutput, calls=%fused_computation.85 | convolution fusion | flops 100679680 | bytes 589824 | tf_op jit(solution)/shard_map/dot_general | solution.py:112
  28.4 3.4 %all-to-all-start = ((f32[8,64,128]{2,1,0:T(8,128)}), f32[8,64,128]{2,1,0:T(8,128)S(1)}, u32[]{:S(2)}, u32[]{:S(2)}) async-start(f32[8,64,128]{2,1,0:T(8,128)} %fusion.37), calls=%async_computation | async-start | bytes 524288 | tf_op jit(solution)/shard_map/all_to_all | solution.py:115
  31.9 9.4 %all-to-all-done = f32[8,64,128]{2,1,0:T(8,128)S(1)} async-done(((f32[8,64,128]{2,1,0:T(8,128)}), f32[8,64,128]{2,1,0:T(8,128)S(1)}, u32[]{:S(2)}, u32[]{:S(2)}) %all-to-all-start) | async-done | bytes 262176 | tf_op jit(solution)/shard_map/all_to_all | solution.py:115
  41.3 0.7 %broadcast_in_dim.24 = f32[8,64,128]{2,1,0:T(8,128)} broadcast(f32[64,128]{1,0:T(8,128)S(1)} %reduce_sum.9), dimensions={1,2} | broadcast | bytes 294912 | tf_op jit(solution)/shard_map/broadcast_in_dim | solution.py:118
  42.0 3.6 %all-to-all-start.1 = ((f32[8,64,128]{2,1,0:T(8,128)}), f32[8,64,128]{2,1,0:T(8,128)S(1)}, u32[]{:S(2)}, u32[]{:S(2)}) async-start(f32[8,64,128]{2,1,0:T(8,128)} %broadcast_in_dim.24), calls=%async_computation.1 | async-start | bytes 524288 | tf_op jit(solution)/shard_map/all_to_all | solution.py:117
  45.8 8.8 %all-to-all-done.1 = f32[8,64,128]{2,1,0:T(8,128)S(1)} async-done(((f32[8,64,128]{2,1,0:T(8,128)}), f32[8,64,128]{2,1,0:T(8,128)S(1)}, u32[]{:S(2)}, u32[]{:S(2)}) %all-to-all-start.1) | async-done | bytes 262176 | tf_op jit(solution)/shard_map/all_to_all | solution.py:117
  54.6 1.2 %fusion.1 = f32[4,8,16,128]{3,2,1,0:T(8,128)} fusion(f32[4,8,16,128]{3,2,1,0:T(8,128)S(1)} %fusion.14, f32[4,8,16,128]{3,2,1,0:T(8,128)S(1)} %bitcast.31, f32[4,8,16,64]{3,2,1,0:T(8,128)S(1)} %compare_select_fusion, f32[8,16,128]{2,1,0:T(8,128)S(1)} %convert_multiply_fusion, f32[128,64]{1,0:T(8,128)S(1)} %get-tuple-element.32, ...), kind=kOutput, calls=%fused_computation.3 | convolution fusion | flops 101007360 | bytes 1048576 | tf_op jit(solution)/shard_map/dot_general | solution.py:122
  (52 shorter events, 4.2 us)
Async XLA Ops:
  1.9 4.9 %collective-permute-start.1 = (f32[6,8,2,128]{3,2,1,0:T(2,128)S(1)}, f32[6,8,2,128]{3,2,1,0:T(2,128)S(1)}, u32[]{:S(2)}, u32[]{:S(2)}) collective-permute-start(f32[6,8,2,128]{3,2,1,0:T(2,128)S(1)} %get-tuple-element.26), channel_id=1, source_target_pairs={{1,0},{2,1},{3,2},{5,4},{6,5},{7,6},{9,8},{10,9},{11,10},{13,12},{... | collective-permute-start | bytes 147464 | tf_op jit(solution)/shard_map/ppermute | solution.py:66
  3.2 3.9 %collective-permute-start = (f32[6,8,2,128]{3,2,1,0:T(2,128)S(1)}, f32[6,8,2,128]{3,2,1,0:T(2,128)S(1)}, u32[]{:S(2)}, u32[]{:S(2)}) collective-permute-start(f32[6,8,2,128]{3,2,1,0:T(2,128)S(1)} %get-tuple-element.25), channel_id=1, source_target_pairs={{0,1},{1,2},{2,3},{4,5},{5,6},{6,7},{8,9},{9,10},{10,11},{12,13},{... | collective-permute-start | bytes 147464 | tf_op jit(solution)/shard_map/ppermute | solution.py:66
  8.4 13.1 %copy-start = (f32[4,8,16,128]{3,2,1,0:T(8,128)S(1)}, f32[4,8,16,128]{3,2,1,0:T(8,128)}, u32[]{:S(2)}) copy-start(f32[4,8,16,128]{3,2,1,0:T(8,128)} %param.5) | copy-start | bytes 786436
  8.4 13.1 %copy-start.1 = (f32[8,16,128]{2,1,0:T(8,128)S(1)}, f32[8,16,128]{2,1,0:T(8,128)}, u32[]{:S(2)}) copy-start(f32[8,16,128]{2,1,0:T(8,128)} %param.6) | copy-start | bytes 196612
  8.6 7.4 %collective-permute-start.3 = (f32[15,128]{1,0:T(8,128)S(1)}, f32[15,128]{1,0:T(8,128)S(1)}, u32[]{:S(2)}, u32[]{:S(2)}) collective-permute-start(f32[15,128]{1,0:T(8,128)S(1)} %reshape.99), channel_id=1, source_target_pairs={{4,0},{8,4},{12,8},{16,12},{20,16},{24,20},{28,24},{0,28},{5,1},{9... | collective-permute-start | bytes 23048 | tf_op jit(solution)/shard_map/ppermute | solution.py:66
  14.9 6.4 %collective-permute-start.2 = (f32[15,128]{1,0:T(8,128)S(1)}, f32[15,128]{1,0:T(8,128)S(1)}, u32[]{:S(2)}, u32[]{:S(2)}) collective-permute-start(f32[15,128]{1,0:T(8,128)S(1)} %reshape.97), channel_id=1, source_target_pairs={{0,4},{4,8},{8,12},{12,16},{16,20},{20,24},{24,28},{28,0},{1,5},{5... | collective-permute-start | bytes 23048 | tf_op jit(solution)/shard_map/ppermute | solution.py:66
  27.3 18.3 %copy-start.3 = (s32[16]{0:T(128)S(1)}, s32[16]{0:T(128)}, u32[]{:S(2)}) copy-start(s32[16]{0:T(128)} %param.8) | copy-start | bytes 196
  27.3 18.3 %copy-start.4 = (s32[16]{0:T(128)S(1)}, s32[16]{0:T(128)}, u32[]{:S(2)}) copy-start(s32[16]{0:T(128)} %param.9) | copy-start | bytes 196
  27.3 18.3 %copy-start.2 = (s32[8,16,128]{2,1,0:T(8,128)S(1)}, s32[8,16,128]{2,1,0:T(8,128)}, u32[]{:S(2)}) copy-start(s32[8,16,128]{2,1,0:T(8,128)} %param.7) | copy-start | bytes 196612
  28.4 12.8 %all-to-all-start = ((f32[8,64,128]{2,1,0:T(8,128)}), f32[8,64,128]{2,1,0:T(8,128)S(1)}, u32[]{:S(2)}, u32[]{:S(2)}) async-start(f32[8,64,128]{2,1,0:T(8,128)} %fusion.37), calls=%async_computation | async-start | bytes 524288 | tf_op jit(solution)/shard_map/all_to_all | solution.py:115
  42.0 12.6 %all-to-all-start.1 = ((f32[8,64,128]{2,1,0:T(8,128)}), f32[8,64,128]{2,1,0:T(8,128)S(1)}, u32[]{:S(2)}, u32[]{:S(2)}) async-start(f32[8,64,128]{2,1,0:T(8,128)} %broadcast_in_dim.24), calls=%async_computation.1 | async-start | bytes 524288 | tf_op jit(solution)/shard_map/all_to_all | solution.py:117

commit v2 on v1

--- a/solution.py
+++ b/solution.py
@@ -2,6 +2,7 @@
 
 import jax
 import jax.numpy as jnp
+import numpy as np
 from jax import lax
 from jax.sharding import PartitionSpec as P
 
@@ -45,10 +46,10 @@
     return inner + wet_in[None] * time_step * (vert - zonal - merid) / thick_in[None]
 
 
-def mode_basis(index, length, modes):
-    turns = jnp.arange(modes, dtype=jnp.int32)[None, :] * index[:, None] % length
-    angle = turns.astype(jnp.float32) * (2.0 * math.pi / length)
-    return jnp.concatenate([jnp.cos(angle), jnp.sin(angle)], axis=1)
+def mode_basis(length, modes):
+    turns = np.arange(modes)[None, :] * np.arange(length)[:, None] % length
+    angle = turns * (2.0 * math.pi / length)
+    return np.concatenate([np.cos(angle), np.sin(angle)], axis=1).astype(np.float32)
 
 
 def mode_weights(counts, modes, length):
@@ -59,9 +60,9 @@
     return jnp.concatenate([weights, weights], axis=1)
 
 
-def swap_edges(before_src, after_src, axis, wrap):
+def swap_edges(before_src, after_src, axis):
     peers = lax.axis_size(axis)
-    up = [(i, (i + 1) % peers) for i in range(peers if wrap else peers - 1)]
+    up = [(i, (i + 1) % peers) for i in range(peers)]
     down = [(j, i) for i, j in up]
     return lax.ppermute(before_src, axis, up), lax.ppermute(after_src, axis, down)
 
@@ -69,15 +70,17 @@
 def widen(fields, width):
     rows, lanes = fields.shape[2:]
     below, above = swap_edges(
-        fields[:, :, rows - width :], fields[:, :, :width], "lat", False
+        fields[:, :, rows - width :], fields[:, :, :width], "lat"
     )
+    lat_pos = lax.axis_index("lat")
+    below = jnp.where(lat_pos > 0, below, 0.0)
+    above = jnp.where(lat_pos < lax.axis_size("lat") - 1, above, 0.0)
     fields = jnp.concatenate([below, fields, above], axis=2)
     shape = fields.shape[:3] + (width,)
     west, east = swap_edges(
         fields[..., lanes - width :].reshape(-1, 128),
         fields[..., :width].reshape(-1, 128),
         "lon",
-        True,
     )
     return jnp.concatenate([west.reshape(shape), fields, east.reshape(shape)], axis=3)
 
@@ -89,7 +92,6 @@
     nlat = rows * lax.axis_size("lat")
     nlon = lanes * lon_peers
     lat_pos = lax.axis_index("lat")
-    lon_pos = lax.axis_index("lon")
     joined = widen(
         jnp.concatenate([ocean_state, thickness[None], wet[None]], axis=0), 2
     )
@@ -106,25 +108,31 @@
     )
     total = 4 * levels * rows
     part = total // lon_peers
-    flat = state.reshape(total, lanes)
-    index = lon_pos * lanes + jnp.arange(lanes, dtype=jnp.int32)
-    basis = mode_basis(index, nlon, MAXM)
-    partial_sum = jnp.dot(
-        flat, basis, precision=lax.Precision.HIGHEST, preferred_element_type=jnp.float32
+    basis = jnp.asarray(mode_basis(nlon, MAXM)).reshape(lon_peers, lanes, 2 * MAXM)
+    circles = lax.all_to_all(
+        state.reshape(lon_peers, part, lanes), "lon", 0, 0, tiled=True
     )
-    pieces = lax.all_to_all(partial_sum, "lon", 0, 0, tiled=True)
-    mine = pieces.reshape(lon_peers, part, 2 * MAXM).sum(axis=0)
-    totals = lax.all_to_all(
-        jnp.broadcast_to(mine[None], (lon_peers, part, 2 * MAXM)), "lon", 0, 0
-    ).reshape(total, 2 * MAXM)
-    counts = mode_counts.astype(jnp.float32)
-    row_counts = jnp.broadcast_to(counts[None], (4 * levels, rows)).reshape(total)
-    smooth = jnp.dot(
-        totals * mode_weights(row_counts, MAXM, nlon),
-        basis.T,
+    totals = jnp.einsum(
+        "opi,oim->pm",
+        circles,
+        basis,
         precision=lax.Precision.HIGHEST,
         preferred_element_type=jnp.float32,
-    ).reshape(state.shape)
+    )
+    counts = mode_counts.astype(jnp.float32)
+    row_counts = lax.dynamic_slice(
+        jnp.broadcast_to(counts[None], (4 * levels, rows)).reshape(total),
+        (lax.axis_index("lon") * part,),
+        (part,),
+    )
+    smooth = jnp.einsum(
+        "pm,oim->opi",
+        totals * mode_weights(row_counts, MAXM, nlon),
+        basis,
+        precision=lax.Precision.HIGHEST,
+        preferred_element_type=jnp.float32,
+    )
+    smooth = lax.all_to_all(smooth, "lon", 0, 0, tiled=True).reshape(state.shape)
     flags = row_flags.astype(jnp.float32)
     return state + flags[None, None, :, None] * wet[None] * (smooth - state)
 

time: 56.2 us -> 54.4 us (0.968)
  starting transfers between devices: 17.4 us -> 13.9 us
  other arithmetic: 8.44 us -> 10.5 us
  waiting for transfers between devices: 24.4 us -> 25.1 us
    ppermute x2, starting transfers between devices: 3.09 us -> 0.06 us  [swap_edges(): lax.ppermute(before_src, axis, up)]
    all_to_all x2, waiting for transfers between devices: 18.2 us -> 15.9 us  [the longest x1 8.05 us: shards(): lax.all_to_all(smooth, 'lon', 0, 0, tiled=True).reshape(state.shape)]
    ppermute x2, waiting for transfers between devices: 0.84 us -> 2.73 us  [swap_edges(): lax.ppermute(after_src, axis, down)]
    add x1, other arithmetic: 0.01 us -> 1.69 us  [shards(): return state + flags[None, None, :, None] * wet[None] * (smooth - state)]
    ppermute x2, waiting for transfers between devices: 5.33 us -> 6.43 us  [swap_edges(): lax.ppermute(before_src, axis, up)]
    broadcast_in_dim x1, local copies, waits for them, and re-layouts: 0.72 us -> 0.01 us  [shards(): jnp.broadcast_to(counts[None], (4 * levels, rows)).reshape(total)]
    add x2, other arithmetic: 1.14 us -> 1.83 us  [advance(): inner + wet_in[None] * time_step * (vert - zonal - merid) / thick_in[None]]
  transfers between devices with their start and end apart: 6 -> 6, of which waited for: 5 -> 6; matrix products, arithmetic and copies ran while one was open for 2% -> 2% of each run, Pallas kernels for 0% -> 0%
where the time goes in v2:
time: 54.4 us; the launch traced here: 54 us
  waiting for transfers between devices  25.1 us (46%)
  starting transfers between devices  13.9 us (26%)
  other arithmetic  10.5 us (19%)
  local copies, waits for them, and re-layouts  2.33 us (4%)
  matrix products  1.83 us (3%)
    all_to_all x1, waiting for transfers between devices, shards(): lax.all_to_all(smooth, 'lon', 0, 0, tiled=True).reshape(state.shape)  8.05 us
    all_to_all x1, waiting for transfers between devices, shards(): lax.all_to_all(state.reshape(lon_peers, part, lanes), 'lon', 0, 0, tiled=...  7.86 us
    ppermute x2, starting transfers between devices, swap_edges(): lax.ppermute(after_src, axis, down)  7.04 us
    ppermute x2, waiting for transfers between devices, swap_edges(): lax.ppermute(before_src, axis, up)  6.43 us
    all_to_all x1, starting transfers between devices, shards(): lax.all_to_all(state.reshape(lon_peers, part, lanes), 'lon', 0, 0, tiled=...  3.41 us
    all_to_all x1, starting transfers between devices, shards(): lax.all_to_all(smooth, 'lon', 0, 0, tiled=True).reshape(state.shape)  3.41 us
    ppermute x2, waiting for transfers between devices, swap_edges(): lax.ppermute(after_src, axis, down)  2.73 us
    add x2, other arithmetic, advance(): inner + wet_in[None] * time_step * (vert - zonal - merid) / thick_in[None]  1.83 us
  transfers between devices with their start and end apart: 6, of which 6 were waited for; matrix products, arithmetic and copies ran while one was open for 2% of the time, Pallas kernels for 0%

profile of v2, /device:TPU:0, one launch (start us, length us, event | category | flops | bytes accessed | tf_op | source)
XLA Modules:
  0.0 54.0 jit_solution(338638493062143463)
XLA Ops:
  0.0 0.8 %convert_bitcast_fusion = f32[1,8,16,128]{3,2,1,0:T(8,128)S(1)} fusion(s32[8,16,128]{2,1,0:T(8,128)} %param.8), kind=kLoop, calls=%fused_computation.76 | loop fusion | flops 16384 | bytes 131072 | tf_op jit(solution)/shard_map/broadcast_in_dim | solution.py:96
  0.8 1.0 %pad_maximum_fusion.4 = (f32[6,8,2,128]{3,2,1,0:T(2,128)S(1)}, f32[6,8,2,128]{3,2,1,0:T(2,128)S(1)}) fusion(f32[1,8,16,128]{3,2,1,0:T(8,128)S(1)} %convert_bitcast_fusion, f32[1,8,16,128]{3,2,1,0:T(8,128)} %bitcast.36, f32[4,8,16,128]{3,2,1,0:T(8,128)} %param.6), kind=kLoop, calls=%fused_computation.85 | loop fusion | flops 49152 | bytes 491520 | tf_op jit(solution)/shard_map/slice | solution.py:73
  1.9 2.4 %collective-permute-start.1 = (f32[6,8,2,128]{3,2,1,0:T(2,128)S(1)}, f32[6,8,2,128]{3,2,1,0:T(2,128)S(1)}, u32[]{:S(2)}, u32[]{:S(2)}) collective-permute-start(f32[6,8,2,128]{3,2,1,0:T(2,128)S(1)} %get-tuple-element.26), channel_id=1, source_target_pairs={{1,0},{2,1},{3,2},{0,3},{5,4},{6,5},{7,6},{4,7},{9,8},{10,9},{11,1... | collective-permute-start | bytes 147464 | tf_op jit(solution)/shard_map/ppermute | solution.py:67
  4.5 1.9 %collective-permute-done.1 = f32[6,8,2,128]{3,2,1,0:T(2,128)S(1)} collective-permute-done((f32[6,8,2,128]{3,2,1,0:T(2,128)S(1)}, f32[6,8,2,128]{3,2,1,0:T(2,128)S(1)}, u32[]{:S(2)}, u32[]{:S(2)}) %collective-permute-start.1) | collective-permute-done | bytes 49184 | tf_op jit(solution)/shard_map/ppermute | solution.py:67
  6.4 1.4 %collective-permute-done = f32[6,8,2,128]{3,2,1,0:T(2,128)S(1)} collective-permute-done((f32[6,8,2,128]{3,2,1,0:T(2,128)S(1)}, f32[6,8,2,128]{3,2,1,0:T(2,128)S(1)}, u32[]{:S(2)}, u32[]{:S(2)}) %collective-permute-start) | collective-permute-done | bytes 49184 | tf_op jit(solution)/shard_map/ppermute | solution.py:67
  7.9 1.1 %pad_maximum_fusion.1 = f32[6,8,20,128]{3,2,1,0:T(8,128)S(1)} fusion(f32[6,8,2,128]{3,2,1,0:T(2,128)S(1)} %broadcast_select_fusion, f32[1,8,16,128]{3,2,1,0:T(8,128)S(1)} %convert_bitcast_fusion, f32[1,8,16,128]{3,2,1,0:T(8,128)} %bitcast.37, f32[4,8,16,128]{3,2,1,0:T(8,128)} %param.6, f32[6,8,2,128]{3,2,1,0:T(2,128)S(1)} %broadcast_select_fusion.1), kind=kLoop, calls=%fused_computation.20 | loop fusion | flops 491520 | bytes 983040 | tf_op jit(solution)/shard_map/concatenate | solution.py:78
  8.9 0.2 fusion.39
  9.4 4.6 %collective-permute-start.3 = (f32[15,128]{1,0:T(8,128)S(1)}, f32[15,128]{1,0:T(8,128)S(1)}, u32[]{:S(2)}, u32[]{:S(2)}) collective-permute-start(f32[15,128]{1,0:T(8,128)S(1)} %reshape.78), channel_id=1, source_target_pairs={{4,0},{8,4},{12,8},{16,12},{20,16},{24,20},{28,24},{0,28},{5,1},{9... | collective-permute-start | bytes 23048 | tf_op jit(solution)/shard_map/ppermute | solution.py:67
  14.5 0.8 %collective-permute-done.3 = f32[15,128]{1,0:T(8,128)S(1)} collective-permute-done((f32[15,128]{1,0:T(8,128)S(1)}, f32[15,128]{1,0:T(8,128)S(1)}, u32[]{:S(2)}, u32[]{:S(2)}) %collective-permute-start.3) | collective-permute-done | bytes 7712 | tf_op jit(solution)/shard_map/ppermute | solution.py:67
  15.6 5.0 %collective-permute-done.2 = f32[15,128]{1,0:T(8,128)S(1)} collective-permute-done((f32[15,128]{1,0:T(8,128)S(1)}, f32[15,128]{1,0:T(8,128)S(1)}, u32[]{:S(2)}, u32[]{:S(2)}) %collective-permute-start.2) | collective-permute-done | bytes 7712 | tf_op jit(solution)/shard_map/ppermute | solution.py:67
  20.8 0.7 %pad_maximum_fusion = f32[6,8,20,132]{3,2,1,0:T(8,128)S(1)} fusion(f32[6,8,20,2]{3,2,1,0:T(8,128)S(1)} %reshape.79, f32[6,8,2,128]{3,2,1,0:T(2,128)S(1)} %broadcast_select_fusion, f32[1,8,16,128]{3,2,1,0:T(8,128)S(1)} %convert_bitcast_fusion, f32[1,8,16,128]{3,2,1,0:T(8,128)S(1)} %bitcast.38, f32[4,8,16,128]{3,2,1,0:T(8,128)S(1)} %copy-done, ...), kind=kLoop, calls=%fused_computation | loop fusion | flops 760320 | bytes 1013760 | tf_op jit(solution)/shard_map/concatenate | solution.py:85
  22.9 0.3 subtract_multiply_fusion.3
  23.2 0.3 fusion.37
  23.7 0.4 fusion.9
  24.1 0.8 %fusion.6 = f32[4,8,18,130]{3,2,1,0:T(8,128)S(1)} fusion(f32[4,8,18,132]{3,2,1,0:T(8,128)S(1)} %get-tuple-element.22, f32[4,8,18,132]{3,2,1,0:T(8,128)S(1)} %get-tuple-element.21, f32[4,8,20,130]{3,2,1,0:T(8,128)S(1)} %get-tuple-element.20, f32[4,8,20,130]{3,2,1,0:T(8,128)S(1)} %get-tuple-element.19, f32[6,8,20,132]{3,2,1,0:T(8,128)S(1)} %pad_maximum_fusion, ...), kind=kLoop, calls=%fused_computation.10 | loop fusion | flops 748800 | bytes 2209032 | tf_op jit(solution)/shard_map/add | solution.py:46
  25.5 0.3 subtract_multiply_fusion.1
  26.3 1.0 %fusion.14 = f32[4,8,16,128]{3,2,1,0:T(8,128)} fusion(f32[4,8,16,130]{3,2,1,0:T(8,128)S(1)} %get-tuple-element.18, f32[4,8,16,130]{3,2,1,0:T(8,128)S(1)} %get-tuple-element.17, f32[4,8,18,128]{3,2,1,0:T(8,128)S(1)} %get-tuple-element.14, f32[4,8,18,128]{3,2,1,0:T(8,128)S(1)} %get-tuple-element.13, f32[4,8,18,130]{3,2,1,0:T(8,128)S(1)} %fusion.6, ...), kind=kLoop, calls=%fused_computation.26 | loop fusion | flops 655360 | bytes 1933376 | tf_op jit(solution)/shard_map/add | solution.py:46
  27.3 3.4 %all-to-all-start = ((f32[8,64,128]{2,1,0:T(8,128)}), f32[8,64,128]{2,1,0:T(8,128)S(1)}, u32[]{:S(2)}, u32[]{:S(2)}) async-start(f32[8,64,128]{2,1,0:T(8,128)} %bitcast.10), calls=%async_computation | async-start | bytes 524288 | tf_op jit(solution)/shard_map/all_to_all | solution.py:112
  31.0 7.9 %all-to-all-done = f32[8,64,128]{2,1,0:T(8,128)S(1)} async-done(((f32[8,64,128]{2,1,0:T(8,128)}), f32[8,64,128]{2,1,0:T(8,128)S(1)}, u32[]{:S(2)}, u32[]{:S(2)}) %all-to-all-start) | async-done | bytes 262176 | tf_op jit(solution)/shard_map/all_to_all | solution.py:112
  38.9 0.4 fusion.1
  39.3 1.4 %convolution_bitcast_fusion = f32[8,64,128]{2,1,0:T(8,128)} fusion(f32[64,128,1]{1,0,2:T(8,128)S(1)} %fusion.1, f32[8,128,128]{2,1,0:T(8,128)S(1)} %copy-done.1), kind=kOutput, calls=%fused_computation.1 | convolution fusion | flops 100663296 | bytes 819200 | tf_op jit(solution)/shard_map/pm,oim->opi/dot_general | solution.py:128
  40.7 3.4 %all-to-all-start.1 = ((f32[8,64,128]{2,1,0:T(8,128)}), f32[8,64,128]{2,1,0:T(8,128)S(1)}, u32[]{:S(2)}, u32[]{:S(2)}) async-start(f32[8,64,128]{2,1,0:T(8,128)} %convolution_bitcast_fusion), calls=%async_computation.1 | async-start | bytes 524288 | tf_op jit(solution)/shard_map/all_to_all | solution.py:135
  44.2 8.1 %all-to-all-done.1 = f32[8,64,128]{2,1,0:T(8,128)S(1)} async-done(((f32[8,64,128]{2,1,0:T(8,128)}), f32[8,64,128]{2,1,0:T(8,128)S(1)}, u32[]{:S(2)}, u32[]{:S(2)}) %all-to-all-start.1) | async-done | bytes 262176 | tf_op jit(solution)/shard_map/all_to_all | solution.py:135
  52.3 1.7 %multiply_add_fusion = f32[4,8,16,128]{3,2,1,0:T(8,128)} fusion(f32[4,8,16,128]{3,2,1,0:T(8,128)} %fusion.14, f32[4,8,16,128]{3,2,1,0:T(8,128)S(1)} %bitcast.35, f32[8,16,128]{2,1,0:T(8,128)S(1)} %convert_multiply_fusion), kind=kLoop, calls=%fused_computation.30 | loop fusion | flops 196608 | bytes 851968 | tf_op jit(solution)/shard_map/add | solution.py:137
  (56 shorter events, 4.2 us)
Async XLA Ops:
  1.9 4.5 %collective-permute-start.1 = (f32[6,8,2,128]{3,2,1,0:T(2,128)S(1)}, f32[6,8,2,128]{3,2,1,0:T(2,128)S(1)}, u32[]{:S(2)}, u32[]{:S(2)}) collective-permute-start(f32[6,8,2,128]{3,2,1,0:T(2,128)S(1)} %get-tuple-element.26), channel_id=1, source_target_pairs={{1,0},{2,1},{3,2},{0,3},{5,4},{6,5},{7,6},{4,7},{9,8},{10,9},{11,1... | collective-permute-start | bytes 147464 | tf_op jit(solution)/shard_map/ppermute | solution.py:67
  4.3 3.5 %collective-permute-start = (f32[6,8,2,128]{3,2,1,0:T(2,128)S(1)}, f32[6,8,2,128]{3,2,1,0:T(2,128)S(1)}, u32[]{:S(2)}, u32[]{:S(2)}) collective-permute-start(f32[6,8,2,128]{3,2,1,0:T(2,128)S(1)} %get-tuple-element.25), channel_id=1, source_target_pairs={{0,1},{1,2},{2,3},{3,0},{4,5},{5,6},{6,7},{7,4},{8,9},{9,10},{10,1... | collective-permute-start | bytes 147464 | tf_op jit(solution)/shard_map/ppermute | solution.py:67
  9.2 11.6 %copy-start = (f32[4,8,16,128]{3,2,1,0:T(8,128)S(1)}, f32[4,8,16,128]{3,2,1,0:T(8,128)}, u32[]{:S(2)}) copy-start(f32[4,8,16,128]{3,2,1,0:T(8,128)} %param.6) | copy-start | bytes 786436
  9.2 11.6 %copy-start.2 = (f32[8,16,128]{2,1,0:T(8,128)S(1)}, f32[8,16,128]{2,1,0:T(8,128)}, u32[]{:S(2)}) copy-start(f32[8,16,128]{2,1,0:T(8,128)} %param.7) | copy-start | bytes 196612
  9.4 6.0 %collective-permute-start.3 = (f32[15,128]{1,0:T(8,128)S(1)}, f32[15,128]{1,0:T(8,128)S(1)}, u32[]{:S(2)}, u32[]{:S(2)}) collective-permute-start(f32[15,128]{1,0:T(8,128)S(1)} %reshape.78), channel_id=1, source_target_pairs={{4,0},{8,4},{12,8},{16,12},{20,16},{24,20},{28,24},{0,28},{5,1},{9... | collective-permute-start | bytes 23048 | tf_op jit(solution)/shard_map/ppermute | solution.py:67
  14.2 6.4 %collective-permute-start.2 = (f32[15,128]{1,0:T(8,128)S(1)}, f32[15,128]{1,0:T(8,128)S(1)}, u32[]{:S(2)}, u32[]{:S(2)}) collective-permute-start(f32[15,128]{1,0:T(8,128)S(1)} %reshape.76), channel_id=1, source_target_pairs={{0,4},{4,8},{8,12},{12,16},{16,20},{20,24},{24,28},{28,0},{1,5},{5... | collective-permute-start | bytes 23048 | tf_op jit(solution)/shard_map/ppermute | solution.py:67
  26.3 4.5 %copy-start.4 = (s32[16]{0:T(128)S(1)}, s32[16]{0:T(128)}, u32[]{:S(2)}) copy-start(s32[16]{0:T(128)} %param.9) | copy-start | bytes 196
  26.3 12.6 %copy-start.1 = (f32[8,128,128]{2,1,0:T(8,128)S(1)}, f32[8,128,128]{2,1,0:T(8,128)}, u32[]{:S(2)}) copy-start(f32[8,128,128]{2,1,0:T(8,128)} %constant.91) | copy-start | bytes 1572868
  27.3 11.6 %all-to-all-start = ((f32[8,64,128]{2,1,0:T(8,128)}), f32[8,64,128]{2,1,0:T(8,128)S(1)}, u32[]{:S(2)}, u32[]{:S(2)}) async-start(f32[8,64,128]{2,1,0:T(8,128)} %bitcast.10), calls=%async_computation | async-start | bytes 524288 | tf_op jit(solution)/shard_map/all_to_all | solution.py:112
  30.7 13.4 %copy-start.5 = (s32[16]{0:T(128)S(1)}, s32[16]{0:T(128)}, u32[]{:S(2)}) copy-start(s32[16]{0:T(128)} %param.10) | copy-start | bytes 196
  30.7 13.4 %copy-start.3 = (s32[8,16,128]{2,1,0:T(8,128)S(1)}, s32[8,16,128]{2,1,0:T(8,128)}, u32[]{:S(2)}) copy-start(s32[8,16,128]{2,1,0:T(8,128)} %param.8) | copy-start | bytes 196612
  40.7 11.6 %all-to-all-start.1 = ((f32[8,64,128]{2,1,0:T(8,128)}), f32[8,64,128]{2,1,0:T(8,128)S(1)}, u32[]{:S(2)}, u32[]{:S(2)}) async-start(f32[8,64,128]{2,1,0:T(8,128)} %convolution_bitcast_fusion), calls=%async_computation.1 | async-start | bytes 524288 | tf_op jit(solution)/shard_map/all_to_all | solution.py:135

commit v3 on v2

v3 whole, which is shorter than its diff:
```python
import math

import jax
import jax.numpy as jnp
import numpy as np
from jax import lax
from jax.experimental import pallas as pl
from jax.experimental.pallas import tpu as pltpu
from jax.sharding import PartitionSpec as P

MAXM = 64
LANES = 128
GROUP = 16


lat_edge = 1.3
diffusion = 0.05
vertical_mix = 0.5
time_step = 0.05


def roll(x, shift, axis):
    shift %= x.shape[axis]
    return pltpu.roll(x, shift, axis) if shift else x


def east(x):
    return roll(x, -1, 1)


def west(x):
    return roll(x, 1, 1)


def north(x):
    return roll(x, -1, 0)


def south(x):
    return roll(x, 1, 0)


def lane_of(shape):
    return lax.broadcasted_iota(jnp.int32, shape, 1)


def face_terms(h, w, inv_c, face):
    open_e = 0.5 * (h + east(h)) * (w * east(w))
    open_n = 0.5 * (h + north(h)) * (w * north(w)) * face
    return 0.25 * open_e, diffusion * open_e * inv_c, 0.25 * open_n, diffusion * open_n


def advance(fields, terms, scale, scale_c, vertical):
    quarter_e, spread_e, quarter_n, spread_n = terms
    u, v = fields[2], fields[3]
    speed_e = quarter_e * (u + east(u))
    speed_n = quarter_n * (v + north(v))
    here_e, there_e = speed_e + spread_e, speed_e - spread_e
    here_n, there_n = speed_n + spread_n, speed_n - spread_n
    fresh = []
    for q, vert in zip(fields, vertical):
        flux_e = here_e * q + there_e * east(q)
        flux_n = here_n * q + there_n * north(q)
        spread = (flux_e - west(flux_e)) + (flux_n - south(flux_n))
        fresh.append(q + scale * vert - scale_c * spread)
    return fresh


def pack_kernel(state_ref, thick_ref, wet_ref, halo_ref, first_ref, last_ref):
    levels, rows, lanes = thick_ref.shape
    lane = lane_of((8, LANES))
    for t in range(rows // 8 + 1):
        first = jnp.zeros((8, LANES), jnp.float32)
        last = jnp.zeros((8, LANES), jnp.float32)
        part = slice(8 * t, 8 * t + 8)
        for f in range(6):
            for k in range(levels):
                if t == rows // 8:
                    x = halo_ref[f, k]
                elif f < 4:
                    x = state_ref[f, k, part]
                elif f == 4:
                    x = thick_ref[k, part]
                else:
                    x = wet_ref[k, part].astype(jnp.float32)
                at = GROUP * f + 2 * k
                mine = (lane >= at) & (lane < at + 2)
                first = jnp.where(mine, roll(x, at, 1), first)
                last = jnp.where(mine, roll(x, at + 2 - lanes, 1), last)
        first_ref[part] = first
        last_ref[part] = last


def inner_kernel(
    state_ref, thick_ref, wet_ref, halo_ref, table_ref, out_ref, own_ref, q_ref, term_ref
):
    levels, rows, lanes = thick_ref.shape
    full = rows + 8
    inv_c, face = table_ref[0], table_ref[1]

    def load(f, k):
        if f < 4:
            own = state_ref[f, k]
        elif f == 4:
            own = thick_ref[k]
        else:
            own = wet_ref[k].astype(jnp.float32)
        return jnp.concatenate([own, halo_ref[f, k]], axis=0)

    lane = lane_of((full, LANES))
    for f in range(6):
        own = jnp.zeros((full, LANES), jnp.float32)
        for k in range(levels):
            x = load(f, k)
            q_ref[f, k] = x
            at = GROUP * k + 2
            own = jnp.where((lane >= at) & (lane < at + 4), roll(x, at, 1), own)
            at = GROUP * k + 8
            own = jnp.where(
                (lane >= at) & (lane < at + 4), roll(x, at + 4 - lanes, 1), own
            )
        own_ref[f] = own

    def solid(k):
        return jnp.where(q_ref[5, k] > 0, q_ref[4, k], 1.0)

    for k in range(levels):
        h, w, hs = q_ref[4, k], q_ref[5, k], solid(k)
        for i, term in enumerate(face_terms(h, w, inv_c, face)):
            term_ref[i, k] = term
        scale = time_step * w / hs
        term_ref[4, k] = scale
        term_ref[5, k] = scale * inv_c
        if k + 1 < levels:
            term_ref[6, k] = w * q_ref[5, k + 1] * vertical_mix / (0.5 * (hs + solid(k + 1)))

    def step(source, target, part):
        for k in range(levels):
            fields = [source[f, k] for f in range(4)]
            vertical = []
            for f in range(4):
                vert = jnp.zeros((full, LANES), jnp.float32)
                if k + 1 < levels:
                    vert = term_ref[6, k] * (source[f, k + 1] - fields[f])
                if k:
                    vert = vert - term_ref[6, k - 1] * (fields[f] - source[f, k - 1])
                vertical.append(vert)
            terms = [term_ref[i, k] for i in range(4)]
            fresh = advance(fields, terms, term_ref[4, k], term_ref[5, k], vertical)
            for f in range(4):
                target[f, k] = fresh[f][:part]

    middle = q_ref.at[6:10]
    step(q_ref, middle, full)
    step(middle, out_ref, rows)


def edge_kernel(inner_ref, own_ref, west_ref, east_ref, table_ref, out_ref):
    levels, rows, lanes = inner_ref.shape[1:]
    full = rows + 8
    lane = lane_of((full, LANES))
    inv_c, face = table_ref[0], table_ref[1]
    from_west, from_east = west_ref[...], east_ref[...]
    tiles = []
    for f in range(6):
        x = own_ref[f]
        for k in range(levels):
            src = GROUP * f + 2 * k
            at = GROUP * k
            x = jnp.where((lane >= at) & (lane < at + 2), roll(from_west, at - src, 1), x)
            at = GROUP * k + 12
            x = jnp.where((lane >= at) & (lane < at + 2), roll(from_east, at - src, 1), x)
        tiles.append(x)
    fields, h, w = tiles[:4], tiles[4], tiles[5]

    def deeper(x):
        return roll(x, -GROUP, 1)

    def shallower(x):
        return roll(x, GROUP, 1)

    hs = jnp.where(w > 0, h, 1.0)
    terms = face_terms(h, w, inv_c, face)
    scale = time_step * w / hs
    scale_c = scale * inv_c
    couple = w * deeper(w) * vertical_mix / (0.5 * (hs + deeper(hs)))
    couple = jnp.where(lane < GROUP * (levels - 1), couple, 0.0)
    for _ in range(2):
        vertical = []
        for q in fields:
            down = couple * (deeper(q) - q)
            vertical.append(down - shallower(down))
        fields = advance(fields, terms, scale, scale_c, vertical)
    lane = lane_of((rows, LANES))
    for f in range(4):
        x = fields[f][:rows]
        for k in range(levels):
            left = roll(x, -(GROUP * k + 2), 1)
            right = roll(x, lanes - 2 - (GROUP * k + 10), 1)
            out_ref[f, k] = jnp.where(
                lane < 2, left, jnp.where(lane >= lanes - 2, right, inner_ref[f, k])
            )


def call(kernel, outs, scratch=(), cost=None):
    vmem = pl.BlockSpec(memory_space=pltpu.VMEM)
    shapes = [jax.ShapeDtypeStruct(s, jnp.float32) for s in outs]

    def run(*args):
        return pl.pallas_call(
            kernel,
            out_shape=shapes,
            in_specs=[vmem] * len(args),
            out_specs=[vmem] * len(outs),
            scratch_shapes=[pltpu.VMEM(s, jnp.float32) for s in scratch],
            compiler_params=pltpu.CompilerParams(vmem_limit_bytes=24 << 20),
            cost_estimate=cost,
        )(*args)

    return run


def swap_edges(before_src, after_src, axis):
    peers = lax.axis_size(axis)
    up = [(i, (i + 1) % peers) for i in range(peers)]
    down = [(j, i) for i, j in up]
    return lax.ppermute(before_src, axis, up), lax.ppermute(after_src, axis, down)


def mode_basis(length, modes):
    turns = np.arange(modes)[None, :] * np.arange(length)[:, None] % length
    angle = turns * (2.0 * math.pi / length)
    return np.concatenate([np.cos(angle), np.sin(angle)], axis=1).astype(np.float32)


def mode_weights(counts, modes, length):
    order = jnp.arange(modes).astype(jnp.float32)
    keep = (order[None, :] < counts[:, None]).astype(jnp.float32)
    scale = jnp.where(order == 0, 1.0, 2.0) / length
    weights = keep * scale[None, :]
    return jnp.concatenate([weights, weights], axis=1)


def row_table(lat_pos, rows, nlat):
    place = np.arange(rows + 8)
    place = np.where(place < rows + 2, place, np.where(place < rows + 6, 0, place - rows - 8))
    place = (lat_pos * rows + jnp.asarray(place, jnp.int32)).astype(jnp.float32)
    centre = jnp.cos(lat_edge * (2.0 * (place + 0.5) / nlat - 1.0))
    faces = jnp.cos(lat_edge * (2.0 * (place + 1.0) / nlat - 1.0))
    table = jnp.stack([1.0 / centre, faces])
    return jnp.broadcast_to(table[:, :, None], table.shape + (LANES,))


def shards(ocean_state, thickness, wet_mask, mode_counts, row_flags):
    levels, rows, lanes = ocean_state.shape[1:]
    assert rows % 8 == 0 and lanes == LANES and levels * GROUP <= LANES
    lon_peers = lax.axis_size("lon")
    lat_peers = lax.axis_size("lat")
    nlat = rows * lat_peers
    nlon = lanes * lon_peers
    lat_pos = lax.axis_index("lat")
    table = row_table(lat_pos, rows, nlat)

    def edge_rows(part):
        return jnp.concatenate(
            [
                ocean_state[:, :, part],
                thickness[None, :, part],
                wet_mask[None, :, part].astype(jnp.float32),
            ]
        )

    below, above = swap_edges(
        edge_rows(slice(rows - 2, rows)), edge_rows(slice(0, 2)), "lat"
    )
    below = jnp.where(lat_pos > 0, below, 0.0)
    above = jnp.where(lat_pos < lat_peers - 1, above, 0.0)
    halo = jnp.concatenate(
        [above, jnp.zeros((6, levels, 4, lanes), jnp.float32), below], axis=2
    )
    full = rows + 8
    first, last = call(pack_kernel, [(full, LANES)] * 2)(
        ocean_state, thickness, wet_mask, halo
    )
    from_west, from_east = swap_edges(last, first, "lon")
    cells = levels * full * lanes
    inner, own = call(
        inner_kernel,
        [ocean_state.shape, (6, full, LANES)],
        [(10, levels, full, lanes), (7, levels, full, lanes)],
        pl.CostEstimate(
            flops=300 * cells, transcendentals=2 * cells, bytes_accessed=60 * cells
        ),
    )(ocean_state, thickness, wet_mask, halo, table)
    state = call(edge_kernel, [ocean_state.shape])(
        inner, own, from_west, from_east, table
    )[0]

    total = 4 * levels * rows
    part = total // lon_peers
    basis = jnp.asarray(mode_basis(nlon, MAXM)).reshape(lon_peers, lanes, 2 * MAXM)
    circles = lax.all_to_all(
        state.reshape(lon_peers, part, lanes), "lon", 0, 0, tiled=True
    )
    totals = jnp.einsum(
        "opi,oim->pm",
        circles,
        basis,
        precision=lax.Precision.HIGHEST,
        preferred_element_type=jnp.float32,
    )
    counts = mode_counts.astype(jnp.float32)
    row_counts = lax.dynamic_slice(
        jnp.broadcast_to(counts[None], (4 * levels, rows)).reshape(total),
        (lax.axis_index("lon") * part,),
        (part,),
    )
    smooth = jnp.einsum(
        "pm,oim->opi",
        totals * mode_weights(row_counts, MAXM, nlon),
        basis,
        precision=lax.Precision.HIGHEST,
        preferred_element_type=jnp.float32,
    )
    smooth = lax.all_to_all(smooth, "lon", 0, 0, tiled=True).reshape(state.shape)
    flags = row_flags.astype(jnp.float32)
    wet = wet_mask.astype(jnp.float32)
    return state + flags[None, None, :, None] * wet[None] * (smooth - state)


def solution(mesh):
    in_specs = (
        P(None, None, "lat", "lon"),
        P(None, "lat", "lon"),
        P(None, "lat", "lon"),
        P("lat"),
        P("lat"),
    )
    out_specs = P(None, None, "lat", "lon")
    return jax.shard_map(shards, mesh=mesh, in_specs=in_specs, out_specs=out_specs, check_vma=False)
```

time: 54.4 us -> 47.7 us (0.88)
  other arithmetic: 10.5 us -> 2.12 us
  Pallas kernels: 0 us -> 5.77 us
  waiting for transfers between devices: 25.1 us -> 19.5 us
  starting transfers between devices: 13.9 us -> 15.9 us
    pallas_call x0 -> x3, Pallas kernels: none -> 5.77 us  [run(): pl.pallas_call(kernel, out_shape=shapes, in_specs=[vmem] * len(args), out...]
    ppermute x2, waiting for transfers between devices: 6.43 us -> 1.5 us  [swap_edges(): lax.ppermute(before_src, axis, up)]
    mul x16 -> x0, other arithmetic: 2.7 us -> none  [the longest x2 0.61 us: advance(): vmix = coupling[None] * (inner[:, 1:] - inner[:, :-1])]
    ppermute x2, starting transfers between devices: 0.06 us -> 2.62 us  [swap_edges(): lax.ppermute(before_src, axis, up)]
    ppermute x2, waiting for transfers between devices: 2.73 us -> 0.32 us  [swap_edges(): lax.ppermute(after_src, axis, down)]
    ppermute x2, starting transfers between devices: 7.04 us -> 5.11 us  [swap_edges(): lax.ppermute(after_src, axis, down)]
    add x2 -> x0, other arithmetic: 1.83 us -> none  [advance(): inner + wet_in[None] * time_step * (vert - zonal - merid) / thick_in[None]]
    concatenate x2 -> x3, other arithmetic: 1.81 us -> 0.14 us  [the longest x1 0.09 us: shards(): jnp.concatenate([above, jnp.zeros((6, levels, 4, lanes), jnp.float32), be...]
  transfers between devices with their start and end apart: 6 -> 6, of which waited for: 6 -> 4; matrix products, arithmetic and copies ran while one was open for 2% -> 1% of each run, Pallas kernels for 0% -> 7%
where the time goes in v3:
time: 47.7 us; the launch traced here: 47.3 us
  waiting for transfers between devices  19.5 us (41%)
  starting transfers between devices  15.9 us (33%)
  Pallas kernels  5.77 us (12%)
  other arithmetic  2.12 us (4%)
  local copies, waits for them, and re-layouts  2.03 us (4%)
  matrix products  1.82 us (4%)
    all_to_all x1, waiting for transfers between devices, shards(): lax.all_to_all(smooth, 'lon', 0, 0, tiled=True).reshape(state.shape)  9.04 us
    all_to_all x1, waiting for transfers between devices, shards(): lax.all_to_all(state.reshape(lon_peers, part, lanes), 'lon', 0, 0, tiled=...  8.69 us
    pallas_call x3, Pallas kernels, run(): pl.pallas_call(kernel, out_shape=shapes, in_specs=[vmem] * len(args), out...  5.77 us
    ppermute x2, starting transfers between devices, swap_edges(): lax.ppermute(after_src, axis, down)  5.11 us
    all_to_all x1, starting transfers between devices, shards(): lax.all_to_all(state.reshape(lon_peers, part, lanes), 'lon', 0, 0, tiled=...  4.46 us
    all_to_all x1, starting transfers between devices, shards(): lax.all_to_all(smooth, 'lon', 0, 0, tiled=True).reshape(state.shape)  3.68 us
    ppermute x2, starting transfers between devices, swap_edges(): lax.ppermute(before_src, axis, up)  2.62 us
    add x1, other arithmetic, shards(): return state + flags[None, None, :, None] * wet[None] * (smooth - state)  1.69 us
  transfers between devices with their start and end apart: 6, of which 4 were waited for; matrix products, arithmetic and copies ran while one was open for 1% of the time, Pallas kernels for 7%

profile of v3, /device:TPU:0, one launch (start us, length us, event | category | flops | bytes accessed | tf_op | source)
XLA Modules:
  0.0 47.3 jit_solution(14817425812116457738)
XLA Ops:
  0.0 1.0 %fusion.3 = (f32[4,8,2,128]{3,2,1,0:T(2,128)S(1)}, f32[4,8,2,128]{3,2,1,0:T(2,128)S(1)}) fusion(f32[4,8,16,128]{3,2,1,0:T(8,128)} %state_ref.3), kind=kLoop, calls=%fused_computation.22 | loop fusion | bytes 131072 | tf_op jit(solution)/shard_map/slice | solution.py:267
  1.1 0.5 %collective-permute-start.1 = (f32[6,8,2,128]{3,2,1,0:T(2,128)S(1)}, f32[6,8,2,128]{3,2,1,0:T(2,128)S(1)}, u32[]{:S(2)}, u32[]{:S(2)}) collective-permute-start(f32[6,8,2,128]{3,2,1,0:T(2,128)S(1)} %pad_maximum_fusion.2), channel_id=1, source_target_pairs={{0,1},{1,2},{2,3},{3,0},{4,5},{5,6},{6,7},{7,4},{8,9},{9,10},{10,1... | collective-permute-start | bytes 147464 | tf_op jit(solution)/shard_map/ppermute | solution.py:227
  1.7 2.0 %collective-permute-start = (f32[6,8,2,128]{3,2,1,0:T(2,128)S(1)}, f32[6,8,2,128]{3,2,1,0:T(2,128)S(1)}, u32[]{:S(2)}, u32[]{:S(2)}) collective-permute-start(f32[6,8,2,128]{3,2,1,0:T(2,128)S(1)} %pad_maximum_fusion.1), channel_id=1, source_target_pairs={{1,0},{2,1},{3,2},{0,3},{5,4},{6,5},{7,6},{4,7},{9,8},{10,9},{11,1... | collective-permute-start | bytes 147464 | tf_op jit(solution)/shard_map/ppermute | solution.py:227
  3.8 0.1 pad.5.clone
  3.8 1.5 %collective-permute-done.1 = f32[6,8,2,128]{3,2,1,0:T(2,128)S(1)} collective-permute-done((f32[6,8,2,128]{3,2,1,0:T(2,128)S(1)}, f32[6,8,2,128]{3,2,1,0:T(2,128)S(1)}, u32[]{:S(2)}, u32[]{:S(2)}) %collective-permute-start.1) | collective-permute-done | bytes 49184 | tf_op jit(solution)/shard_map/ppermute | solution.py:227
  5.4 0.3 collective-permute-done
  5.7 0.1 pad_maximum_fusion.halo_ref
  5.8 0.4 shard_map.74
  6.2 2.1 %collective-permute-start.2 = (f32[24,128]{1,0:T(8,128)S(1)}, f32[24,128]{1,0:T(8,128)S(1)}, u32[]{:S(2)}, u32[]{:S(2)}) collective-permute-start(f32[24,128]{1,0:T(8,128)S(1)} %get-tuple-element.11), channel_id=1, source_target_pairs={{0,4},{4,8},{8,12},{12,16},{16,20},{20,24},{24,28},{28,0},{1,5},{5... | collective-permute-start | bytes 36872 | tf_op jit(solution)/shard_map/ppermute | solution.py:227
  8.3 3.1 %collective-permute-start.3 = (f32[24,128]{1,0:T(8,128)S(1)}, f32[24,128]{1,0:T(8,128)S(1)}, u32[]{:S(2)}, u32[]{:S(2)}) collective-permute-start(f32[24,128]{1,0:T(8,128)S(1)} %get-tuple-element.12), channel_id=1, source_target_pairs={{4,0},{8,4},{12,8},{16,12},{20,16},{24,20},{28,24},{0,28},{5,1},{9... | collective-permute-start | bytes 36872 | tf_op jit(solution)/shard_map/ppermute | solution.py:227
  11.5 3.1 %shard_map.73 = (f32[4,8,16,128]{3,2,1,0:T(8,128)S(1)}, f32[6,24,128]{2,1,0:T(8,128)S(1)}) custom-call(f32[4,8,16,128]{3,2,1,0:T(8,128)S(1)} %copy-done, f32[8,16,128]{2,1,0:T(8,128)S(1)} %copy-done.2, s32[8,16,128]{2,1,0:T(8,128)S(1)} %copy-done.1, f32[6,8,8,128]{3,2,1,0:T(8,128)S(1)} %pad_maximum_fusion.halo_ref, f32[2,24,128]{2,1,0:T(8,128)S(1)} %broadcast_in_dim.45.table_ref), custom_call_target="tpu_custom_call" | custom-call | flops 7372800 | bytes 1474560 | tf_op jit(solution)/shard_map/pallas_call | solution.py:210
  14.6 2.3 %shard_map.75 = f32[4,8,16,128]{3,2,1,0:T(8,128)} custom-call(f32[4,8,16,128]{3,2,1,0:T(8,128)S(1)} %get-tuple-element.9.inner_ref, f32[6,24,128]{2,1,0:T(8,128)S(1)} %get-tuple-element.10.own_ref, f32[24,128]{1,0:T(8,128)S(1)} %collective-permute-done.2.west_ref, f32[24,128]{1,0:T(8,128)S(1)} %collective-permute-done.3.east_ref, ...), custom_call_target="tpu_custom_call" | custom-call | tf_op jit(solution)/shard_map/pallas_call | solution.py:210
  16.9 4.5 %all-to-all-start = ((f32[8,64,128]{2,1,0:T(8,128)}), f32[8,64,128]{2,1,0:T(8,128)S(1)}, u32[]{:S(2)}, u32[]{:S(2)}) async-start(f32[8,64,128]{2,1,0:T(8,128)} %bitcast.6), calls=%async_computation | async-start | bytes 524288 | tf_op jit(solution)/shard_map/all_to_all | solution.py:302
  21.4 0.7 %copy-done.5 = s32[16]{0:T(128)S(1)} copy-done((s32[16]{0:T(128)S(1)}, s32[16]{0:T(128)}, u32[]{:S(2)}) %copy-start.5) | copy-done | bytes 88
  22.0 0.1 reshape.33
  22.1 0.1 dynamic_slice.3
  22.2 0.1 compare_select_fusion
  22.3 8.7 %all-to-all-done = f32[8,64,128]{2,1,0:T(8,128)S(1)} async-done(((f32[8,64,128]{2,1,0:T(8,128)}), f32[8,64,128]{2,1,0:T(8,128)S(1)}, u32[]{:S(2)}, u32[]{:S(2)}) %all-to-all-start) | async-done | bytes 262176 | tf_op jit(solution)/shard_map/all_to_all | solution.py:302
  31.0 0.4 fusion.1
  31.4 1.4 %convolution_bitcast_fusion = f32[8,64,128]{2,1,0:T(8,128)} fusion(f32[64,128,1]{1,0,2:T(8,128)S(1)} %fusion.1, f32[8,128,128]{2,1,0:T(8,128)S(1)} %copy-done.3), kind=kOutput, calls=%fused_computation | convolution fusion | flops 100663296 | bytes 819200 | tf_op jit(solution)/shard_map/pm,oim->opi/dot_general | solution.py:318
  32.8 3.7 %all-to-all-start.1 = ((f32[8,64,128]{2,1,0:T(8,128)}), f32[8,64,128]{2,1,0:T(8,128)S(1)}, u32[]{:S(2)}, u32[]{:S(2)}) async-start(f32[8,64,128]{2,1,0:T(8,128)} %convolution_bitcast_fusion), calls=%async_computation.1 | async-start | bytes 524288 | tf_op jit(solution)/shard_map/all_to_all | solution.py:325
  36.5 0.1 convert_multiply_fusion
  36.6 9.0 %all-to-all-done.1 = f32[8,64,128]{2,1,0:T(8,128)S(1)} async-done(((f32[8,64,128]{2,1,0:T(8,128)}), f32[8,64,128]{2,1,0:T(8,128)S(1)}, u32[]{:S(2)}, u32[]{:S(2)}) %all-to-all-start.1) | async-done | bytes 262176 | tf_op jit(solution)/shard_map/all_to_all | solution.py:325
  45.6 1.7 %multiply_add_fusion = f32[4,8,16,128]{3,2,1,0:T(8,128)} fusion(f32[4,8,16,128]{3,2,1,0:T(8,128)} %shard_map.75, f32[4,8,16,128]{3,2,1,0:T(8,128)S(1)} %bitcast.28, f32[8,16,128]{2,1,0:T(8,128)S(1)} %convert_multiply_fusion), kind=kLoop, calls=%fused_computation.4 | loop fusion | flops 196608 | bytes 851968 | tf_op jit(solution)/shard_map/add | solution.py:328
  (30 shorter events, 0.3 us)
Async XLA Ops:
  0.0 1.0 %copy-start.2 = (f32[8,16,128]{2,1,0:T(8,128)S(1)}, f32[8,16,128]{2,1,0:T(8,128)}, u32[]{:S(2)}) copy-start(f32[8,16,128]{2,1,0:T(8,128)} %thick_ref.3) | copy-start | bytes 196612
  0.0 1.1 %copy-start.1 = (s32[8,16,128]{2,1,0:T(8,128)S(1)}, s32[8,16,128]{2,1,0:T(8,128)}, u32[]{:S(2)}) copy-start(s32[8,16,128]{2,1,0:T(8,128)} %wet_ref.3) | copy-start | bytes 196612
  1.1 4.2 %collective-permute-start.1 = (f32[6,8,2,128]{3,2,1,0:T(2,128)S(1)}, f32[6,8,2,128]{3,2,1,0:T(2,128)S(1)}, u32[]{:S(2)}, u32[]{:S(2)}) collective-permute-start(f32[6,8,2,128]{3,2,1,0:T(2,128)S(1)} %pad_maximum_fusion.2), channel_id=1, source_target_pairs={{0,1},{1,2},{2,3},{3,0},{4,5},{5,6},{6,7},{7,4},{8,9},{9,10},{10,1... | collective-permute-start | bytes 147464 | tf_op jit(solution)/shard_map/ppermute | solution.py:227
  1.6 2.0 %copy-start.4 = (s32[24]{0:T(128)S(1)}, s32[24]{0:T(128)}, u32[]{:S(2)}) copy-start(s32[24]{0:T(128)} %constant.50.clone) | copy-start | bytes 292
  1.7 4.1 %copy-start = (f32[4,8,16,128]{3,2,1,0:T(8,128)S(1)}, f32[4,8,16,128]{3,2,1,0:T(8,128)}, u32[]{:S(2)}) copy-start(f32[4,8,16,128]{3,2,1,0:T(8,128)} %state_ref.3) | copy-start | bytes 786436
  1.7 4.0 %collective-permute-start = (f32[6,8,2,128]{3,2,1,0:T(2,128)S(1)}, f32[6,8,2,128]{3,2,1,0:T(2,128)S(1)}, u32[]{:S(2)}, u32[]{:S(2)}) collective-permute-start(f32[6,8,2,128]{3,2,1,0:T(2,128)S(1)} %pad_maximum_fusion.1), channel_id=1, source_target_pairs={{1,0},{2,1},{3,2},{0,3},{5,4},{6,5},{7,6},{4,7},{9,8},{10,9},{11,1... | collective-permute-start | bytes 147464 | tf_op jit(solution)/shard_map/ppermute | solution.py:227
  6.2 8.4 %collective-permute-start.2 = (f32[24,128]{1,0:T(8,128)S(1)}, f32[24,128]{1,0:T(8,128)S(1)}, u32[]{:S(2)}, u32[]{:S(2)}) collective-permute-start(f32[24,128]{1,0:T(8,128)S(1)} %get-tuple-element.11), channel_id=1, source_target_pairs={{0,4},{4,8},{8,12},{12,16},{16,20},{20,24},{24,28},{28,0},{1,5},{5... | collective-permute-start | bytes 36872 | tf_op jit(solution)/shard_map/ppermute | solution.py:227
  8.3 6.3 %collective-permute-start.3 = (f32[24,128]{1,0:T(8,128)S(1)}, f32[24,128]{1,0:T(8,128)S(1)}, u32[]{:S(2)}, u32[]{:S(2)}) collective-permute-start(f32[24,128]{1,0:T(8,128)S(1)} %get-tuple-element.12), channel_id=1, source_target_pairs={{4,0},{8,4},{12,8},{16,12},{20,16},{24,20},{28,24},{0,28},{5,1},{9... | collective-permute-start | bytes 36872 | tf_op jit(solution)/shard_map/ppermute | solution.py:227
  14.6 16.4 %copy-start.3 = (f32[8,128,128]{2,1,0:T(8,128)S(1)}, f32[8,128,128]{2,1,0:T(8,128)}, u32[]{:S(2)}) copy-start(f32[8,128,128]{2,1,0:T(8,128)} %constant.52) | copy-start | bytes 1572868
  16.9 14.1 %all-to-all-start = ((f32[8,64,128]{2,1,0:T(8,128)}), f32[8,64,128]{2,1,0:T(8,128)S(1)}, u32[]{:S(2)}, u32[]{:S(2)}) async-start(f32[8,64,128]{2,1,0:T(8,128)} %bitcast.6), calls=%async_computation | async-start | bytes 524288 | tf_op jit(solution)/shard_map/all_to_all | solution.py:302
  21.4 0.7 %copy-start.5 = (s32[16]{0:T(128)S(1)}, s32[16]{0:T(128)}, u32[]{:S(2)}) copy-start(s32[16]{0:T(128)} %param.10) | copy-start | bytes 196
  32.8 3.7 %copy-start.6 = (s32[16]{0:T(128)S(1)}, s32[16]{0:T(128)}, u32[]{:S(2)}) copy-start(s32[16]{0:T(128)} %param.11) | copy-start | bytes 196
  32.8 12.8 %all-to-all-start.1 = ((f32[8,64,128]{2,1,0:T(8,128)}), f32[8,64,128]{2,1,0:T(8,128)S(1)}, u32[]{:S(2)}, u32[]{:S(2)}) async-start(f32[8,64,128]{2,1,0:T(8,128)} %convolution_bitcast_fusion), calls=%async_computation.1 | async-start | bytes 524288 | tf_op jit(solution)/shard_map/all_to_all | solution.py:325

commit v4 on v3

v4 whole, which is shorter than its diff:
```python
import math

import jax
import jax.numpy as jnp
import numpy as np
from jax import lax
from jax.experimental import pallas as pl
from jax.experimental.pallas import tpu as pltpu
from jax.sharding import PartitionSpec as P

MAXM = 64
LANES = 128
GROUP = 16


lat_edge = 1.3
diffusion = 0.05
vertical_mix = 0.5
time_step = 0.05


def roll(x, shift, axis):
    shift %= x.shape[axis]
    return pltpu.roll(x, shift, axis) if shift else x


def east(x):
    return roll(x, -1, 1)


def west(x):
    return roll(x, 1, 1)


def north(x):
    return roll(x, -1, 0)


def south(x):
    return roll(x, 1, 0)


def lane_of(shape):
    return lax.broadcasted_iota(jnp.int32, shape, 1)


def east_terms(h, w, inv_c):
    open_e = 0.5 * (h + east(h)) * (w * east(w))
    return 0.25 * open_e, diffusion * open_e * inv_c


def north_terms(h, w, face):
    open_n = 0.5 * (h + north(h)) * (w * north(w)) * face
    return 0.25 * open_n, diffusion * open_n


def advance(fields, terms, scale, scale_c, vertical):
    quarter_e, spread_e, quarter_n, spread_n = terms
    u, v = fields[2], fields[3]
    speed_e = quarter_e * (u + east(u))
    speed_n = quarter_n * (v + north(v))
    here_e, there_e = speed_e + spread_e, speed_e - spread_e
    here_n, there_n = speed_n + spread_n, speed_n - spread_n
    fresh = []
    for q, vert in zip(fields, vertical):
        flux_e = here_e * q + there_e * east(q)
        flux_n = here_n * q + there_n * north(q)
        spread = (flux_e - west(flux_e)) + (flux_n - south(flux_n))
        fresh.append(q + scale * vert - scale_c * spread)
    return fresh


def own_columns(load, levels, lanes, rows):
    lane = lane_of((rows, LANES))
    own = jnp.zeros((rows, LANES), jnp.float32)
    for k in range(levels):
        x = load(k)
        at = GROUP * k + 2
        own = jnp.where((lane >= at) & (lane < at + 4), roll(x, at, 1), own)
        at = GROUP * k + 8
        own = jnp.where((lane >= at) & (lane < at + 4), roll(x, at + 4 - lanes, 1), own)
    return own


def row_terms(thick, wet, inv_c, levels, term_ref):
    w, h = wet(0), thick(0)
    hs = jnp.where(w > 0, h, 1.0)
    for k in range(levels):
        term_ref[0, k], term_ref[1, k] = east_terms(h, w, inv_c)
        scale = time_step * w / hs
        term_ref[2, k] = scale
        term_ref[3, k] = scale * inv_c
        if k + 1 < levels:
            w_next, h_next = wet(k + 1), thick(k + 1)
            hs_next = jnp.where(w_next > 0, h_next, 1.0)
            term_ref[4, k] = w * w_next * vertical_mix / (0.5 * (hs + hs_next))
            w, h, hs = w_next, h_next, hs_next


def ready_kernel(state_ref, thick_ref, wet_ref, table_ref, own_ref, term_ref):
    levels, rows, lanes = thick_ref.shape

    def thick(k):
        return thick_ref[k]

    def wet(k):
        return wet_ref[k].astype(jnp.float32)

    for f in range(4):
        own_ref[f] = own_columns(lambda k, f=f: state_ref[f, k], levels, lanes, rows)
    own_ref[4] = own_columns(thick, levels, lanes, rows)
    own_ref[5] = own_columns(wet, levels, lanes, rows)
    row_terms(thick, wet, table_ref[0, :rows], levels, term_ref)


def pack_kernel(
    state_ref, thick_ref, wet_ref, below_ref, above_ref, first_ref, last_ref, halo_ref
):
    levels, rows, lanes = thick_ref.shape
    lat_pos = lax.axis_index("lat")
    with_below = jnp.where(lat_pos > 0, 1.0, 0.0)
    with_above = jnp.where(lat_pos < lax.axis_size("lat") - 1, 1.0, 0.0)
    lane = lane_of((8, LANES))
    for f in range(6):
        for k in range(levels):
            halo_ref[f, k, 0:2] = above_ref[f, k] * with_above
            halo_ref[f, k, 2:6] = jnp.zeros((4, lanes), jnp.float32)
            halo_ref[f, k, 6:8] = below_ref[f, k] * with_below
    for t in range(rows // 8 + 1):
        first = jnp.zeros((8, LANES), jnp.float32)
        last = jnp.zeros((8, LANES), jnp.float32)
        part = slice(8 * t, 8 * t + 8)
        for f in range(6):
            for k in range(levels):
                if t == rows // 8:
                    x = halo_ref[f, k]
                elif f < 4:
                    x = state_ref[f, k, part]
                elif f == 4:
                    x = thick_ref[k, part]
                else:
                    x = wet_ref[k, part].astype(jnp.float32)
                at = GROUP * f + 2 * k
                mine = (lane >= at) & (lane < at + 2)
                first = jnp.where(mine, roll(x, at, 1), first)
                last = jnp.where(mine, roll(x, at + 2 - lanes, 1), last)
        first_ref[part] = first
        last_ref[part] = last


def inner_kernel(
    state_ref,
    thick_ref,
    wet_ref,
    halo_ref,
    table_ref,
    own_ref,
    term_ref,
    out_ref,
    edge_ref,
    halo_term_ref,
    north_ref,
):
    levels, rows, lanes = thick_ref.shape
    full = rows + 8
    face = table_ref[1]

    def joined(x, y):
        return jnp.concatenate([x, y], axis=0)

    def halo(f):
        return lambda k: halo_ref[f, k]

    for f in range(6):
        edge_ref[f, :rows] = own_ref[f]
        edge_ref[f, rows:] = own_columns(halo(f), levels, lanes, 8)
    row_terms(halo(4), halo(5), table_ref[0, rows:], levels, halo_term_ref)
    for k in range(levels):
        h = joined(thick_ref[k], halo_ref[4, k])
        w = joined(wet_ref[k].astype(jnp.float32), halo_ref[5, k])
        north_ref[0, k], north_ref[1, k] = north_terms(h, w, face)
        for f in range(4):
            out_ref[0, f, k] = joined(state_ref[f, k], halo_ref[f, k])

    def term(i, k):
        return joined(term_ref[i, k], halo_term_ref[i, k])

    def step(i, _):
        source, target = out_ref.at[i], out_ref.at[i + 1]
        fields = [source[f, 0] for f in range(4)]
        above = [jnp.zeros((full, LANES), jnp.float32)] * 4
        for k in range(levels):
            deeper = below = above
            if k + 1 < levels:
                couple = term(4, k)
                deeper = [source[f, k + 1] for f in range(4)]
                below = [couple * (d - q) for d, q in zip(deeper, fields)]
                vertical = [b - a for b, a in zip(below, above)]
            else:
                vertical = [-a for a in above]
            terms = term(0, k), term(1, k), north_ref[0, k], north_ref[1, k]
            fresh = advance(fields, terms, term(2, k), term(3, k), vertical)
            for f in range(4):
                target[f, k] = fresh[f]
            fields, above = deeper, below
        return 0

    lax.fori_loop(0, 2, step, 0)


def edge_kernel(
    inner_ref, own_ref, west_ref, east_ref, table_ref, out_ref, send_ref, tile_ref, term_ref, sems
):
    levels, rows, lanes = out_ref.shape[1:]
    full = rows + 8
    lane = lane_of((full, LANES))
    inv_c, face = table_ref[0], table_ref[1]
    from_west, from_east = west_ref[...], east_ref[...]

    def joined(f):
        x = own_ref[f]
        for k in range(levels):
            src = GROUP * f + 2 * k
            at = GROUP * k
            x = jnp.where((lane >= at) & (lane < at + 2), roll(from_west, at - src, 1), x)
            at = GROUP * k + 12
            x = jnp.where((lane >= at) & (lane < at + 2), roll(from_east, at - src, 1), x)
        return x

    def deeper(x):
        return roll(x, -GROUP, 1)

    def shallower(x):
        return roll(x, GROUP, 1)

    h, w = joined(4), joined(5)
    for f in range(4):
        tile_ref[f] = joined(f)
    hs = jnp.where(w > 0, h, 1.0)
    scale = time_step * w / hs
    couple = w * deeper(w) * vertical_mix / (0.5 * (hs + deeper(hs)))
    couple = jnp.where(lane < GROUP * (levels - 1), couple, 0.0)
    terms = east_terms(h, w, inv_c) + north_terms(h, w, face)
    for i, term in enumerate(terms + (scale, scale * inv_c, couple)):
        term_ref[i] = term

    def step(_, __):
        terms = [term_ref[i] for i in range(7)]
        fields = [tile_ref[f] for f in range(4)]
        vertical = []
        for q in fields:
            down = terms[6] * (deeper(q) - q)
            vertical.append(down - shallower(down))
        for f, q in enumerate(advance(fields, terms[:4], terms[4], terms[5], vertical)):
            tile_ref[f] = q
        return 0

    lax.fori_loop(0, 2, step, 0)
    lane = lane_of((rows, LANES))
    for f in range(4):
        x = tile_ref[f, :rows]
        for k in range(levels):
            left = roll(x, -(GROUP * k + 2), 1)
            right = roll(x, lanes - 2 - (GROUP * k + 10), 1)
            out_ref[f, k] = jnp.where(
                lane < 2,
                left,
                jnp.where(lane >= lanes - 2, right, inner_ref[2, f, k, :rows]),
            )
        pltpu.make_async_copy(out_ref.at[f], send_ref.at[f], sems.at[f]).start()
    for f in range(4):
        pltpu.make_async_copy(out_ref.at[f], send_ref.at[f], sems.at[f]).wait()


def product(a, b, dims):
    return lax.dot_general(
        a,
        b,
        (dims, ((), ())),
        precision=lax.Precision.HIGHEST,
        preferred_element_type=jnp.float32,
    )


def filter_kernel(circle_ref, basis_ref, weight_ref, out_ref, totals_ref, piece_ref, sems):
    pieces = circle_ref.shape[0]
    total = jnp.zeros(totals_ref.shape, jnp.float32)
    for o in range(pieces):
        total = total + product(circle_ref[o], basis_ref[o], ((1,), (0,)))
    totals_ref[...] = total * weight_ref[...]
    copies = []
    for o in range(pieces):
        piece_ref[o] = product(totals_ref[...], basis_ref[o], ((1,), (1,)))
        copies.append(pltpu.make_async_copy(piece_ref.at[o], out_ref.at[o], sems.at[o]))
        copies[-1].start()
    for copy in copies:
        copy.wait()


def blend_kernel(state_ref, smooth_ref, wet_ref, flag_ref, out_ref, piece_ref, sems):
    levels = wet_ref.shape[0]
    flag = flag_ref[...]
    copies = []
    for f in range(4):
        for k in range(levels):
            state = state_ref[f, k]
            gate = flag * wet_ref[k].astype(jnp.float32)
            piece_ref[f, k] = state + gate * (smooth_ref[f, k] - state)
        copies.append(pltpu.make_async_copy(piece_ref.at[f], out_ref.at[f], sems.at[f]))
        copies[-1].start()
    for copy in copies:
        copy.wait()


def call(kernel, outs, scratch=(), sems=0, sent=False, flops=0):
    vmem = pl.BlockSpec(memory_space=pltpu.VMEM)
    specs = [vmem] * len(outs)
    if sent:
        specs[-1] = pl.BlockSpec(memory_space=pl.ANY)
    buffers = [pltpu.VMEM(s, jnp.float32) for s in scratch]
    if sems:
        buffers.append(pltpu.SemaphoreType.DMA((sems,)))
    cost = pl.CostEstimate(
        flops=flops, transcendentals=0, bytes_accessed=4 * sum(map(math.prod, outs))
    )

    def run(*args):
        return pl.pallas_call(
            kernel,
            out_shape=[jax.ShapeDtypeStruct(s, jnp.float32) for s in outs],
            in_specs=[vmem] * len(args),
            out_specs=specs,
            scratch_shapes=buffers,
            compiler_params=pltpu.CompilerParams(vmem_limit_bytes=24 << 20),
            cost_estimate=cost,
        )(*args)

    return run


def swap_edges(before_src, after_src, axis):
    peers = lax.axis_size(axis)
    up = [(i, (i + 1) % peers) for i in range(peers)]
    down = [(j, i) for i, j in up]
    return lax.ppermute(before_src, axis, up), lax.ppermute(after_src, axis, down)


def mode_basis(length, modes):
    turns = np.arange(modes)[None, :] * np.arange(length)[:, None] % length
    angle = turns * (2.0 * math.pi / length)
    return np.concatenate([np.cos(angle), np.sin(angle)], axis=1).astype(np.float32)


def mode_weights(counts, modes, length):
    order = jnp.arange(modes).astype(jnp.float32)
    keep = (order[None, :] < counts[:, None]).astype(jnp.float32)
    scale = jnp.where(order == 0, 1.0, 2.0) / length
    weights = keep * scale[None, :]
    return jnp.concatenate([weights, weights], axis=1)


def row_table(lat_pos, rows, nlat):
    place = np.arange(rows + 8)
    place = np.where(place < rows + 2, place, np.where(place < rows + 6, 0, place - rows - 8))
    place = (lat_pos * rows + jnp.asarray(place, jnp.int32)).astype(jnp.float32)
    centre = jnp.cos(lat_edge * (2.0 * (place + 0.5) / nlat - 1.0))
    faces = jnp.cos(lat_edge * (2.0 * (place + 1.0) / nlat - 1.0))
    table = jnp.stack([1.0 / centre, faces])
    return jnp.broadcast_to(table[:, :, None], table.shape + (LANES,))


def shards(ocean_state, thickness, wet_mask, mode_counts, row_flags):
    levels, rows, lanes = ocean_state.shape[1:]
    assert rows % 8 == 0 and lanes == LANES and levels * GROUP <= LANES
    lon_peers = lax.axis_size("lon")
    lat_peers = lax.axis_size("lat")
    nlat = rows * lat_peers
    nlon = lanes * lon_peers
    full = rows + 8
    total = 4 * levels * rows
    part = total // lon_peers
    table = row_table(lax.axis_index("lat"), rows, nlat)
    block = (ocean_state, thickness, wet_mask)
    cells = 4 * levels * full * lanes

    def edge_rows(part):
        return jnp.concatenate(
            [
                ocean_state[:, :, part],
                thickness[None, :, part],
                wet_mask[None, :, part].astype(jnp.float32),
            ]
        )

    below, above = swap_edges(
        edge_rows(slice(rows - 2, rows)), edge_rows(slice(0, 2)), "lat"
    )
    own, terms = call(
        ready_kernel, [(6, rows, LANES), (5, levels, rows, lanes)], flops=20 * cells
    )(*block, table)
    first, last, halo = call(
        pack_kernel, [(full, LANES)] * 2 + [(6, levels, 8, lanes)]
    )(*block, below, above)
    from_west, from_east = swap_edges(last, first, "lon")
    inner, edges = call(
        inner_kernel,
        [(3, 4, levels, full, lanes), (6, full, LANES)],
        [(5, levels, 8, lanes), (2, levels, full, lanes)],
        flops=60 * cells,
    )(*block, halo, table, own, terms)
    state, sent = call(
        edge_kernel,
        [ocean_state.shape] * 2,
        [(4, full, LANES), (7, full, LANES)],
        sems=4,
        sent=True,
    )(inner, edges, from_west, from_east, table)

    basis = jnp.asarray(mode_basis(nlon, MAXM)).reshape(lon_peers, lanes, 2 * MAXM)
    counts = mode_counts.astype(jnp.float32)
    row_counts = lax.dynamic_slice(
        jnp.broadcast_to(counts[None], (4 * levels, rows)).reshape(total),
        (lax.axis_index("lon") * part,),
        (part,),
    )
    weights = mode_weights(row_counts, MAXM, nlon)
    circles = lax.all_to_all(
        sent.reshape(lon_peers, part, lanes), "lon", 0, 0, tiled=True
    )
    smooth = call(
        filter_kernel,
        [circles.shape],
        [(part, 2 * MAXM), circles.shape],
        sems=lon_peers,
        sent=True,
    )(circles, basis, weights)[0]
    smooth = lax.all_to_all(smooth, "lon", 0, 0, tiled=True).reshape(ocean_state.shape)
    flags = jnp.broadcast_to(row_flags.astype(jnp.float32)[:, None], (rows, lanes))
    return call(blend_kernel, [ocean_state.shape], [ocean_state.shape], sems=4, sent=True)(
        state, smooth, wet_mask, flags
    )[0]


def solution(mesh):
    in_specs = (
        P(None, None, "lat", "lon"),
        P(None, "lat", "lon"),
        P(None, "lat", "lon"),
        P("lat"),
        P("lat"),
    )
    out_specs = P(None, None, "lat", "lon")
    return jax.shard_map(shards, mesh=mesh, in_specs=in_specs, out_specs=out_specs, check_vma=False)
```

time: 47.7 us -> 51.6 us (1.082)
  local copies, waits for them, and re-layouts: 2.03 us -> 4.73 us
  Pallas kernels: 5.77 us -> 7.75 us
  matrix products: 1.82 us -> 0 us
  starting transfers between devices: 15.9 us -> 17 us
    pallas_call x3 -> x6, Pallas kernels: 5.77 us -> 7.75 us  [run(): pl.pallas_call(kernel, out_shape=[jax.ShapeDtypeStruct(s, jnp.float32) fo...]
    unnamed x14, local copies, waits for them, and re-layouts: 0.68 us -> 2.65 us
    dot_general x2 -> x0, matrix products: 1.82 us -> none  [the longest x1 1.38 us: shards(): jnp.einsum('pm,oim->opi', totals * mode_weights(row_counts, MAXM, nlon),...]
    add x1 -> x0, other arithmetic: 1.69 us -> none  [shards(): return state + flags[None, None, :, None] * wet[None] * (smooth - state)]
    all_to_all x2, starting transfers between devices: 8.14 us -> 9.25 us  [the longest x1 5.65 us: shards(): lax.all_to_all(sent.reshape(lon_peers, part, lanes), 'lon', 0, 0, tiled=T...]
    broadcast_in_dim x1, local copies, waits for them, and re-layouts: 0.01 us -> 0.78 us  [edge_rows(): thickness[None, :, part]]
    convert_element_type x1, other arithmetic: 0.01 us -> 0.78 us  [edge_rows(): wet_mask[None, :, part].astype(jnp.float32)]
    another operation x2, other arithmetic: 0.06 us -> 0.72 us  [row_table(): table = jnp.stack([1.0 / centre, faces])]
  transfers between devices with their start and end apart: 6 -> 6, of which waited for: 4 -> 4; matrix products, arithmetic and copies ran while one was open for 1% -> 2% of each run, Pallas kernels for 7% -> 4%
where the time goes in v4:
time: 51.6 us; the launch traced here: 50.9 us
  waiting for transfers between devices  19.6 us (38%)
  starting transfers between devices  17 us (33%)
  Pallas kernels  7.75 us (15%)
  local copies, waits for them, and re-layouts  4.73 us (9%)
  other arithmetic  1.72 us (3%)
    all_to_all x1, waiting for transfers between devices, shards(): lax.all_to_all(sent.reshape(lon_peers, part, lanes), 'lon', 0, 0, tiled=T...  9.2 us
    all_to_all x1, waiting for transfers between devices, shards(): lax.all_to_all(smooth, 'lon', 0, 0, tiled=True).reshape(ocean_state.shape)  9.11 us
    pallas_call x6, Pallas kernels, run(): pl.pallas_call(kernel, out_shape=[jax.ShapeDtypeStruct(s, jnp.float32) fo...  7.75 us
    all_to_all x1, starting transfers between devices, shards(): lax.all_to_all(sent.reshape(lon_peers, part, lanes), 'lon', 0, 0, tiled=T...  5.65 us
    ppermute x2, starting transfers between devices, swap_edges(): lax.ppermute(after_src, axis, down)  5.1 us
    all_to_all x1, starting transfers between devices, shards(): lax.all_to_all(smooth, 'lon', 0, 0, tiled=True).reshape(ocean_state.shape)  3.6 us
    unnamed x14, local copies, waits for them, and re-layouts  2.65 us
    ppermute x2, starting transfers between devices, swap_edges(): lax.ppermute(before_src, axis, up)  2.6 us
  transfers between devices with their start and end apart: 6, of which 4 were waited for; matrix products, arithmetic and copies ran while one was open for 2% of the time, Pallas kernels for 4%

profile of v4, /device:TPU:0, one launch (start us, length us, event | category | flops | bytes accessed | tf_op | source)
XLA Modules:
  0.0 50.9 jit_solution(12929323626884917512)
XLA Ops:
  0.0 1.0 %fusion.1 = (f32[4,8,2,128]{3,2,1,0:T(2,128)S(1)}, f32[4,8,2,128]{3,2,1,0:T(2,128)S(1)}) fusion(f32[4,8,16,128]{3,2,1,0:T(8,128)} %state_ref.5), kind=kLoop, calls=%fused_computation.14 | loop fusion | bytes 131072 | tf_op jit(solution)/shard_map/slice | solution.py:389
  1.0 0.8 %slice_bitcast_fusion = (f32[1,8,2,128]{3,2,1,0:T(2,128)S(1)}, f32[1,8,2,128]{3,2,1,0:T(2,128)S(1)}) fusion(f32[8,16,128]{2,1,0:T(8,128)} %thick_ref.5), kind=kLoop, calls=%fused_computation.5 | loop fusion | bytes 32768 | tf_op jit(solution)/shard_map/broadcast_in_dim | solution.py:390
  1.8 0.8 %convert_bitcast_fusion = (f32[1,8,2,128]{3,2,1,0:T(2,128)S(1)}, f32[1,8,2,128]{3,2,1,0:T(2,128)S(1)}) fusion(s32[8,16,128]{2,1,0:T(8,128)} %wet_ref.7), kind=kLoop, calls=%fused_computation.4 | loop fusion | flops 4096 | bytes 32768 | tf_op jit(solution)/shard_map/convert_element_type | solution.py:391
  2.6 0.5 collective-permute-start
  3.1 2.0 %collective-permute-start.1 = (f32[6,8,2,128]{3,2,1,0:T(2,128)S(1)}, f32[6,8,2,128]{3,2,1,0:T(2,128)S(1)}, u32[]{:S(2)}, u32[]{:S(2)}) collective-permute-start(f32[6,8,2,128]{3,2,1,0:T(2,128)S(1)} %pad_maximum_fusion.1), channel_id=1, source_target_pairs={{1,0},{2,1},{3,2},{0,3},{5,4},{6,5},{7,6},{4,7},{9,8},{10,9},{11,1... | collective-permute-start | bytes 147464 | tf_op jit(solution)/shard_map/ppermute | solution.py:345
  5.1 0.7 %divide_bitcast_fusion = (f32[1,24]{1,0:T(1,128)S(1)}, f32[1,24]{1,0:T(1,128)S(1)}) fusion(s32[24]{0:T(128)} %constant.46.clone, s32[]{:T(128)S(6)} %mul.22), kind=kLoop, calls=%fused_computation.13 | loop fusion | flops 264 | bytes 292 | tf_op jit(solution)/shard_map/stack | solution.py:368
  5.8 1.0 %collective-permute-done.below_ref = f32[6,8,2,128]{3,2,1,0:T(2,128)S(1)} collective-permute-done((f32[6,8,2,128]{3,2,1,0:T(2,128)S(1)}, f32[6,8,2,128]{3,2,1,0:T(2,128)S(1)}, u32[]{:S(2)}, u32[]{:S(2)}) %collective-permute-start) | collective-permute-done | bytes 49184 | tf_op jit(solution)/shard_map/ppermute | solution.py:345
  6.8 0.3 collective-permute-done.1.above_ref
  7.1 0.9 %copy-done = f32[4,8,16,128]{3,2,1,0:T(8,128)S(1)} copy-done((f32[4,8,16,128]{3,2,1,0:T(8,128)S(1)}, f32[4,8,16,128]{3,2,1,0:T(8,128)}, u32[]{:S(2)}) %copy-start) | copy-done | bytes 262168
  8.1 0.8 %copy-done.1 = s32[8,16,128]{2,1,0:T(8,128)S(1)} copy-done((s32[8,16,128]{2,1,0:T(8,128)S(1)}, s32[8,16,128]{2,1,0:T(8,128)}, u32[]{:S(2)}) %copy-start.1) | copy-done | bytes 65560
  8.9 0.8 %copy-done.3 = f32[8,16,128]{2,1,0:T(8,128)S(1)} copy-done((f32[8,16,128]{2,1,0:T(8,128)S(1)}, f32[8,16,128]{2,1,0:T(8,128)}, u32[]{:S(2)}) %copy-start.3) | copy-done | bytes 65560
  9.8 0.4 shard_map.73
  10.2 2.1 %collective-permute-start.2 = (f32[24,128]{1,0:T(8,128)S(1)}, f32[24,128]{1,0:T(8,128)S(1)}, u32[]{:S(2)}, u32[]{:S(2)}) collective-permute-start(f32[24,128]{1,0:T(8,128)S(1)} %get-tuple-element.19), channel_id=1, source_target_pairs={{0,4},{4,8},{8,12},{12,16},{16,20},{20,24},{24,28},{28,0},{1,5},{5... | collective-permute-start | bytes 36872 | tf_op jit(solution)/shard_map/ppermute | solution.py:345
  12.3 3.1 %collective-permute-start.3 = (f32[24,128]{1,0:T(8,128)S(1)}, f32[24,128]{1,0:T(8,128)S(1)}, u32[]{:S(2)}, u32[]{:S(2)}) collective-permute-start(f32[24,128]{1,0:T(8,128)S(1)} %get-tuple-element.20), channel_id=1, source_target_pairs={{4,0},{8,4},{12,8},{16,12},{20,16},{24,20},{28,24},{0,28},{5,1},{9... | collective-permute-start | bytes 36872 | tf_op jit(solution)/shard_map/ppermute | solution.py:345
  15.4 0.3 shard_map.74
  15.8 1.7 %shard_map.75 = (f32[3,4,8,24,128]{4,3,2,1,0:T(8,128)S(1)}, f32[6,24,128]{2,1,0:T(8,128)S(1)}) custom-call(f32[4,8,16,128]{3,2,1,0:T(8,128)S(1)} %copy-done, f32[8,16,128]{2,1,0:T(8,128)S(1)} %copy-done.3, s32[8,16,128]{2,1,0:T(8,128)S(1)} %copy-done.1, f32[6,8,8,128]{3,2,1,0:T(8,128)S(1)} %get-tuple-element.14.halo_ref, ...), custom_call_target="tpu_custom_call" | custom-call | flops 5898240 | bytes 1253376 | tf_op jit(solution)/shard_map/pallas_call | solution.py:328
  17.5 1.6 %shard_map.76 = (f32[4,8,16,128]{3,2,1,0:T(8,128)S(1)}, f32[4,8,16,128]{3,2,1,0:T(8,128)}) custom-call(f32[3,4,8,24,128]{4,3,2,1,0:T(8,128)S(1)} %get-tuple-element.17.inner_ref, f32[6,24,128]{2,1,0:T(8,128)S(1)} %get-tuple-element.18.own_ref, f32[24,128]{1,0:T(8,128)S(1)} %collective-permute-done.2.west_ref, f32[24,128]{1,0:T(8,128)S(1)} %collective-permute-done.3.east_ref, ...), custom_call_target="tpu_custom_call" | custom-call | bytes 524288 | tf_op jit(solution)/shard_map/pallas_call | solution.py:328
  19.1 5.7 %all-to-all-start = ((f32[8,64,128]{2,1,0:T(8,128)}), f32[8,64,128]{2,1,0:T(8,128)S(1)}, u32[]{:S(2)}, u32[]{:S(2)}) async-start(f32[8,64,128]{2,1,0:T(8,128)} %bitcast.6), calls=%async_computation | async-start | bytes 524288 | tf_op jit(solution)/shard_map/all_to_all | solution.py:427
  25.1 0.1 pad_maximum_fusion.2.weight_ref
  25.2 9.2 %all-to-all-done.circle_ref = f32[8,64,128]{2,1,0:T(8,128)S(1)} async-done(((f32[8,64,128]{2,1,0:T(8,128)}), f32[8,64,128]{2,1,0:T(8,128)S(1)}, u32[]{:S(2)}, u32[]{:S(2)}) %all-to-all-start) | async-done | bytes 262176 | tf_op jit(solution)/shard_map/all_to_all | solution.py:427
  34.4 3.0 %shard_map.77 = f32[8,64,128]{2,1,0:T(8,128)} custom-call(f32[8,64,128]{2,1,0:T(8,128)S(1)} %all-to-all-done.circle_ref, f32[8,128,128]{2,1,0:T(8,128)S(1)} %copy-done.4, f32[64,128]{1,0:T(8,128)S(1)} %pad_maximum_fusion.2.weight_ref), custom_call_target="tpu_custom_call" | custom-call | bytes 262144 | tf_op jit(solution)/shard_map/pallas_call | solution.py:328
  37.4 3.6 %all-to-all-start.1 = ((f32[8,64,128]{2,1,0:T(8,128)}), f32[8,64,128]{2,1,0:T(8,128)S(1)}, u32[]{:S(2)}, u32[]{:S(2)}) async-start(f32[8,64,128]{2,1,0:T(8,128)} %shard_map.77), calls=%async_computation.1 | async-start | bytes 524288 | tf_op jit(solution)/shard_map/all_to_all | solution.py:437
  41.0 9.1 %all-to-all-done.1 = f32[8,64,128]{2,1,0:T(8,128)S(1)} async-done(((f32[8,64,128]{2,1,0:T(8,128)}), f32[8,64,128]{2,1,0:T(8,128)S(1)}, u32[]{:S(2)}, u32[]{:S(2)}) %all-to-all-start.1) | async-done | bytes 262176 | tf_op jit(solution)/shard_map/all_to_all | solution.py:437
  50.2 0.7 %shard_map.78 = f32[4,8,16,128]{3,2,1,0:T(8,128)} custom-call(f32[4,8,16,128]{3,2,1,0:T(8,128)S(1)} %get-tuple-element.21.state_ref, f32[4,8,16,128]{3,2,1,0:T(8,128)S(1)} %bitcast.14, s32[8,16,128]{2,1,0:T(8,128)S(1)} %copy-done.2, f32[16,128]{1,0:T(8,128)S(1)} %broadcast_in_dim.43.flag_ref), custom_call_target="tpu_custom_call" | custom-call | bytes 262144 | tf_op jit(solution)/shard_map/pallas_call | solution.py:328
  (26 shorter events, 0.5 us)
Async XLA Ops:
  2.6 4.2 %collective-permute-start = (f32[6,8,2,128]{3,2,1,0:T(2,128)S(1)}, f32[6,8,2,128]{3,2,1,0:T(2,128)S(1)}, u32[]{:S(2)}, u32[]{:S(2)}) collective-permute-start(f32[6,8,2,128]{3,2,1,0:T(2,128)S(1)} %pad_maximum_fusion), channel_id=1, source_target_pairs={{0,1},{1,2},{2,3},{3,0},{4,5},{5,6},{6,7},{7,4},{8,9},{9,10},{10,1... | collective-permute-start | bytes 147464 | tf_op jit(solution)/shard_map/ppermute | solution.py:345
  3.1 4.0 %collective-permute-start.1 = (f32[6,8,2,128]{3,2,1,0:T(2,128)S(1)}, f32[6,8,2,128]{3,2,1,0:T(2,128)S(1)}, u32[]{:S(2)}, u32[]{:S(2)}) collective-permute-start(f32[6,8,2,128]{3,2,1,0:T(2,128)S(1)} %pad_maximum_fusion.1), channel_id=1, source_target_pairs={{1,0},{2,1},{3,2},{0,3},{5,4},{6,5},{7,6},{4,7},{9,8},{10,9},{11,1... | collective-permute-start | bytes 147464 | tf_op jit(solution)/shard_map/ppermute | solution.py:345
  7.1 0.9 %copy-start = (f32[4,8,16,128]{3,2,1,0:T(8,128)S(1)}, f32[4,8,16,128]{3,2,1,0:T(8,128)}, u32[]{:S(2)}) copy-start(f32[4,8,16,128]{3,2,1,0:T(8,128)} %state_ref.5) | copy-start | bytes 786436
  8.1 0.8 %copy-start.1 = (s32[8,16,128]{2,1,0:T(8,128)S(1)}, s32[8,16,128]{2,1,0:T(8,128)}, u32[]{:S(2)}) copy-start(s32[8,16,128]{2,1,0:T(8,128)} %wet_ref.7) | copy-start | bytes 196612
  8.9 0.8 %copy-start.3 = (f32[8,16,128]{2,1,0:T(8,128)S(1)}, f32[8,16,128]{2,1,0:T(8,128)}, u32[]{:S(2)}) copy-start(f32[8,16,128]{2,1,0:T(8,128)} %thick_ref.5) | copy-start | bytes 196612
  10.2 7.3 %collective-permute-start.2 = (f32[24,128]{1,0:T(8,128)S(1)}, f32[24,128]{1,0:T(8,128)S(1)}, u32[]{:S(2)}, u32[]{:S(2)}) collective-permute-start(f32[24,128]{1,0:T(8,128)S(1)} %get-tuple-element.19), channel_id=1, source_target_pairs={{0,4},{4,8},{8,12},{12,16},{16,20},{20,24},{24,28},{28,0},{1,5},{5... | collective-permute-start | bytes 36872 | tf_op jit(solution)/shard_map/ppermute | solution.py:345
  12.3 5.3 %collective-permute-start.3 = (f32[24,128]{1,0:T(8,128)S(1)}, f32[24,128]{1,0:T(8,128)S(1)}, u32[]{:S(2)}, u32[]{:S(2)}) collective-permute-start(f32[24,128]{1,0:T(8,128)S(1)} %get-tuple-element.20), channel_id=1, source_target_pairs={{4,0},{8,4},{12,8},{16,12},{20,16},{24,20},{28,24},{0,28},{5,1},{9... | collective-permute-start | bytes 36872 | tf_op jit(solution)/shard_map/ppermute | solution.py:345
  15.8 9.1 %copy-start.5 = (s32[16]{0:T(128)S(1)}, s32[16]{0:T(128)}, u32[]{:S(2)}) copy-start(s32[16]{0:T(128)} %param.10) | copy-start | bytes 196
  17.5 16.9 %copy-start.4 = (f32[8,128,128]{2,1,0:T(8,128)S(1)}, f32[8,128,128]{2,1,0:T(8,128)}, u32[]{:S(2)}) copy-start(f32[8,128,128]{2,1,0:T(8,128)} %constant.48.basis_ref) | copy-start | bytes 1572868
  19.1 21.9 %copy-start.6 = (s32[16]{0:T(128)S(1)}, s32[16]{0:T(128)}, u32[]{:S(2)}) copy-start(s32[16]{0:T(128)} %param.11) | copy-start | bytes 196
  19.1 31.0 %copy-start.2 = (s32[8,16,128]{2,1,0:T(8,128)S(1)}, s32[8,16,128]{2,1,0:T(8,128)}, u32[]{:S(2)}) copy-start(s32[8,16,128]{2,1,0:T(8,128)} %wet_ref.7) | copy-start | bytes 196612
  19.1 15.2 %all-to-all-start = ((f32[8,64,128]{2,1,0:T(8,128)}), f32[8,64,128]{2,1,0:T(8,128)S(1)}, u32[]{:S(2)}, u32[]{:S(2)}) async-start(f32[8,64,128]{2,1,0:T(8,128)} %bitcast.6), calls=%async_computation | async-start | bytes 524288 | tf_op jit(solution)/shard_map/all_to_all | solution.py:427
  37.4 12.7 %all-to-all-start.1 = ((f32[8,64,128]{2,1,0:T(8,128)}), f32[8,64,128]{2,1,0:T(8,128)S(1)}, u32[]{:S(2)}, u32[]{:S(2)}) async-start(f32[8,64,128]{2,1,0:T(8,128)} %shard_map.77), calls=%async_computation.1 | async-start | bytes 524288 | tf_op jit(solution)/shard_map/all_to_all | solution.py:437

commit v5 on v4

--- a/solution.py
+++ b/solution.py
@@ -2,6 +2,7 @@
 
 import jax
 import jax.numpy as jnp
+import ml_dtypes
 import numpy as np
 from jax import lax
 from jax.experimental import pallas as pl
@@ -97,6 +98,27 @@
             w, h, hs = w_next, h_next, hs_next
 
 
+def load_kernel(
+    state_any, thick_any, wet_any, state_ref, thick_ref, wet_ref, first_ref, last_ref, raw_ref, sems
+):
+    levels, rows = thick_ref.shape[:2]
+    moves = [(wet_any, raw_ref), (thick_any, thick_ref)]
+    moves += [(state_any.at[f], state_ref.at[f]) for f in range(4)]
+    copies = [pltpu.make_async_copy(*pair, sems.at[i]) for i, pair in enumerate(moves)]
+    for copy in copies:
+        copy.start()
+    copies[0].wait()
+    for k in range(levels):
+        wet_ref[k] = raw_ref[k].astype(jnp.float32)
+    for copy in copies[1:]:
+        copy.wait()
+    for f in range(6):
+        for k in range(levels):
+            x = state_ref.at[f, k] if f < 4 else (thick_ref, wet_ref)[f - 4].at[k]
+            first_ref[f, k] = x[0:2]
+            last_ref[f, k] = x[rows - 2 : rows]
+
+
 def ready_kernel(state_ref, thick_ref, wet_ref, table_ref, own_ref, term_ref):
     levels, rows, lanes = thick_ref.shape
 
@@ -104,7 +126,7 @@
         return thick_ref[k]
 
     def wet(k):
-        return wet_ref[k].astype(jnp.float32)
+        return wet_ref[k]
 
     for f in range(4):
         own_ref[f] = own_columns(lambda k, f=f: state_ref[f, k], levels, lanes, rows)
@@ -139,7 +161,7 @@
                 elif f == 4:
                     x = thick_ref[k, part]
                 else:
-                    x = wet_ref[k, part].astype(jnp.float32)
+                    x = wet_ref[k, part]
                 at = GROUP * f + 2 * k
                 mine = (lane >= at) & (lane < at + 2)
                 first = jnp.where(mine, roll(x, at, 1), first)
@@ -177,7 +199,7 @@
     row_terms(halo(4), halo(5), table_ref[0, rows:], levels, halo_term_ref)
     for k in range(levels):
         h = joined(thick_ref[k], halo_ref[4, k])
-        w = joined(wet_ref[k].astype(jnp.float32), halo_ref[5, k])
+        w = joined(wet_ref[k], halo_ref[5, k])
         north_ref[0, k], north_ref[1, k] = north_terms(h, w, face)
         for f in range(4):
             out_ref[0, f, k] = joined(state_ref[f, k], halo_ref[f, k])
@@ -272,26 +294,37 @@
         pltpu.make_async_copy(out_ref.at[f], send_ref.at[f], sems.at[f]).wait()
 
 
+def split(x):
+    high = x.astype(jnp.bfloat16)
+    return high, (x - high.astype(jnp.float32)).astype(jnp.bfloat16)
+
+
 def product(a, b, dims):
-    return lax.dot_general(
-        a,
-        b,
-        (dims, ((), ())),
-        precision=lax.Precision.HIGHEST,
-        preferred_element_type=jnp.float32,
-    )
-
-
-def filter_kernel(circle_ref, basis_ref, weight_ref, out_ref, totals_ref, piece_ref, sems):
-    pieces = circle_ref.shape[0]
-    total = jnp.zeros(totals_ref.shape, jnp.float32)
-    for o in range(pieces):
-        total = total + product(circle_ref[o], basis_ref[o], ((1,), (0,)))
-    totals_ref[...] = total * weight_ref[...]
+    return lax.dot_general(a, b, (dims, ((), ())), preferred_element_type=jnp.float32)
+
+
+def filter_kernel(circle_ref, basis_ref, weight_ref, out_ref, piece_ref, sems):
+    pieces, part, lanes = circle_ref.shape
+    modes = weight_ref.shape[1]
+    pairs = range(0, pieces, 2)
+    total = jnp.zeros((2 * part, 2 * modes), jnp.float32)
+    for o in pairs:
+        parts = zip(split(circle_ref[o]), split(circle_ref[o + 1]))
+        x = jnp.concatenate([jnp.concatenate(p, axis=1) for p in parts], axis=0)
+        total = total + product(x, basis_ref[lanes * o : lanes * (o + 2)], ((1,), (0,)))
+    total = total[:part] + total[part:]
+    total = (total[:, :modes] + total[:, modes:]) * weight_ref[...]
+    y = jnp.concatenate([jnp.concatenate([p, p], axis=1) for p in split(total)], axis=0)
     copies = []
-    for o in range(pieces):
-        piece_ref[o] = product(totals_ref[...], basis_ref[o], ((1,), (1,)))
-        copies.append(pltpu.make_async_copy(piece_ref.at[o], out_ref.at[o], sems.at[o]))
+    for o in pairs:
+        x = product(y, basis_ref[lanes * o : lanes * (o + 2)], ((1,), (1,)))
+        x = x[:part] + x[part:]
+        piece_ref[o] = x[:, :lanes]
+        piece_ref[o + 1] = x[:, lanes:]
+        both = pl.ds(o, 2)
+        copies.append(
+            pltpu.make_async_copy(piece_ref.at[both], out_ref.at[both], sems.at[o // 2])
+        )
         copies[-1].start()
     for copy in copies:
         copy.wait()
@@ -304,7 +337,7 @@
     for f in range(4):
         for k in range(levels):
             state = state_ref[f, k]
-            gate = flag * wet_ref[k].astype(jnp.float32)
+            gate = flag * wet_ref[k]
             piece_ref[f, k] = state + gate * (smooth_ref[f, k] - state)
         copies.append(pltpu.make_async_copy(piece_ref.at[f], out_ref.at[f], sems.at[f]))
         copies[-1].start()
@@ -312,12 +345,13 @@
         copy.wait()
 
 
-def call(kernel, outs, scratch=(), sems=0, sent=False, flops=0):
+def call(kernel, outs, scratch=(), sems=0, raw=False, sent=False, flops=0):
     vmem = pl.BlockSpec(memory_space=pltpu.VMEM)
+    away = pl.BlockSpec(memory_space=pl.ANY)
     specs = [vmem] * len(outs)
     if sent:
-        specs[-1] = pl.BlockSpec(memory_space=pl.ANY)
-    buffers = [pltpu.VMEM(s, jnp.float32) for s in scratch]
+        specs[-1] = away
+    buffers = [pltpu.VMEM(s, jnp.float32) if isinstance(s, tuple) else s for s in scratch]
     if sems:
         buffers.append(pltpu.SemaphoreType.DMA((sems,)))
     cost = pl.CostEstimate(
@@ -325,10 +359,12 @@
     )
 
     def run(*args):
+        if raw:
+            args = [pltpu.with_memory_space_constraint(x, pltpu.HBM) for x in args]
         return pl.pallas_call(
             kernel,
             out_shape=[jax.ShapeDtypeStruct(s, jnp.float32) for s in outs],
-            in_specs=[vmem] * len(args),
+            in_specs=[away if raw else vmem] * len(args),
             out_specs=specs,
             scratch_shapes=buffers,
             compiler_params=pltpu.CompilerParams(vmem_limit_bytes=24 << 20),
@@ -348,7 +384,10 @@
 def mode_basis(length, modes):
     turns = np.arange(modes)[None, :] * np.arange(length)[:, None] % length
     angle = turns * (2.0 * math.pi / length)
-    return np.concatenate([np.cos(angle), np.sin(angle)], axis=1).astype(np.float32)
+    basis = np.concatenate([np.cos(angle), np.sin(angle)], axis=1).astype(np.float32)
+    high = basis.astype(ml_dtypes.bfloat16)
+    low = (basis - high.astype(np.float32)).astype(ml_dtypes.bfloat16)
+    return np.concatenate([high, low], axis=1)
 
 
 def mode_weights(counts, modes, length):
@@ -380,24 +419,21 @@
     total = 4 * levels * rows
     part = total // lon_peers
     table = row_table(lax.axis_index("lat"), rows, nlat)
-    block = (ocean_state, thickness, wet_mask)
     cells = 4 * levels * full * lanes
-
-    def edge_rows(part):
-        return jnp.concatenate(
-            [
-                ocean_state[:, :, part],
-                thickness[None, :, part],
-                wet_mask[None, :, part].astype(jnp.float32),
-            ]
-        )
-
-    below, above = swap_edges(
-        edge_rows(slice(rows - 2, rows)), edge_rows(slice(0, 2)), "lat"
-    )
+    edge_rows = (6, levels, 2, lanes)
+
+    *block, first, last = call(
+        load_kernel,
+        [ocean_state.shape, thickness.shape, thickness.shape, edge_rows, edge_rows],
+        [pltpu.VMEM(thickness.shape, jnp.int32)],
+        sems=6,
+        raw=True,
+    )(ocean_state, thickness, wet_mask)
+    below, above = swap_edges(last, first, "lat")
     own, terms = call(
         ready_kernel, [(6, rows, LANES), (5, levels, rows, lanes)], flops=20 * cells
     )(*block, table)
+    below, above, own, terms = lax.optimization_barrier((below, above, own, terms))
     first, last, halo = call(
         pack_kernel, [(full, LANES)] * 2 + [(6, levels, 8, lanes)]
     )(*block, below, above)
@@ -416,7 +452,7 @@
         sent=True,
     )(inner, edges, from_west, from_east, table)
 
-    basis = jnp.asarray(mode_basis(nlon, MAXM)).reshape(lon_peers, lanes, 2 * MAXM)
+    basis = jnp.asarray(mode_basis(nlon, MAXM))
     counts = mode_counts.astype(jnp.float32)
     row_counts = lax.dynamic_slice(
         jnp.broadcast_to(counts[None], (4 * levels, rows)).reshape(total),
@@ -430,14 +466,14 @@
     smooth = call(
         filter_kernel,
         [circles.shape],
-        [(part, 2 * MAXM), circles.shape],
-        sems=lon_peers,
+        [circles.shape],
+        sems=lon_peers // 2,
         sent=True,
     )(circles, basis, weights)[0]
     smooth = lax.all_to_all(smooth, "lon", 0, 0, tiled=True).reshape(ocean_state.shape)
     flags = jnp.broadcast_to(row_flags.astype(jnp.float32)[:, None], (rows, lanes))
     return call(blend_kernel, [ocean_state.shape], [ocean_state.shape], sems=4, sent=True)(
-        state, smooth, wet_mask, flags
+        state, smooth, block[2], flags
     )[0]
 
 

time: 51.6 us -> 45.1 us (0.87)
  local copies, waits for them, and re-layouts: 4.73 us -> 0.32 us
  other arithmetic: 1.72 us -> 0.89 us
  Pallas kernels: 7.75 us -> 7.04 us
    unnamed x14 -> x6, local copies, waits for them, and re-layouts: 2.65 us -> 0.02 us
    slice x1 -> x0, local copies, waits for them, and re-layouts: 0.99 us -> none  [edge_rows(): ocean_state[:, :, part]]
    broadcast_in_dim x1 -> x0, local copies, waits for them, and re-layouts: 0.78 us -> none  [edge_rows(): thickness[None, :, part]]
    convert_element_type x1 -> x0, other arithmetic: 0.78 us -> none  [edge_rows(): wet_mask[None, :, part].astype(jnp.float32)]
    pallas_call x6 -> x7, Pallas kernels: 7.75 us -> 7.04 us  [run(): pl.pallas_call(kernel, out_shape=[jax.ShapeDtypeStruct(s, jnp.float32) fo...]
  transfers between devices with their start and end apart: 6 -> 6, of which waited for: 4 -> 4; matrix products, arithmetic and copies ran while one was open for 2% -> 3% of each run, Pallas kernels for 4% -> 4%
where the time goes in v5:
time: 45.1 us; the launch traced here: 44.8 us
  waiting for transfers between devices  19.2 us (43%)
  starting transfers between devices  17.2 us (38%)
  Pallas kernels  7.04 us (16%)
  other arithmetic  0.89 us (2%)
    all_to_all x1, waiting for transfers between devices, shards(): lax.all_to_all(sent.reshape(lon_peers, part, lanes), 'lon', 0, 0, tiled=T...  9.18 us
    all_to_all x1, waiting for transfers between devices, shards(): lax.all_to_all(smooth, 'lon', 0, 0, tiled=True).reshape(ocean_state.shape)  9.08 us
    pallas_call x7, Pallas kernels, run(): pl.pallas_call(kernel, out_shape=[jax.ShapeDtypeStruct(s, jnp.float32) fo...  7.04 us
    all_to_all x1, starting transfers between devices, shards(): lax.all_to_all(sent.reshape(lon_peers, part, lanes), 'lon', 0, 0, tiled=T...  5.94 us
    ppermute x2, starting transfers between devices, swap_edges(): lax.ppermute(after_src, axis, down)  5.09 us
    all_to_all x1, starting transfers between devices, shards(): lax.all_to_all(smooth, 'lon', 0, 0, tiled=True).reshape(ocean_state.shape)  3.6 us
    ppermute x2, starting transfers between devices, swap_edges(): lax.ppermute(before_src, axis, up)  2.54 us
  transfers between devices with their start and end apart: 6, of which 4 were waited for; matrix products, arithmetic and copies ran while one was open for 3% of the time, Pallas kernels for 4%

profile of v5, /device:TPU:0, one launch (start us, length us, event | category | flops | bytes accessed | tf_op | source)
XLA Modules:
  0.0 44.8 jit_solution(12811872789610658055)
XLA Ops:
  0.0 1.1 %shard_map.73 = (f32[4,8,16,128]{3,2,1,0:T(8,128)S(1)}, f32[8,16,128]{2,1,0:T(8,128)S(1)}, f32[8,16,128]{2,1,0:T(8,128)S(1)}, f32[6,8,2,128]{3,2,1,0:T(2,128)S(1)}, f32[6,8,2,128]{3,2,1,0:T(2,128)S(1)}) custom-call(f32[4,8,16,128]{3,2,1,0:T(8,128)} %state_any.1, f32[8,16,128]{2,1,0:T(8,128)} %thick_any.1, s32[8,16,128]{2,1,0:T(8,128)} %wet_any.1), custom_call_target="tpu_custom_call" | custom-call | bytes 491520 | tf_op jit(solution)/shard_map/pallas_call | solution.py:364
  1.1 0.5 %collective-permute-start = (f32[6,8,2,128]{3,2,1,0:T(2,128)S(1)}, f32[6,8,2,128]{3,2,1,0:T(2,128)S(1)}, u32[]{:S(2)}, u32[]{:S(2)}) collective-permute-start(f32[6,8,2,128]{3,2,1,0:T(2,128)S(1)} %get-tuple-element.26), channel_id=1, source_target_pairs={{0,1},{1,2},{2,3},{3,0},{4,5},{5,6},{6,7},{7,4},{8,9},{9,10},{10,1... | collective-permute-start | bytes 147464 | tf_op jit(solution)/shard_map/ppermute | solution.py:381
  1.6 2.0 %collective-permute-start.1 = (f32[6,8,2,128]{3,2,1,0:T(2,128)S(1)}, f32[6,8,2,128]{3,2,1,0:T(2,128)S(1)}, u32[]{:S(2)}, u32[]{:S(2)}) collective-permute-start(f32[6,8,2,128]{3,2,1,0:T(2,128)S(1)} %get-tuple-element.27), channel_id=1, source_target_pairs={{1,0},{2,1},{3,2},{0,3},{5,4},{6,5},{7,6},{4,7},{9,8},{10,9},{11,1... | collective-permute-start | bytes 147464 | tf_op jit(solution)/shard_map/ppermute | solution.py:381
  3.6 0.7 %divide_bitcast_fusion = (f32[1,24]{1,0:T(1,128)S(1)}, f32[1,24]{1,0:T(1,128)S(1)}) fusion(s32[24]{0:T(128)} %constant.46.clone, s32[]{:T(128)S(6)} %mul.22), kind=kLoop, calls=%fused_computation.7 | loop fusion | flops 264 | bytes 292 | tf_op jit(solution)/shard_map/stack | solution.py:407
  4.3 0.1 broadcast_in_dim.14.table_ref
  4.4 0.3 shard_map.74
  4.7 0.6 %collective-permute-done.below_ref = f32[6,8,2,128]{3,2,1,0:T(2,128)S(1)} collective-permute-done((f32[6,8,2,128]{3,2,1,0:T(2,128)S(1)}, f32[6,8,2,128]{3,2,1,0:T(2,128)S(1)}, u32[]{:S(2)}, u32[]{:S(2)}) %collective-permute-start) | collective-permute-done | bytes 49184 | tf_op jit(solution)/shard_map/ppermute | solution.py:381
  5.3 0.3 collective-permute-done.1.above_ref
  5.6 0.4 shard_map.75
  6.0 2.0 %collective-permute-start.2 = (f32[24,128]{1,0:T(8,128)S(1)}, f32[24,128]{1,0:T(8,128)S(1)}, u32[]{:S(2)}, u32[]{:S(2)}) collective-permute-start(f32[24,128]{1,0:T(8,128)S(1)} %get-tuple-element.37), channel_id=1, source_target_pairs={{0,4},{4,8},{8,12},{12,16},{16,20},{20,24},{24,28},{28,0},{1,5},{5... | collective-permute-start | bytes 36872 | tf_op jit(solution)/shard_map/ppermute | solution.py:381
  8.1 3.1 %collective-permute-start.3 = (f32[24,128]{1,0:T(8,128)S(1)}, f32[24,128]{1,0:T(8,128)S(1)}, u32[]{:S(2)}, u32[]{:S(2)}) collective-permute-start(f32[24,128]{1,0:T(8,128)S(1)} %get-tuple-element.38), channel_id=1, source_target_pairs={{4,0},{8,4},{12,8},{16,12},{20,16},{24,20},{28,24},{0,28},{5,1},{9... | collective-permute-start | bytes 36872 | tf_op jit(solution)/shard_map/ppermute | solution.py:381
  11.2 1.7 %shard_map.76 = (f32[3,4,8,24,128]{4,3,2,1,0:T(8,128)S(1)}, f32[6,24,128]{2,1,0:T(8,128)S(1)}) custom-call(f32[4,8,16,128]{3,2,1,0:T(8,128)S(1)} %get-tuple-element.23.state_ref, f32[8,16,128]{2,1,0:T(8,128)S(1)} %get-tuple-element.24.thick_ref, f32[8,16,128]{2,1,0:T(8,128)S(1)} %get-tuple-element.25.wet_ref, ...), custom_call_target="tpu_custom_call" | custom-call | flops 5898240 | bytes 1253376 | tf_op jit(solution)/shard_map/pallas_call | solution.py:364
  12.9 1.6 %shard_map.77 = (f32[4,8,16,128]{3,2,1,0:T(8,128)S(1)}, f32[4,8,16,128]{3,2,1,0:T(8,128)}) custom-call(f32[3,4,8,24,128]{4,3,2,1,0:T(8,128)S(1)} %get-tuple-element.35.inner_ref, f32[6,24,128]{2,1,0:T(8,128)S(1)} %get-tuple-element.36.own_ref, f32[24,128]{1,0:T(8,128)S(1)} %collective-permute-done.2.west_ref, f32[24,128]{1,0:T(8,128)S(1)} %collective-permute-done.3.east_ref, ...), custom_call_target="tpu_custom_call" | custom-call | bytes 524288 | tf_op jit(solution)/shard_map/pallas_call | solution.py:364
  14.5 5.9 %all-to-all-start = ((f32[8,64,128]{2,1,0:T(8,128)}), f32[8,64,128]{2,1,0:T(8,128)S(1)}, u32[]{:S(2)}, u32[]{:S(2)}) async-start(f32[8,64,128]{2,1,0:T(8,128)} %bitcast.2), calls=%async_computation | async-start | bytes 524288 | tf_op jit(solution)/shard_map/all_to_all | solution.py:463
  20.5 0.1 reshape.23
  20.6 0.1 dynamic_slice.3
  20.7 0.1 compare_select_fusion
  20.7 0.1 pad_maximum_fusion.weight_ref
  20.8 9.2 %all-to-all-done.circle_ref = f32[8,64,128]{2,1,0:T(8,128)S(1)} async-done(((f32[8,64,128]{2,1,0:T(8,128)}), f32[8,64,128]{2,1,0:T(8,128)S(1)}, u32[]{:S(2)}, u32[]{:S(2)}) %all-to-all-start) | async-done | bytes 262176 | tf_op jit(solution)/shard_map/all_to_all | solution.py:463
  30.0 1.2 %shard_map.78 = f32[8,64,128]{2,1,0:T(8,128)} custom-call(f32[8,64,128]{2,1,0:T(8,128)S(1)} %all-to-all-done.circle_ref, bf16[1024,256]{1,0:T(8,128)(2,1)S(1)} %copy-done, f32[64,128]{1,0:T(8,128)S(1)} %pad_maximum_fusion.weight_ref), custom_call_target="tpu_custom_call" | custom-call | bytes 262144 | tf_op jit(solution)/shard_map/pallas_call | solution.py:364
  31.2 3.6 %all-to-all-start.1 = ((f32[8,64,128]{2,1,0:T(8,128)}), f32[8,64,128]{2,1,0:T(8,128)S(1)}, u32[]{:S(2)}, u32[]{:S(2)}) async-start(f32[8,64,128]{2,1,0:T(8,128)} %shard_map.78), calls=%async_computation.1 | async-start | bytes 524288 | tf_op jit(solution)/shard_map/all_to_all | solution.py:473
  34.9 9.1 %all-to-all-done.1 = f32[8,64,128]{2,1,0:T(8,128)S(1)} async-done(((f32[8,64,128]{2,1,0:T(8,128)}), f32[8,64,128]{2,1,0:T(8,128)S(1)}, u32[]{:S(2)}, u32[]{:S(2)}) %all-to-all-start.1) | async-done | bytes 262176 | tf_op jit(solution)/shard_map/all_to_all | solution.py:473
  43.9 0.1 broadcast_in_dim.18.flag_ref
  44.0 0.7 %shard_map.79 = f32[4,8,16,128]{3,2,1,0:T(8,128)} custom-call(f32[4,8,16,128]{3,2,1,0:T(8,128)S(1)} %get-tuple-element.39.state_ref, f32[4,8,16,128]{3,2,1,0:T(8,128)S(1)} %bitcast.6, f32[8,16,128]{2,1,0:T(8,128)S(1)} %get-tuple-element.25.wet_ref, f32[16,128]{1,0:T(8,128)S(1)} %broadcast_in_dim.18.flag_ref), custom_call_target="tpu_custom_call" | custom-call | bytes 262144 | tf_op jit(solution)/shard_map/pallas_call | solution.py:364
  (14 shorter events, 0.1 us)
Async XLA Ops:
  1.1 4.2 %collective-permute-start = (f32[6,8,2,128]{3,2,1,0:T(2,128)S(1)}, f32[6,8,2,128]{3,2,1,0:T(2,128)S(1)}, u32[]{:S(2)}, u32[]{:S(2)}) collective-permute-start(f32[6,8,2,128]{3,2,1,0:T(2,128)S(1)} %get-tuple-element.26), channel_id=1, source_target_pairs={{0,1},{1,2},{2,3},{3,0},{4,5},{5,6},{6,7},{7,4},{8,9},{9,10},{10,1... | collective-permute-start | bytes 147464 | tf_op jit(solution)/shard_map/ppermute | solution.py:381
  1.6 4.0 %collective-permute-start.1 = (f32[6,8,2,128]{3,2,1,0:T(2,128)S(1)}, f32[6,8,2,128]{3,2,1,0:T(2,128)S(1)}, u32[]{:S(2)}, u32[]{:S(2)}) collective-permute-start(f32[6,8,2,128]{3,2,1,0:T(2,128)S(1)} %get-tuple-element.27), channel_id=1, source_target_pairs={{1,0},{2,1},{3,2},{0,3},{5,4},{6,5},{7,6},{4,7},{9,8},{10,9},{11,1... | collective-permute-start | bytes 147464 | tf_op jit(solution)/shard_map/ppermute | solution.py:381
  6.0 6.9 %collective-permute-start.2 = (f32[24,128]{1,0:T(8,128)S(1)}, f32[24,128]{1,0:T(8,128)S(1)}, u32[]{:S(2)}, u32[]{:S(2)}) collective-permute-start(f32[24,128]{1,0:T(8,128)S(1)} %get-tuple-element.37), channel_id=1, source_target_pairs={{0,4},{4,8},{8,12},{12,16},{16,20},{20,24},{24,28},{28,0},{1,5},{5... | collective-permute-start | bytes 36872 | tf_op jit(solution)/shard_map/ppermute | solution.py:381
  8.1 4.8 %collective-permute-start.3 = (f32[24,128]{1,0:T(8,128)S(1)}, f32[24,128]{1,0:T(8,128)S(1)}, u32[]{:S(2)}, u32[]{:S(2)}) collective-permute-start(f32[24,128]{1,0:T(8,128)S(1)} %get-tuple-element.38), channel_id=1, source_target_pairs={{4,0},{8,4},{12,8},{16,12},{20,16},{24,20},{28,24},{0,28},{5,1},{9... | collective-permute-start | bytes 36872 | tf_op jit(solution)/shard_map/ppermute | solution.py:381
  11.2 9.3 %copy-start.1 = (s32[16]{0:T(128)S(1)}, s32[16]{0:T(128)}, u32[]{:S(2)}) copy-start(s32[16]{0:T(128)} %param.10) | copy-start | bytes 196
  12.9 17.1 %copy-start = (bf16[1024,256]{1,0:T(8,128)(2,1)S(1)}, bf16[1024,256]{1,0:T(8,128)(2,1)}, u32[]{:S(2)}) copy-start(bf16[1024,256]{1,0:T(8,128)(2,1)} %constant.47.clone.basis_ref) | copy-start | bytes 1572868
  14.5 20.3 %copy-start.2 = (s32[16]{0:T(128)S(1)}, s32[16]{0:T(128)}, u32[]{:S(2)}) copy-start(s32[16]{0:T(128)} %param.11) | copy-start | bytes 196
  14.5 15.5 %all-to-all-start = ((f32[8,64,128]{2,1,0:T(8,128)}), f32[8,64,128]{2,1,0:T(8,128)S(1)}, u32[]{:S(2)}, u32[]{:S(2)}) async-start(f32[8,64,128]{2,1,0:T(8,128)} %bitcast.2), calls=%async_computation | async-start | bytes 524288 | tf_op jit(solution)/shard_map/all_to_all | solution.py:463
  31.2 12.7 %all-to-all-start.1 = ((f32[8,64,128]{2,1,0:T(8,128)}), f32[8,64,128]{2,1,0:T(8,128)S(1)}, u32[]{:S(2)}, u32[]{:S(2)}) async-start(f32[8,64,128]{2,1,0:T(8,128)} %shard_map.78), calls=%async_computation.1 | async-start | bytes 524288 | tf_op jit(solution)/shard_map/all_to_all | solution.py:473

commit v6 on v5

--- a/solution.py
+++ b/solution.py
@@ -9,6 +9,7 @@
 from jax.experimental.pallas import tpu as pltpu
 from jax.sharding import PartitionSpec as P
 
+FBAND = 16
 MAXM = 64
 LANES = 128
 GROUP = 16
@@ -418,7 +419,8 @@
     full = rows + 8
     total = 4 * levels * rows
     part = total // lon_peers
-    table = row_table(lax.axis_index("lat"), rows, nlat)
+    lat_pos = lax.axis_index("lat")
+    table = row_table(lat_pos, rows, nlat)
     cells = 4 * levels * full * lanes
     edge_rows = (6, levels, 2, lanes)
 
@@ -452,29 +454,31 @@
         sent=True,
     )(inner, edges, from_west, from_east, table)
 
-    basis = jnp.asarray(mode_basis(nlon, MAXM))
-    counts = mode_counts.astype(jnp.float32)
-    row_counts = lax.dynamic_slice(
-        jnp.broadcast_to(counts[None], (4 * levels, rows)).reshape(total),
-        (lax.axis_index("lon") * part,),
-        (part,),
-    )
-    weights = mode_weights(row_counts, MAXM, nlon)
-    circles = lax.all_to_all(
-        sent.reshape(lon_peers, part, lanes), "lon", 0, 0, tiled=True
-    )
-    smooth = call(
-        filter_kernel,
-        [circles.shape],
-        [circles.shape],
-        sems=lon_peers // 2,
-        sent=True,
-    )(circles, basis, weights)[0]
-    smooth = lax.all_to_all(smooth, "lon", 0, 0, tiled=True).reshape(ocean_state.shape)
-    flags = jnp.broadcast_to(row_flags.astype(jnp.float32)[:, None], (rows, lanes))
-    return call(blend_kernel, [ocean_state.shape], [ocean_state.shape], sems=4, sent=True)(
-        state, smooth, block[2], flags
-    )[0]
+    basis = lax.optimization_barrier(jnp.asarray(mode_basis(nlon, MAXM)))
+
+    def filtered(state, sent, wet):
+        counts = mode_counts.astype(jnp.float32)
+        row_counts = lax.dynamic_slice(
+            jnp.broadcast_to(counts[None], (4 * levels, rows)).reshape(total),
+            (lax.axis_index("lon") * part,),
+            (part,),
+        )
+        weights = mode_weights(row_counts, MAXM, nlon)
+        circles = lax.all_to_all(
+            sent.reshape(lon_peers, part, lanes), "lon", 0, 0, tiled=True
+        )
+        smooth = call(
+            filter_kernel, [circles.shape], [circles.shape], sems=lon_peers // 2, sent=True
+        )(circles, basis, weights)[0]
+        smooth = lax.all_to_all(smooth, "lon", 0, 0, tiled=True).reshape(state.shape)
+        flags = jnp.broadcast_to(row_flags.astype(jnp.float32)[:, None], (rows, lanes))
+        return call(blend_kernel, [state.shape], [state.shape], sems=4, sent=True)(
+            state, smooth, wet, flags
+        )[0]
+
+    first_row = lat_pos * rows
+    banded = (first_row < FBAND) | (first_row + rows > nlat - FBAND)
+    return lax.cond(banded, filtered, lambda state, sent, wet: sent, state, sent, block[2])
 
 
 def solution(mesh):

time: 45.1 us -> 42.8 us (0.949)
  waiting for transfers between devices: 19.2 us -> 17 us
    all_to_all x2, waiting for transfers between devices: 18.3 us -> 16 us  [the longest x1 8.15 us: filtered(): lax.all_to_all(smooth, 'lon', 0, 0, tiled=True).reshape(state.shape)]
  transfers between devices with their start and end apart: 6 -> 6, of which waited for: 4 -> 4; matrix products, arithmetic and copies ran while one was open for 3% -> 3% of each run, Pallas kernels for 4% -> 5%
where the time goes in v6:
time: 42.8 us; the launch traced here: 42.4 us
  starting transfers between devices  17 us (40%)
  waiting for transfers between devices  17 us (40%)
  Pallas kernels  7.05 us (16%)
  other arithmetic  0.89 us (2%)
    all_to_all x1, waiting for transfers between devices, filtered(): lax.all_to_all(smooth, 'lon', 0, 0, tiled=True).reshape(state.shape)  8.15 us
    all_to_all x1, waiting for transfers between devices, filtered(): lax.all_to_all(sent.reshape(lon_peers, part, lanes), 'lon', 0, 0, tiled=T...  7.87 us
    pallas_call x7, Pallas kernels, run(): pl.pallas_call(kernel, out_shape=[jax.ShapeDtypeStruct(s, jnp.float32) fo...  7.05 us
    all_to_all x1, starting transfers between devices, filtered(): lax.all_to_all(sent.reshape(lon_peers, part, lanes), 'lon', 0, 0, tiled=T...  5.94 us
    ppermute x2, starting transfers between devices, swap_edges(): lax.ppermute(after_src, axis, down)  5.09 us
    all_to_all x1, starting transfers between devices, filtered(): lax.all_to_all(smooth, 'lon', 0, 0, tiled=True).reshape(state.shape)  3.42 us
    ppermute x2, starting transfers between devices, swap_edges(): lax.ppermute(before_src, axis, up)  2.54 us
  transfers between devices with their start and end apart: 6, of which 4 were waited for; matrix products, arithmetic and copies ran while one was open for 3% of the time, Pallas kernels for 5%

profile of v6, /device:TPU:0, one launch (start us, length us, event | category | flops | bytes accessed | tf_op | source)
XLA Modules:
  0.0 42.4 jit_solution(14615380295240471850)
XLA Ops:
  0.0 1.1 %shard_map.77 = (f32[4,8,16,128]{3,2,1,0:T(8,128)S(1)}, f32[8,16,128]{2,1,0:T(8,128)S(1)}, f32[8,16,128]{2,1,0:T(8,128)S(1)}, f32[6,8,2,128]{3,2,1,0:T(2,128)S(1)}, f32[6,8,2,128]{3,2,1,0:T(2,128)S(1)}) custom-call(f32[4,8,16,128]{3,2,1,0:T(8,128)} %state_any.1, f32[8,16,128]{2,1,0:T(8,128)} %thick_any.1, s32[8,16,128]{2,1,0:T(8,128)} %wet_any.1), custom_call_target="tpu_custom_call" | custom-call | bytes 491520 | tf_op jit(solution)/shard_map/pallas_call | solution.py:365
  1.1 0.5 %collective-permute-start = (f32[6,8,2,128]{3,2,1,0:T(2,128)S(1)}, f32[6,8,2,128]{3,2,1,0:T(2,128)S(1)}, u32[]{:S(2)}, u32[]{:S(2)}) collective-permute-start(f32[6,8,2,128]{3,2,1,0:T(2,128)S(1)} %get-tuple-element.48), channel_id=1, source_target_pairs={{0,1},{1,2},{2,3},{3,0},{4,5},{5,6},{6,7},{7,4},{8,9},{9,10},{10,1... | collective-permute-start | bytes 147464 | tf_op jit(solution)/shard_map/ppermute | solution.py:382
  1.6 2.0 %collective-permute-start.1 = (f32[6,8,2,128]{3,2,1,0:T(2,128)S(1)}, f32[6,8,2,128]{3,2,1,0:T(2,128)S(1)}, u32[]{:S(2)}, u32[]{:S(2)}) collective-permute-start(f32[6,8,2,128]{3,2,1,0:T(2,128)S(1)} %get-tuple-element.49), channel_id=1, source_target_pairs={{1,0},{2,1},{3,2},{0,3},{5,4},{6,5},{7,6},{4,7},{9,8},{10,9},{11,1... | collective-permute-start | bytes 147464 | tf_op jit(solution)/shard_map/ppermute | solution.py:382
  3.6 0.7 %divide_bitcast_fusion = (f32[1,24]{1,0:T(1,128)S(1)}, f32[1,24]{1,0:T(1,128)S(1)}) fusion(s32[24]{0:T(128)} %constant.50.clone, s32[]{:T(128)S(6)} %mul.23), kind=kLoop, calls=%fused_computation.7 | loop fusion | flops 264 | bytes 292 | tf_op jit(solution)/shard_map/stack | solution.py:408
  4.3 0.1 broadcast_in_dim.14.table_ref
  4.4 0.3 shard_map.78
  4.7 0.6 %collective-permute-done.below_ref = f32[6,8,2,128]{3,2,1,0:T(2,128)S(1)} collective-permute-done((f32[6,8,2,128]{3,2,1,0:T(2,128)S(1)}, f32[6,8,2,128]{3,2,1,0:T(2,128)S(1)}, u32[]{:S(2)}, u32[]{:S(2)}) %collective-permute-start) | collective-permute-done | bytes 49184 | tf_op jit(solution)/shard_map/ppermute | solution.py:382
  5.3 0.3 collective-permute-done.1.above_ref
  5.6 0.4 shard_map.79
  6.1 2.0 %collective-permute-start.2 = (f32[24,128]{1,0:T(8,128)S(1)}, f32[24,128]{1,0:T(8,128)S(1)}, u32[]{:S(2)}, u32[]{:S(2)}) collective-permute-start(f32[24,128]{1,0:T(8,128)S(1)} %get-tuple-element.59), channel_id=1, source_target_pairs={{0,4},{4,8},{8,12},{12,16},{16,20},{20,24},{24,28},{28,0},{1,5},{5... | collective-permute-start | bytes 36872 | tf_op jit(solution)/shard_map/ppermute | solution.py:382
  8.1 3.1 %collective-permute-start.3 = (f32[24,128]{1,0:T(8,128)S(1)}, f32[24,128]{1,0:T(8,128)S(1)}, u32[]{:S(2)}, u32[]{:S(2)}) collective-permute-start(f32[24,128]{1,0:T(8,128)S(1)} %get-tuple-element.60), channel_id=1, source_target_pairs={{4,0},{8,4},{12,8},{16,12},{20,16},{24,20},{28,24},{0,28},{5,1},{9... | collective-permute-start | bytes 36872 | tf_op jit(solution)/shard_map/ppermute | solution.py:382
  11.2 1.7 %shard_map.80 = (f32[3,4,8,24,128]{4,3,2,1,0:T(8,128)S(1)}, f32[6,24,128]{2,1,0:T(8,128)S(1)}) custom-call(f32[4,8,16,128]{3,2,1,0:T(8,128)S(1)} %get-tuple-element.45.state_ref, f32[8,16,128]{2,1,0:T(8,128)S(1)} %get-tuple-element.46.thick_ref, f32[8,16,128]{2,1,0:T(8,128)S(1)} %get-tuple-element.47.wet_ref, ...), custom_call_target="tpu_custom_call" | custom-call | flops 5898240 | bytes 1253376 | tf_op jit(solution)/shard_map/pallas_call | solution.py:365
  12.9 1.6 %shard_map.81 = (f32[4,8,16,128]{3,2,1,0:T(8,128)S(1)}, f32[4,8,16,128]{3,2,1,0:T(8,128)}) custom-call(f32[3,4,8,24,128]{4,3,2,1,0:T(8,128)S(1)} %get-tuple-element.57.inner_ref, f32[6,24,128]{2,1,0:T(8,128)S(1)} %get-tuple-element.58.own_ref, f32[24,128]{1,0:T(8,128)S(1)} %collective-permute-done.2.west_ref, f32[24,128]{1,0:T(8,128)S(1)} %collective-permute-done.3.east_ref, ...), custom_call_target="tpu_custom_call" | custom-call | bytes 524288 | tf_op jit(solution)/shard_map/pallas_call | solution.py:365
  14.6 27.8 %conditional.1 = (f32[4,8,16,128]{3,2,1,0:T(8,128)}) conditional(s32[]{:T(128)} %convert_element_type.25, f32[4,8,16,128]{3,2,1,0:T(8,128)} %get-tuple-element.61, (f32[4,8,16,128]{3,2,1,0:T(8,128)}, s32[16]{0:T(128)S(1)}, bf16[1024,256]{1,0:T(8,128)(2,1)S(1)}, s32[16]{0:T(128)S(1)}, f32[4,8,16,128]{3,2,1,0:T(8,128)S(1)}, ...), branch_computations={%region_0.0_spmd, %region_1.2_spmd} | conditional | flops 16743 | bytes 2179354 | solution.py:481
  14.6 5.9 %all-to-all-start = ((f32[8,64,128]{2,1,0:T(8,128)}), f32[8,64,128]{2,1,0:T(8,128)S(1)}, u32[]{:S(2)}, u32[]{:S(2)}) async-start(f32[8,64,128]{2,1,0:T(8,128)} %bitcast), calls=%async_computation | async-start | bytes 524288 | tf_op jit(solution)/shard_map/cond/branch_1_fun/all_to_all | solution.py:467
  20.6 0.1 reshape.20
  20.6 0.1 dynamic_slice.2
  20.7 0.1 compare_select_fusion
  20.8 0.1 pad_maximum_fusion.weight_ref
  20.9 7.9 %all-to-all-done.circle_ref = f32[8,64,128]{2,1,0:T(8,128)S(1)} async-done(((f32[8,64,128]{2,1,0:T(8,128)}), f32[8,64,128]{2,1,0:T(8,128)S(1)}, u32[]{:S(2)}, u32[]{:S(2)}) %all-to-all-start) | async-done | bytes 262176 | tf_op jit(solution)/shard_map/cond/branch_1_fun/all_to_all | solution.py:467
  28.8 1.2 %branch_1_fun.2 = f32[8,64,128]{2,1,0:T(8,128)} custom-call(f32[8,64,128]{2,1,0:T(8,128)S(1)} %all-to-all-done.circle_ref, bf16[1024,256]{1,0:T(8,128)(2,1)S(1)} %get-tuple-element.23.basis_ref, f32[64,128]{1,0:T(8,128)S(1)} %pad_maximum_fusion.weight_ref), custom_call_target="tpu_custom_call" | custom-call | bytes 262144 | tf_op jit(solution)/shard_map/cond/branch_1_fun/pallas_call | solution.py:365
  30.0 3.4 %all-to-all-start.1 = ((f32[8,64,128]{2,1,0:T(8,128)}), f32[8,64,128]{2,1,0:T(8,128)S(1)}, u32[]{:S(2)}, u32[]{:S(2)}) async-start(f32[8,64,128]{2,1,0:T(8,128)} %branch_1_fun.2), calls=%async_computation.1 | async-start | bytes 524288 | tf_op jit(solution)/shard_map/cond/branch_1_fun/all_to_all | solution.py:473
  33.4 8.1 %all-to-all-done.1 = f32[8,64,128]{2,1,0:T(8,128)S(1)} async-done(((f32[8,64,128]{2,1,0:T(8,128)}), f32[8,64,128]{2,1,0:T(8,128)S(1)}, u32[]{:S(2)}, u32[]{:S(2)}) %all-to-all-start.1) | async-done | bytes 262176 | tf_op jit(solution)/shard_map/cond/branch_1_fun/all_to_all | solution.py:473
  41.7 0.8 %branch_1_fun.3 = f32[4,8,16,128]{3,2,1,0:T(8,128)} custom-call(f32[4,8,16,128]{3,2,1,0:T(8,128)S(1)} %get-tuple-element.21.state_ref, f32[4,8,16,128]{3,2,1,0:T(8,128)S(1)} %bitcast.6, f32[8,16,128]{2,1,0:T(8,128)S(1)} %get-tuple-element.25.wet_ref, f32[16,128]{1,0:T(8,128)S(1)} %broadcast_in_dim.10.flag_ref), custom_call_target="tpu_custom_call" | custom-call | bytes 262144 | tf_op jit(solution)/shard_map/cond/branch_1_fun/pallas_call | solution.py:365
  (15 shorter events, 0.1 us)
Async XLA Ops:
  1.1 4.2 %collective-permute-start = (f32[6,8,2,128]{3,2,1,0:T(2,128)S(1)}, f32[6,8,2,128]{3,2,1,0:T(2,128)S(1)}, u32[]{:S(2)}, u32[]{:S(2)}) collective-permute-start(f32[6,8,2,128]{3,2,1,0:T(2,128)S(1)} %get-tuple-element.48), channel_id=1, source_target_pairs={{0,1},{1,2},{2,3},{3,0},{4,5},{5,6},{6,7},{7,4},{8,9},{9,10},{10,1... | collective-permute-start | bytes 147464 | tf_op jit(solution)/shard_map/ppermute | solution.py:382
  1.6 4.0 %collective-permute-start.1 = (f32[6,8,2,128]{3,2,1,0:T(2,128)S(1)}, f32[6,8,2,128]{3,2,1,0:T(2,128)S(1)}, u32[]{:S(2)}, u32[]{:S(2)}) collective-permute-start(f32[6,8,2,128]{3,2,1,0:T(2,128)S(1)} %get-tuple-element.49), channel_id=1, source_target_pairs={{1,0},{2,1},{3,2},{0,3},{5,4},{6,5},{7,6},{4,7},{9,8},{10,9},{11,1... | collective-permute-start | bytes 147464 | tf_op jit(solution)/shard_map/ppermute | solution.py:382
  6.0 8.5 %copy-start = (bf16[1024,256]{1,0:T(8,128)(2,1)S(1)}, bf16[1024,256]{1,0:T(8,128)(2,1)}, u32[]{:S(2)}) copy-start(bf16[1024,256]{1,0:T(8,128)(2,1)} %constant.51.clone) | copy-start | bytes 1572868
  6.0 8.5 %copy-start.1 = (s32[16]{0:T(128)S(1)}, s32[16]{0:T(128)}, u32[]{:S(2)}) copy-start(s32[16]{0:T(128)} %param.12) | copy-start | bytes 196
  6.1 8.5 %copy-start.2 = (s32[16]{0:T(128)S(1)}, s32[16]{0:T(128)}, u32[]{:S(2)}) copy-start(s32[16]{0:T(128)} %param.13) | copy-start | bytes 196
  6.1 6.9 %collective-permute-start.2 = (f32[24,128]{1,0:T(8,128)S(1)}, f32[24,128]{1,0:T(8,128)S(1)}, u32[]{:S(2)}, u32[]{:S(2)}) collective-permute-start(f32[24,128]{1,0:T(8,128)S(1)} %get-tuple-element.59), channel_id=1, source_target_pairs={{0,4},{4,8},{8,12},{12,16},{16,20},{20,24},{24,28},{28,0},{1,5},{5... | collective-permute-start | bytes 36872 | tf_op jit(solution)/shard_map/ppermute | solution.py:382
  8.1 4.8 %collective-permute-start.3 = (f32[24,128]{1,0:T(8,128)S(1)}, f32[24,128]{1,0:T(8,128)S(1)}, u32[]{:S(2)}, u32[]{:S(2)}) collective-permute-start(f32[24,128]{1,0:T(8,128)S(1)} %get-tuple-element.60), channel_id=1, source_target_pairs={{4,0},{8,4},{12,8},{16,12},{20,16},{24,20},{28,24},{0,28},{5,1},{9... | collective-permute-start | bytes 36872 | tf_op jit(solution)/shard_map/ppermute | solution.py:382
  14.6 14.2 %all-to-all-start = ((f32[8,64,128]{2,1,0:T(8,128)}), f32[8,64,128]{2,1,0:T(8,128)S(1)}, u32[]{:S(2)}, u32[]{:S(2)}) async-start(f32[8,64,128]{2,1,0:T(8,128)} %bitcast), calls=%async_computation | async-start | bytes 524288 | tf_op jit(solution)/shard_map/cond/branch_1_fun/all_to_all | solution.py:467
  30.0 11.6 %all-to-all-start.1 = ((f32[8,64,128]{2,1,0:T(8,128)}), f32[8,64,128]{2,1,0:T(8,128)S(1)}, u32[]{:S(2)}, u32[]{:S(2)}) async-start(f32[8,64,128]{2,1,0:T(8,128)} %branch_1_fun.2), calls=%async_computation.1 | async-start | bytes 524288 | tf_op jit(solution)/shard_map/cond/branch_1_fun/all_to_all | solution.py:473

commit v7 on v6

--- a/solution.py
+++ b/solution.py
@@ -136,19 +136,9 @@
     row_terms(thick, wet, table_ref[0, :rows], levels, term_ref)
 
 
-def pack_kernel(
-    state_ref, thick_ref, wet_ref, below_ref, above_ref, first_ref, last_ref, halo_ref
-):
+def pack_kernel(state_ref, thick_ref, wet_ref, halo_ref, first_ref, last_ref):
     levels, rows, lanes = thick_ref.shape
-    lat_pos = lax.axis_index("lat")
-    with_below = jnp.where(lat_pos > 0, 1.0, 0.0)
-    with_above = jnp.where(lat_pos < lax.axis_size("lat") - 1, 1.0, 0.0)
     lane = lane_of((8, LANES))
-    for f in range(6):
-        for k in range(levels):
-            halo_ref[f, k, 0:2] = above_ref[f, k] * with_above
-            halo_ref[f, k, 2:6] = jnp.zeros((4, lanes), jnp.float32)
-            halo_ref[f, k, 6:8] = below_ref[f, k] * with_below
     for t in range(rows // 8 + 1):
         first = jnp.zeros((8, LANES), jnp.float32)
         last = jnp.zeros((8, LANES), jnp.float32)
@@ -175,18 +165,28 @@
     state_ref,
     thick_ref,
     wet_ref,
-    halo_ref,
+    below_ref,
+    above_ref,
     table_ref,
     own_ref,
     term_ref,
     out_ref,
     edge_ref,
+    halo_ref,
     halo_term_ref,
     north_ref,
 ):
     levels, rows, lanes = thick_ref.shape
     full = rows + 8
     face = table_ref[1]
+    lat_pos = lax.axis_index("lat")
+    with_below = jnp.where(lat_pos > 0, 1.0, 0.0)
+    with_above = jnp.where(lat_pos < lax.axis_size("lat") - 1, 1.0, 0.0)
+    for f in range(6):
+        for k in range(levels):
+            halo_ref[f, k, 0:2] = above_ref[f, k] * with_above
+            halo_ref[f, k, 2:6] = jnp.zeros((4, lanes), jnp.float32)
+            halo_ref[f, k, 6:8] = below_ref[f, k] * with_below
 
     def joined(x, y):
         return jnp.concatenate([x, y], axis=0)
@@ -231,24 +231,9 @@
     lax.fori_loop(0, 2, step, 0)
 
 
-def edge_kernel(
-    inner_ref, own_ref, west_ref, east_ref, table_ref, out_ref, send_ref, tile_ref, term_ref, sems
-):
-    levels, rows, lanes = out_ref.shape[1:]
-    full = rows + 8
-    lane = lane_of((full, LANES))
+def step_tile(tile_ref, h, w, levels, table_ref, term_ref):
     inv_c, face = table_ref[0], table_ref[1]
-    from_west, from_east = west_ref[...], east_ref[...]
-
-    def joined(f):
-        x = own_ref[f]
-        for k in range(levels):
-            src = GROUP * f + 2 * k
-            at = GROUP * k
-            x = jnp.where((lane >= at) & (lane < at + 2), roll(from_west, at - src, 1), x)
-            at = GROUP * k + 12
-            x = jnp.where((lane >= at) & (lane < at + 2), roll(from_east, at - src, 1), x)
-        return x
+    lane = lane_of(h.shape)
 
     def deeper(x):
         return roll(x, -GROUP, 1)
@@ -256,9 +241,6 @@
     def shallower(x):
         return roll(x, GROUP, 1)
 
-    h, w = joined(4), joined(5)
-    for f in range(4):
-        tile_ref[f] = joined(f)
     hs = jnp.where(w > 0, h, 1.0)
     scale = time_step * w / hs
     couple = w * deeper(w) * vertical_mix / (0.5 * (hs + deeper(hs)))
@@ -279,6 +261,29 @@
         return 0
 
     lax.fori_loop(0, 2, step, 0)
+
+
+def edge_kernel(
+    inner_ref, own_ref, west_ref, east_ref, table_ref, out_ref, send_ref, tile_ref, term_ref, sems
+):
+    levels, rows, lanes = out_ref.shape[1:]
+    full = rows + 8
+    lane = lane_of((full, LANES))
+    from_west, from_east = west_ref[...], east_ref[...]
+
+    def joined(f):
+        x = own_ref[f]
+        for k in range(levels):
+            src = GROUP * f + 2 * k
+            at = GROUP * k
+            x = jnp.where((lane >= at) & (lane < at + 2), roll(from_west, at - src, 1), x)
+            at = GROUP * k + 12
+            x = jnp.where((lane >= at) & (lane < at + 2), roll(from_east, at - src, 1), x)
+        return x
+
+    for f in range(4):
+        tile_ref[f] = joined(f)
+    step_tile(tile_ref, joined(4), joined(5), levels, table_ref, term_ref)
     lane = lane_of((rows, LANES))
     for f in range(4):
         x = tile_ref[f, :rows]
@@ -302,6 +307,170 @@
 
 def product(a, b, dims):
     return lax.dot_general(a, b, (dims, ((), ())), preferred_element_type=jnp.float32)
+
+
+def within(lane, low, high):
+    c = lane % GROUP
+    return (c >= low) & (c < high)
+
+
+def pairs_of_rows(tiles, t, place):
+    sub = lax.broadcasted_iota(jnp.int32, tiles[0].shape, 0) // 2
+    for y in range(4):
+        made = roll(tiles[0], -2 * y, 0)
+        for x in range(1, 4):
+            made = jnp.where(sub == x, roll(tiles[x], 2 * (x - y), 0), made)
+        place(y, made)
+
+
+def send_kernel(inner_ref, own_ref, out_ref, piece_ref, raw_ref, sems):
+    levels, full = inner_ref.shape[2:4]
+    rows = full - 8
+    peers = out_ref.shape[0]
+    main = 8 * levels
+    c = lane_of((full, LANES)) % GROUP
+    for i in range(3):
+        a, b = own_ref[2 * i], own_ref[2 * i + 1]
+        one = jnp.where(c < 4, roll(a, -2, 1), roll(a, -4, 1))
+        two = jnp.where(c < 12, roll(b, 6, 1), roll(b, 4, 1))
+        both = jnp.where(c < 8, one, two)
+        raw_ref[i, 0:2] = both[full - 2 : full]
+        raw_ref[i, 2 : rows + 4] = both[: rows + 2]
+        raw_ref[i, rows + 4 : full] = jnp.zeros((4, LANES), jnp.float32)
+    copies = []
+    for t in range(rows // 8):
+        for k in range(levels):
+            tiles = [inner_ref[2, f, k, 8 * t : 8 * t + 8] for f in range(4)]
+
+            def place(y, tile, t=t, k=k):
+                piece_ref[4 * t + y, 8 * k : 8 * k + 8] = tile
+
+            pairs_of_rows(tiles, t, place)
+        for p in range(4 * t, 4 * t + 4):
+            for i in range(3):
+                piece_ref[p, main + 8 * i : main + 8 * i + 8] = raw_ref[i, 2 * p : 2 * p + 8]
+        part = pl.ds(4 * t, 4)
+        copies.append(pltpu.make_async_copy(piece_ref.at[part], out_ref.at[part], sems.at[t]))
+        copies[-1].start()
+    assert 4 * (rows // 8) == peers
+    for copy in copies:
+        copy.wait()
+
+
+def circle_kernel(
+    circle_ref,
+    table_ref,
+    basis_ref,
+    joint_basis_ref,
+    weight_ref,
+    out_ref,
+    tile_ref,
+    term_ref,
+    joint_ref,
+    piece_ref,
+    sems,
+):
+    peers = circle_ref.shape[0]
+    main, modes = weight_ref.shape
+    levels = main // 8
+    lanes = LANES
+    lane = lane_of((8, LANES))
+    left, right = within(lane, 4, 8), within(lane, 8, 12)
+    for o in range(peers):
+        after = (o + 1) % peers
+        for i in range(3):
+            at = pl.ds(main + 8 * i, 8)
+            x, y = circle_ref[o, at], circle_ref[after, at]
+            one = jnp.where(left, x, jnp.where(right, roll(y, 8, 1), 0.0))
+            two = jnp.where(left, roll(x, -8, 1), jnp.where(right, y, 0.0))
+            tile_ref[2 * i, 8 * o : 8 * o + 8] = one
+            tile_ref[2 * i + 1, 8 * o : 8 * o + 8] = two
+    step_tile(tile_ref, tile_ref[4], tile_ref[5], levels, table_ref, term_ref)
+    sub = lax.broadcasted_iota(jnp.int32, (8, LANES), 0) // 2
+    for o in range(peers):
+        made = jnp.zeros((8, LANES), jnp.float32)
+        for f in range(4):
+            x = tile_ref[f, 8 * o : 8 * o + 8]
+            made = jnp.where(sub == f, roll(x, 2 * f - 2, 0), made)
+        joint_ref[8 * o : 8 * o + 8] = jnp.where(within(lane, 6, 10), made, 0.0)
+    lane_main = lane_of((main, LANES))
+    inside = (lane_main >= 2) & (lane_main < lanes - 2)
+    level = lax.broadcasted_iota(jnp.int32, (main, LANES), 0) // 8
+    at_level = lane_main // GROUP == level
+
+    def block(o):
+        return jnp.where(inside, circle_ref[o, :main], 0.0)
+
+    def joint(o):
+        x = joint_ref[8 * o : 8 * o + 8]
+        return jnp.where(at_level, jnp.concatenate([x] * levels, axis=0), 0.0)
+
+    total = jnp.zeros((2 * main, 2 * modes), jnp.float32)
+    for o in range(0, peers, 2):
+        span = slice(lanes * o, lanes * (o + 2))
+        for source, basis in ((block, basis_ref), (joint, joint_basis_ref)):
+            parts = zip(split(source(o)), split(source(o + 1)))
+            x = jnp.concatenate([jnp.concatenate(p, axis=1) for p in parts], axis=0)
+            total = total + product(x, basis[span], ((1,), (0,)))
+    total = total[:main] + total[main:]
+    total = (total[:, :modes] + total[:, modes:]) * weight_ref[...]
+    y = jnp.concatenate([jnp.concatenate([p, p], axis=1) for p in split(total)], axis=0)
+    copies = []
+    for o in range(0, peers, 2):
+        x = product(y, basis_ref[lanes * o : lanes * (o + 2)], ((1,), (1,)))
+        x = x[:main] + x[main:]
+        for i in range(2):
+            before = (o + i - 1) % peers
+            piece_ref[o + i, :main] = x[:, lanes * i : lanes * (i + 1)]
+            piece_ref[o + i, main:] = jnp.where(
+                lane % GROUP < 8,
+                joint_ref[8 * (o + i) : 8 * (o + i) + 8],
+                joint_ref[8 * before : 8 * before + 8],
+            )
+        both = pl.ds(o, 2)
+        copies.append(
+            pltpu.make_async_copy(piece_ref.at[both], out_ref.at[both], sems.at[o // 2])
+        )
+        copies[-1].start()
+    for copy in copies:
+        copy.wait()
+
+
+def join_kernel(inner_ref, piece_ref, wet_ref, flag_ref, out_ref, made_ref, sems):
+    levels, rows, lanes = wet_ref.shape
+    main = 8 * levels
+    lane = lane_of((8, LANES))
+
+    def edges_of(t, into):
+        tiles = [piece_ref[4 * t + x, main : main + 8] for x in range(4)]
+        pairs_of_rows(tiles, t, into)
+
+    for t in range(rows // 8):
+        part = slice(8 * t, 8 * t + 8)
+        flag = flag_ref[part]
+        edges = {}
+        edges_of(t, edges.__setitem__)
+        for k in range(levels):
+            tiles = [piece_ref[4 * t + x, 8 * k : 8 * k + 8] for x in range(4)]
+            gate = flag * wet_ref[k, part]
+
+            def place(f, smooth, k=k, gate=gate, part=part, edges=edges):
+                first = roll(edges[f], -(GROUP * k + 8), 1)
+                last = roll(edges[f], lanes - 2 - (GROUP * k + 6), 1)
+                state = jnp.where(
+                    lane < 2,
+                    first,
+                    jnp.where(lane >= lanes - 2, last, inner_ref[2, f, k, part]),
+                )
+                made_ref[f, k, part] = state + gate * (smooth - state)
+
+            pairs_of_rows(tiles, t, place)
+    copies = []
+    for f in range(4):
+        copies.append(pltpu.make_async_copy(made_ref.at[f], out_ref.at[f], sems.at[f]))
+        copies[-1].start()
+    for copy in copies:
+        copy.wait()
 
 
 def filter_kernel(circle_ref, basis_ref, weight_ref, out_ref, piece_ref, sems):
@@ -391,6 +560,14 @@
     return np.concatenate([high, low], axis=1)
 
 
+def joint_basis(basis, lanes):
+    length = basis.shape[0]
+    joint, lane = np.divmod(np.arange(length), lanes)
+    c = lane % GROUP
+    column = (lanes * (joint + 1) + c - 8) % length
+    return np.where(((c >= 6) & (c < 10))[:, None], basis[column], np.zeros_like(basis))
+
+
 def mode_weights(counts, modes, length):
     order = jnp.arange(modes).astype(jnp.float32)
     keep = (order[None, :] < counts[:, None]).astype(jnp.float32)
@@ -399,14 +576,17 @@
     return jnp.concatenate([weights, weights], axis=1)
 
 
-def row_table(lat_pos, rows, nlat):
-    place = np.arange(rows + 8)
-    place = np.where(place < rows + 2, place, np.where(place < rows + 6, 0, place - rows - 8))
-    place = (lat_pos * rows + jnp.asarray(place, jnp.int32)).astype(jnp.float32)
+def row_table(place, nlat):
+    place = place.astype(jnp.float32)
     centre = jnp.cos(lat_edge * (2.0 * (place + 0.5) / nlat - 1.0))
     faces = jnp.cos(lat_edge * (2.0 * (place + 1.0) / nlat - 1.0))
     table = jnp.stack([1.0 / centre, faces])
     return jnp.broadcast_to(table[:, :, None], table.shape + (LANES,))
+
+
+def ring_rows(rows):
+    place = np.arange(rows + 8)
+    return np.where(place < rows + 2, place, np.where(place < rows + 6, 0, place - rows - 8))
 
 
 def shards(ocean_state, thickness, wet_mask, mode_counts, row_flags):
@@ -420,7 +600,8 @@
     total = 4 * levels * rows
     part = total // lon_peers
     lat_pos = lax.axis_index("lat")
-    table = row_table(lat_pos, rows, nlat)
+    first_row = lat_pos * rows
+    table = row_table(first_row + jnp.asarray(ring_rows(rows), jnp.int32), nlat)
     cells = 4 * levels * full * lanes
     edge_rows = (6, levels, 2, lanes)
 
@@ -436,49 +617,86 @@
         ready_kernel, [(6, rows, LANES), (5, levels, rows, lanes)], flops=20 * cells
     )(*block, table)
     below, above, own, terms = lax.optimization_barrier((below, above, own, terms))
-    first, last, halo = call(
-        pack_kernel, [(full, LANES)] * 2 + [(6, levels, 8, lanes)]
-    )(*block, below, above)
-    from_west, from_east = swap_edges(last, first, "lon")
-    inner, edges = call(
+    inner, edges, halo = call(
         inner_kernel,
-        [(3, 4, levels, full, lanes), (6, full, LANES)],
+        [(3, 4, levels, full, lanes), (6, full, LANES), (6, levels, 8, lanes)],
         [(5, levels, 8, lanes), (2, levels, full, lanes)],
         flops=60 * cells,
-    )(*block, halo, table, own, terms)
-    state, sent = call(
-        edge_kernel,
-        [ocean_state.shape] * 2,
-        [(4, full, LANES), (7, full, LANES)],
-        sems=4,
-        sent=True,
-    )(inner, edges, from_west, from_east, table)
-
-    basis = lax.optimization_barrier(jnp.asarray(mode_basis(nlon, MAXM)))
-
-    def filtered(state, sent, wet):
-        counts = mode_counts.astype(jnp.float32)
+    )(*block, below, above, table, own, terms)
+
+    def exchanged():
+        first, last = call(pack_kernel, [(full, LANES)] * 2)(*block, halo)
+        from_west, from_east = swap_edges(last, first, "lon")
+        return call(
+            edge_kernel,
+            [ocean_state.shape] * 2,
+            [(4, full, LANES), (7, full, LANES)],
+            sems=4,
+            sent=True,
+        )(inner, edges, from_west, from_east, table)
+
+    banded = (first_row < FBAND) | (first_row + rows > nlat - FBAND)
+    flags = jnp.broadcast_to(row_flags.astype(jnp.float32)[:, None], (rows, lanes))
+    counts = mode_counts.astype(jnp.float32)
+    modes = mode_basis(nlon, MAXM)
+    basis, at_joints = lax.optimization_barrier(
+        (jnp.asarray(modes), jnp.asarray(joint_basis(modes, lanes)))
+    )
+    lon_pos = lax.axis_index("lon")
+
+    def circled():
+        main = 8 * levels
+        sent = call(
+            send_kernel,
+            [(lon_peers, main + 24, lanes)],
+            [(lon_peers, main + 24, lanes), (3, full, lanes)],
+            sems=rows // 8,
+            sent=True,
+        )(inner, edges)[0]
+        circles = lax.all_to_all(sent, "lon", 0, 0, tiled=True)
+        place = first_row + 2 * lon_pos - 2 + jnp.minimum(jnp.arange(8, dtype=jnp.int32), 5)
+        joint_table = jnp.tile(row_table(place, nlat), (1, lon_peers, 1))
+        row_counts = jnp.tile(lax.dynamic_slice(counts, (2 * lon_pos,), (2,)), 4 * levels)
+        pieces = call(
+            circle_kernel,
+            [(lon_peers, main + 8, lanes)],
+            [
+                (6, 8 * lon_peers, lanes),
+                (7, 8 * lon_peers, lanes),
+                (8 * lon_peers, lanes),
+                (lon_peers, main + 8, lanes),
+            ],
+            sems=lon_peers // 2,
+            sent=True,
+        )(circles, joint_table, basis, at_joints, mode_weights(row_counts, MAXM, nlon))[0]
+        pieces = lax.all_to_all(pieces, "lon", 0, 0, tiled=True)
+        return call(join_kernel, [ocean_state.shape], [ocean_state.shape], sems=4, sent=True)(
+            inner, pieces, block[2], flags
+        )[0]
+
+    if rows == 2 * lon_peers:
+        return lax.cond(banded, circled, lambda: exchanged()[1])
+
+    state, sent = exchanged()
+
+    def filtered():
         row_counts = lax.dynamic_slice(
             jnp.broadcast_to(counts[None], (4 * levels, rows)).reshape(total),
-            (lax.axis_index("lon") * part,),
+            (lon_pos * part,),
             (part,),
         )
-        weights = mode_weights(row_counts, MAXM, nlon)
         circles = lax.all_to_all(
             sent.reshape(lon_peers, part, lanes), "lon", 0, 0, tiled=True
         )
         smooth = call(
             filter_kernel, [circles.shape], [circles.shape], sems=lon_peers // 2, sent=True
-        )(circles, basis, weights)[0]
+        )(circles, basis, mode_weights(row_counts, MAXM, nlon))[0]
         smooth = lax.all_to_all(smooth, "lon", 0, 0, tiled=True).reshape(state.shape)
-        flags = jnp.broadcast_to(row_flags.astype(jnp.float32)[:, None], (rows, lanes))
         return call(blend_kernel, [state.shape], [state.shape], sems=4, sent=True)(
-            state, smooth, wet, flags
+            state, smooth, block[2], flags
         )[0]
 
-    first_row = lat_pos * rows
-    banded = (first_row < FBAND) | (first_row + rows > nlat - FBAND)
-    return lax.cond(banded, filtered, lambda state, sent, wet: sent, state, sent, block[2])
+    return lax.cond(banded, filtered, lambda: sent)
 
 
 def solution(mesh):

time: 42.8 us -> 40.2 us (0.939)
  blocking collectives: 0 us -> 11.8 us
  waiting for transfers between devices: 17 us -> 8.42 us
  starting transfers between devices: 17 us -> 9.09 us
  other arithmetic: 0.89 us -> 2.27 us
  local copies, waits for them, and re-layouts: 0.32 us -> 1.18 us
    all_to_all x0 -> x1, blocking collectives: none -> 11.8 us  [circled(): pieces = lax.all_to_all(pieces, 'lon', 0, 0, tiled=True)]
    all_to_all x2 -> x1, waiting for transfers between devices: 16 us -> 8.41 us  [circled(): circles = lax.all_to_all(sent, 'lon', 0, 0, tiled=True)]
    ppermute x2 -> x1, starting transfers between devices: 5.09 us -> 1.99 us  [swap_edges(): lax.ppermute(after_src, axis, down)]
    all_to_all x2 -> x1, starting transfers between devices: 9.36 us -> 6.6 us  [circled(): circles = lax.all_to_all(sent, 'lon', 0, 0, tiled=True)]
    ppermute x2 -> x1, starting transfers between devices: 2.54 us -> 0.5 us  [swap_edges(): lax.ppermute(before_src, axis, up)]
    convert_element_type x2, other arithmetic: 0.01 us -> 1.32 us  [the longest x1 0.66 us: shards(): counts = mode_counts.astype(jnp.float32)]
    unnamed x6, local copies, waits for them, and re-layouts: 0.02 us -> 0.7 us
    ppermute x2 -> x1, waiting for transfers between devices: 0.6 us -> 0.01 us  [swap_edges(): lax.ppermute(before_src, axis, up)]
  transfers between devices with their start and end apart: 6 -> 3, of which waited for: 4 -> 1; matrix products, arithmetic and copies ran while one was open for 3% -> 7% of each run, Pallas kernels for 5% -> 1%
where the time goes in v7:
time: 40.2 us; the launch traced here: 39.9 us
  blocking collectives  11.8 us (29%)
  starting transfers between devices  9.09 us (23%)
  waiting for transfers between devices  8.42 us (21%)
  Pallas kernels  6.93 us (17%)
  other arithmetic  2.27 us (6%)
  local copies, waits for them, and re-layouts  1.18 us (3%)
    all_to_all x1, blocking collectives, circled(): pieces = lax.all_to_all(pieces, 'lon', 0, 0, tiled=True)  11.8 us
    all_to_all x1, waiting for transfers between devices, circled(): circles = lax.all_to_all(sent, 'lon', 0, 0, tiled=True)  8.41 us
    pallas_call x6, Pallas kernels, run(): pl.pallas_call(kernel, out_shape=[jax.ShapeDtypeStruct(s, jnp.float32) fo...  6.93 us
    all_to_all x1, starting transfers between devices, circled(): circles = lax.all_to_all(sent, 'lon', 0, 0, tiled=True)  6.6 us
    ppermute x1, starting transfers between devices, swap_edges(): lax.ppermute(after_src, axis, down)  1.99 us
  transfers between devices with their start and end apart: 3, of which 1 were waited for; matrix products, arithmetic and copies ran while one was open for 7% of the time, Pallas kernels for 1%

profile of v7, /device:TPU:0, one launch (start us, length us, event | category | flops | bytes accessed | tf_op | source)
XLA Modules:
  0.0 39.9 jit_solution(10202830781862607558)
XLA Ops:
  0.0 1.2 %shard_map.84 = (f32[4,8,16,128]{3,2,1,0:T(8,128)S(1)}, f32[8,16,128]{2,1,0:T(8,128)S(1)}, f32[8,16,128]{2,1,0:T(8,128)S(1)}, f32[6,8,2,128]{3,2,1,0:T(2,128)S(1)}, f32[6,8,2,128]{3,2,1,0:T(2,128)S(1)}) custom-call(f32[4,8,16,128]{3,2,1,0:T(8,128)} %state_any.1, f32[8,16,128]{2,1,0:T(8,128)} %thick_any.1, s32[8,16,128]{2,1,0:T(8,128)} %wet_any.1), custom_call_target="tpu_custom_call" | custom-call | bytes 491520 | tf_op jit(solution)/shard_map/pallas_call | solution.py:534
  1.2 0.5 %collective-permute-start.2 = (f32[6,8,2,128]{3,2,1,0:T(2,128)S(1)}, f32[6,8,2,128]{3,2,1,0:T(2,128)S(1)}, u32[]{:S(2)}, u32[]{:S(2)}) collective-permute-start(f32[6,8,2,128]{3,2,1,0:T(2,128)S(1)} %get-tuple-element.79), channel_id=1, source_target_pairs={{0,1},{1,2},{2,3},{3,0},{4,5},{5,6},{6,7},{7,4},{8,9},{9,10},{10,1... | collective-permute-start | bytes 147464 | tf_op jit(solution)/shard_map/ppermute | solution.py:551
  1.7 2.0 %collective-permute-start.3 = (f32[6,8,2,128]{3,2,1,0:T(2,128)S(1)}, f32[6,8,2,128]{3,2,1,0:T(2,128)S(1)}, u32[]{:S(2)}, u32[]{:S(2)}) collective-permute-start(f32[6,8,2,128]{3,2,1,0:T(2,128)S(1)} %get-tuple-element.80), channel_id=1, source_target_pairs={{1,0},{2,1},{3,2},{0,3},{5,4},{6,5},{7,6},{4,7},{9,8},{10,9},{11,1... | collective-permute-start | bytes 147464 | tf_op jit(solution)/shard_map/ppermute | solution.py:551
  3.7 0.7 %divide_bitcast_fusion = (f32[1,24]{1,0:T(1,128)S(1)}, f32[1,24]{1,0:T(1,128)S(1)}) fusion(s32[24]{0:T(128)} %constant.70.clone, s32[]{:T(128)} %mul.47), kind=kLoop, calls=%fused_computation.11 | loop fusion | flops 264 | bytes 292 | tf_op jit(solution)/shard_map/stack | solution.py:583
  4.4 0.7 %convert_element_type.41 = f32[16]{0:T(128)S(1)} convert(s32[16]{0:T(128)} %param.13) | non-fusion elementwise | flops 16 | bytes 128 | tf_op jit(solution)/shard_map/convert_element_type | solution.py:640
  5.1 0.7 %convert_element_type.42 = f32[16]{0:T(128)S(1)} convert(s32[16]{0:T(128)} %param.14) | non-fusion elementwise | flops 16 | bytes 128 | tf_op jit(solution)/shard_map/convert_element_type | solution.py:639
  5.7 0.1 broadcast_in_dim.11.table_ref
  5.8 0.3 shard_map.85
  6.1 1.7 %shard_map.86 = (f32[3,4,8,24,128]{4,3,2,1,0:T(8,128)S(1)}, f32[6,24,128]{2,1,0:T(8,128)S(1)}, f32[6,8,8,128]{3,2,1,0:T(8,128)S(1)}) custom-call(f32[4,8,16,128]{3,2,1,0:T(8,128)S(1)} %get-tuple-element.76.state_ref, f32[8,16,128]{2,1,0:T(8,128)S(1)} %get-tuple-element.77.thick_ref, f32[8,16,128]{2,1,0:T(8,128)S(1)} %get-tuple-element.78.wet_ref, ...), custom_call_target="tpu_custom_call" | custom-call | flops 5898240 | bytes 1449984 | tf_op jit(solution)/shard_map/pallas_call | solution.py:534
  7.9 31.2 %conditional.1 = (f32[4,8,16,128]{3,2,1,0:T(8,128)S(1)}) conditional(s32[]{:T(128)} %convert_element_type.39, (f32[4,8,16,128]{3,2,1,0:T(8,128)S(1)}, f32[8,16,128]{2,1,0:T(8,128)S(1)}, f32[8,16,128]{2,1,0:T(8,128)S(1)}, f32[6,8,8,128]{3,2,1,0:T(8,128)S(1)}, f32[3,4,8,24,128]{4,3,2,1,0:T(8,128)S(1)}, /*index=5*/f32[6,24,128]{2,1,0:T(8,128)S(1)}, ...), branch_computations={%region_0.0_spmd, %region_1.2_spmd} | conditional | flops 16822 | bytes 2732494 | solution.py:678
  7.9 0.9 %branch_1_fun.3 = f32[8,88,128]{2,1,0:T(8,128)} custom-call(f32[3,4,8,24,128]{4,3,2,1,0:T(8,128)S(1)} %get-tuple-element.51.inner_ref, f32[6,24,128]{2,1,0:T(8,128)S(1)} %get-tuple-element.52.own_ref), custom_call_target="tpu_custom_call" | custom-call | bytes 360448 | tf_op jit(solution)/shard_map/cond/branch_1_fun/pallas_call | solution.py:534
  8.8 6.6 %all-to-all-start = ((f32[8,88,128]{2,1,0:T(8,128)}), f32[8,88,128]{2,1,0:T(8,128)S(1)}, u32[]{:S(2)}, u32[]{:S(2)}) async-start(f32[8,88,128]{2,1,0:T(8,128)} %branch_1_fun.3), calls=%async_computation | async-start | bytes 720896 | tf_op jit(solution)/shard_map/cond/branch_1_fun/all_to_all | solution.py:656
  15.5 0.1 tile.1
  15.6 0.1 dynamic_slice.2
  15.7 0.1 lt.5
  15.8 0.1 compare_select_fusion
  15.9 0.1 pad_maximum_fusion.weight_ref
  16.0 8.4 %all-to-all-done.circle_ref = f32[8,88,128]{2,1,0:T(8,128)S(1)} async-done(((f32[8,88,128]{2,1,0:T(8,128)}), f32[8,88,128]{2,1,0:T(8,128)S(1)}, u32[]{:S(2)}, u32[]{:S(2)}) %all-to-all-start) | async-done | bytes 360480 | tf_op jit(solution)/shard_map/cond/branch_1_fun/all_to_all | solution.py:656
  24.4 0.1 tile.2.table_ref
  24.4 2.3 %branch_1_fun.4 = f32[8,72,128]{2,1,0:T(8,128)S(1)} custom-call(f32[8,88,128]{2,1,0:T(8,128)S(1)} %all-to-all-done.circle_ref, f32[2,64,128]{2,1,0:T(8,128)S(1)} %tile.2.table_ref, bf16[1024,256]{1,0:T(8,128)(2,1)S(1)} %get-tuple-element.55.basis_ref, bf16[1024,256]{1,0:T(8,128)(2,1)S(1)} %get-tuple-element.56.joint_basis_ref, ...), custom_call_target="tpu_custom_call" | custom-call | bytes 294912 | tf_op jit(solution)/shard_map/cond/branch_1_fun/pallas_call | solution.py:534
  26.8 11.8 %all_to_all.8.piece_ref = f32[8,72,128]{2,1,0:T(8,128)S(1)} all-to-all(f32[8,72,128]{2,1,0:T(8,128)S(1)} %branch_1_fun.4), channel_id=1, replica_groups=mesh['lon'=8,'lat'=4] {'lon'}, dimensions={0} | all-to-all | bytes 589824 | tf_op jit(solution)/shard_map/cond/branch_1_fun/all_to_all | solution.py:672
  38.6 0.1 broadcast_in_dim.9.flag_ref
  38.6 0.5 %branch_1_fun.5 = f32[4,8,16,128]{3,2,1,0:T(8,128)S(1)} custom-call(f32[3,4,8,24,128]{4,3,2,1,0:T(8,128)S(1)} %get-tuple-element.51.inner_ref, f32[8,72,128]{2,1,0:T(8,128)S(1)} %all_to_all.8.piece_ref, f32[8,16,128]{2,1,0:T(8,128)S(1)} %get-tuple-element.58.wet_ref, f32[16,128]{1,0:T(8,128)S(1)} %broadcast_in_dim.9.flag_ref), custom_call_target="tpu_custom_call" | custom-call | bytes 262144 | tf_op jit(solution)/shard_map/cond/branch_1_fun/pallas_call | solution.py:534
  39.2 0.7 %copy-done.2 = f32[4,8,16,128]{3,2,1,0:T(8,128)} copy-done((f32[4,8,16,128]{3,2,1,0:T(8,128)}, f32[4,8,16,128]{3,2,1,0:T(8,128)S(1)}, u32[]{:S(2)}) %copy-start.2) | copy-done | bytes 262168
  (14 shorter events, 0.1 us)
Async XLA Ops:
  0.0 7.9 %copy-start = (bf16[1024,256]{1,0:T(8,128)(2,1)S(1)}, bf16[1024,256]{1,0:T(8,128)(2,1)}, u32[]{:S(2)}) copy-start(bf16[1024,256]{1,0:T(8,128)(2,1)} %constant.71.clone) | copy-start | bytes 1572868
  0.0 7.9 %copy-start.1 = (bf16[1024,256]{1,0:T(8,128)(2,1)S(1)}, bf16[1024,256]{1,0:T(8,128)(2,1)}, u32[]{:S(2)}) copy-start(bf16[1024,256]{1,0:T(8,128)(2,1)} %constant.72.clone) | copy-start | bytes 1572868
  1.2 4.9 %collective-permute-start.2 = (f32[6,8,2,128]{3,2,1,0:T(2,128)S(1)}, f32[6,8,2,128]{3,2,1,0:T(2,128)S(1)}, u32[]{:S(2)}, u32[]{:S(2)}) collective-permute-start(f32[6,8,2,128]{3,2,1,0:T(2,128)S(1)} %get-tuple-element.79), channel_id=1, source_target_pairs={{0,1},{1,2},{2,3},{3,0},{4,5},{5,6},{6,7},{7,4},{8,9},{9,10},{10,1... | collective-permute-start | bytes 147464 | tf_op jit(solution)/shard_map/ppermute | solution.py:551
  1.7 4.4 %collective-permute-start.3 = (f32[6,8,2,128]{3,2,1,0:T(2,128)S(1)}, f32[6,8,2,128]{3,2,1,0:T(2,128)S(1)}, u32[]{:S(2)}, u32[]{:S(2)}) collective-permute-start(f32[6,8,2,128]{3,2,1,0:T(2,128)S(1)} %get-tuple-element.80), channel_id=1, source_target_pairs={{1,0},{2,1},{3,2},{0,3},{5,4},{6,5},{7,6},{4,7},{9,8},{10,9},{11,1... | collective-permute-start | bytes 147464 | tf_op jit(solution)/shard_map/ppermute | solution.py:551
  8.8 15.5 %all-to-all-start = ((f32[8,88,128]{2,1,0:T(8,128)}), f32[8,88,128]{2,1,0:T(8,128)S(1)}, u32[]{:S(2)}, u32[]{:S(2)}) async-start(f32[8,88,128]{2,1,0:T(8,128)} %branch_1_fun.3), calls=%async_computation | async-start | bytes 720896 | tf_op jit(solution)/shard_map/cond/branch_1_fun/all_to_all | solution.py:656
  39.2 0.7 %copy-start.2 = (f32[4,8,16,128]{3,2,1,0:T(8,128)}, f32[4,8,16,128]{3,2,1,0:T(8,128)S(1)}, u32[]{:S(2)}) copy-start(f32[4,8,16,128]{3,2,1,0:T(8,128)S(1)} %get-tuple-element.108) | copy-start | bytes 786436

commit v8 on v7

--- a/solution.py
+++ b/solution.py
@@ -100,18 +100,41 @@
 
 
 def load_kernel(
-    state_any, thick_any, wet_any, state_ref, thick_ref, wet_ref, first_ref, last_ref, raw_ref, sems
+    state_any,
+    thick_any,
+    wet_any,
+    flag_any,
+    count_any,
+    state_ref,
+    thick_ref,
+    wet_ref,
+    first_ref,
+    last_ref,
+    flag_ref,
+    count_ref,
+    raw_ref,
+    raw_flag_ref,
+    raw_count_ref,
+    sems,
 ):
     levels, rows = thick_ref.shape[:2]
-    moves = [(wet_any, raw_ref), (thick_any, thick_ref)]
+    moves = [(flag_any, raw_flag_ref), (count_any, raw_count_ref), (wet_any, raw_ref)]
+    moves += [(thick_any, thick_ref)]
     moves += [(state_any.at[f], state_ref.at[f]) for f in range(4)]
     copies = [pltpu.make_async_copy(*pair, sems.at[i]) for i, pair in enumerate(moves)]
     for copy in copies:
         copy.start()
-    copies[0].wait()
+    for copy in copies[:3]:
+        copy.wait()
+    shape = (rows, rows)
+    diagonal = lax.broadcasted_iota(jnp.int32, shape, 0) == lane_of(shape)
+    for raw, ref in ((raw_flag_ref, flag_ref), (raw_count_ref, count_ref)):
+        spread = jnp.broadcast_to(raw[...].astype(jnp.float32), shape)
+        value = jnp.sum(jnp.where(diagonal, spread, 0.0), axis=1, keepdims=True)
+        ref[...] = jnp.broadcast_to(value, (rows, LANES))
     for k in range(levels):
         wet_ref[k] = raw_ref[k].astype(jnp.float32)
-    for copy in copies[1:]:
+    for copy in copies[3:]:
         copy.wait()
     for f in range(6):
         for k in range(levels):
@@ -309,11 +332,6 @@
     return lax.dot_general(a, b, (dims, ((), ())), preferred_element_type=jnp.float32)
 
 
-def within(lane, low, high):
-    c = lane % GROUP
-    return (c >= low) & (c < high)
-
-
 def pairs_of_rows(tiles, t, place):
     sub = lax.broadcasted_iota(jnp.int32, tiles[0].shape, 0) // 2
     for y in range(4):
@@ -323,10 +341,9 @@
         place(y, made)
 
 
-def send_kernel(inner_ref, own_ref, out_ref, piece_ref, raw_ref, sems):
+def send_kernel(inner_ref, own_ref, out_ref, raw_ref):
     levels, full = inner_ref.shape[2:4]
     rows = full - 8
-    peers = out_ref.shape[0]
     main = 8 * levels
     c = lane_of((full, LANES)) % GROUP
     for i in range(3):
@@ -337,24 +354,17 @@
         raw_ref[i, 0:2] = both[full - 2 : full]
         raw_ref[i, 2 : rows + 4] = both[: rows + 2]
         raw_ref[i, rows + 4 : full] = jnp.zeros((4, LANES), jnp.float32)
-    copies = []
     for t in range(rows // 8):
         for k in range(levels):
             tiles = [inner_ref[2, f, k, 8 * t : 8 * t + 8] for f in range(4)]
 
             def place(y, tile, t=t, k=k):
-                piece_ref[4 * t + y, 8 * k : 8 * k + 8] = tile
+                out_ref[4 * t + y, 8 * k : 8 * k + 8] = tile
 
             pairs_of_rows(tiles, t, place)
         for p in range(4 * t, 4 * t + 4):
             for i in range(3):
-                piece_ref[p, main + 8 * i : main + 8 * i + 8] = raw_ref[i, 2 * p : 2 * p + 8]
-        part = pl.ds(4 * t, 4)
-        copies.append(pltpu.make_async_copy(piece_ref.at[part], out_ref.at[part], sems.at[t]))
-        copies[-1].start()
-    assert 4 * (rows // 8) == peers
-    for copy in copies:
-        copy.wait()
+                out_ref[p, main + 8 * i : main + 8 * i + 8] = raw_ref[i, 2 * p : 2 * p + 8]
 
 
 def circle_kernel(
@@ -362,78 +372,82 @@
     table_ref,
     basis_ref,
     joint_basis_ref,
-    weight_ref,
+    count_ref,
     out_ref,
     tile_ref,
     term_ref,
     joint_ref,
-    piece_ref,
-    sems,
 ):
     peers = circle_ref.shape[0]
-    main, modes = weight_ref.shape
+    modes = basis_ref.shape[1] // 2
+    length = basis_ref.shape[0]
+    main = circle_ref.shape[1] - 24
     levels = main // 8
     lanes = LANES
     lane = lane_of((8, LANES))
-    left, right = within(lane, 4, 8), within(lane, 8, 12)
-    for o in range(peers):
-        after = (o + 1) % peers
+    c = lane % GROUP
+    for j in range(0, peers, 2):
+        part = slice(4 * j, 4 * j + 8)
         for i in range(3):
-            at = pl.ds(main + 8 * i, 8)
-            x, y = circle_ref[o, at], circle_ref[after, at]
-            one = jnp.where(left, x, jnp.where(right, roll(y, 8, 1), 0.0))
-            two = jnp.where(left, roll(x, -8, 1), jnp.where(right, y, 0.0))
-            tile_ref[2 * i, 8 * o : 8 * o + 8] = one
-            tile_ref[2 * i + 1, 8 * o : 8 * o + 8] = two
+            x, y, z = (
+                circle_ref[(j + d) % peers, main + 8 * i : main + 8 * i + 8] for d in range(3)
+            )
+            for f, shift in ((2 * i, 0), (2 * i + 1, -8)):
+                middle = jnp.where(c < 12, roll(y, 4 + shift, 1), roll(z, 12 + shift, 1))
+                tile_ref[f, part] = jnp.where(c < 4, roll(x, shift - 4, 1), middle)
     step_tile(tile_ref, tile_ref[4], tile_ref[5], levels, table_ref, term_ref)
     sub = lax.broadcasted_iota(jnp.int32, (8, LANES), 0) // 2
-    for o in range(peers):
+    right = (c % 8 >= 2) & (c % 8 < 6)
+    for j in range(peers // 2):
         made = jnp.zeros((8, LANES), jnp.float32)
         for f in range(4):
-            x = tile_ref[f, 8 * o : 8 * o + 8]
+            x = tile_ref[f, 8 * j : 8 * j + 8]
             made = jnp.where(sub == f, roll(x, 2 * f - 2, 0), made)
-        joint_ref[8 * o : 8 * o + 8] = jnp.where(within(lane, 6, 10), made, 0.0)
+        joint_ref[8 * j : 8 * j + 8] = jnp.where(right, made, 0.0)
     lane_main = lane_of((main, LANES))
+    row_main = lax.broadcasted_iota(jnp.int32, (main, LANES), 0)
     inside = (lane_main >= 2) & (lane_main < lanes - 2)
-    level = lax.broadcasted_iota(jnp.int32, (main, LANES), 0) // 8
-    at_level = lane_main // GROUP == level
+    at_level = lane_main // GROUP == row_main // 8
 
     def block(o):
         return jnp.where(inside, circle_ref[o, :main], 0.0)
 
-    def joint(o):
-        x = joint_ref[8 * o : 8 * o + 8]
+    def joint(j):
+        x = joint_ref[8 * j : 8 * j + 8]
         return jnp.where(at_level, jnp.concatenate([x] * levels, axis=0), 0.0)
 
     total = jnp.zeros((2 * main, 2 * modes), jnp.float32)
-    for o in range(0, peers, 2):
-        span = slice(lanes * o, lanes * (o + 2))
-        for source, basis in ((block, basis_ref), (joint, joint_basis_ref)):
+    for source, basis, count in (
+        (block, basis_ref, peers),
+        (joint, joint_basis_ref, peers // 2),
+    ):
+        for o in range(0, count, 2):
             parts = zip(split(source(o)), split(source(o + 1)))
             x = jnp.concatenate([jnp.concatenate(p, axis=1) for p in parts], axis=0)
-            total = total + product(x, basis[span], ((1,), (0,)))
+            total = total + product(x, basis[lanes * o : lanes * (o + 2)], ((1,), (0,)))
     total = total[:main] + total[main:]
-    total = (total[:, :modes] + total[:, modes:]) * weight_ref[...]
+    counts = count_ref[...]
+    row = lax.broadcasted_iota(jnp.int32, counts.shape, 0)
+    own = 2 * lax.axis_index("lon")
+    even, odd = (
+        jnp.sum(jnp.where(row == own + r, counts, 0.0), axis=0, keepdims=True) for r in (0, 1)
+    )
+    limit = jnp.where(row_main % 2 == 0, even, odd)
+    order = (lane_main % (modes // 2)).astype(jnp.float32)
+    weight = jnp.where(order < limit, jnp.where(order == 0.0, 1.0 / length, 2.0 / length), 0.0)
+    total = (total[:, :modes] + total[:, modes:]) * weight
     y = jnp.concatenate([jnp.concatenate([p, p], axis=1) for p in split(total)], axis=0)
-    copies = []
     for o in range(0, peers, 2):
         x = product(y, basis_ref[lanes * o : lanes * (o + 2)], ((1,), (1,)))
         x = x[:main] + x[main:]
-        for i in range(2):
-            before = (o + i - 1) % peers
-            piece_ref[o + i, :main] = x[:, lanes * i : lanes * (i + 1)]
-            piece_ref[o + i, main:] = jnp.where(
-                lane % GROUP < 8,
-                joint_ref[8 * (o + i) : 8 * (o + i) + 8],
-                joint_ref[8 * before : 8 * before + 8],
-            )
-        both = pl.ds(o, 2)
-        copies.append(
-            pltpu.make_async_copy(piece_ref.at[both], out_ref.at[both], sems.at[o // 2])
+        out_ref[o, :main] = x[:, :lanes]
+        out_ref[o + 1, :main] = x[:, lanes:]
+        before = (4 * o - 8) % (4 * peers)
+        here = joint_ref[4 * o : 4 * o + 8]
+        out_ref[o, main:] = jnp.where(
+            c < 8, roll(joint_ref[before : before + 8], -8, 1), roll(here, 8, 1)
         )
-        copies[-1].start()
-    for copy in copies:
-        copy.wait()
+        out_ref[o + 1, main:] = here
 
 
 def join_kernel(inner_ref, piece_ref, wet_ref, flag_ref, out_ref, made_ref, sems):
@@ -455,8 +469,8 @@
             gate = flag * wet_ref[k, part]
 
             def place(f, smooth, k=k, gate=gate, part=part, edges=edges):
-                first = roll(edges[f], -(GROUP * k + 8), 1)
-                last = roll(edges[f], lanes - 2 - (GROUP * k + 6), 1)
+                first = roll(edges[f], -(GROUP * k + 4), 1)
+                last = roll(edges[f], lanes - 2 - (GROUP * k + 10), 1)
                 state = jnp.where(
                     lane < 2,
                     first,
@@ -519,8 +533,10 @@
     vmem = pl.BlockSpec(memory_space=pltpu.VMEM)
     away = pl.BlockSpec(memory_space=pl.ANY)
     specs = [vmem] * len(outs)
+    shapes = [jax.ShapeDtypeStruct(s, jnp.float32) for s in outs]
     if sent:
         specs[-1] = away
+        shapes[-1] = pltpu.HBM(outs[-1], jnp.float32)
     buffers = [pltpu.VMEM(s, jnp.float32) if isinstance(s, tuple) else s for s in scratch]
     if sems:
         buffers.append(pltpu.SemaphoreType.DMA((sems,)))
@@ -533,7 +549,7 @@
             args = [pltpu.with_memory_space_constraint(x, pltpu.HBM) for x in args]
         return pl.pallas_call(
             kernel,
-            out_shape=[jax.ShapeDtypeStruct(s, jnp.float32) for s in outs],
+            out_shape=shapes,
             in_specs=[away if raw else vmem] * len(args),
             out_specs=specs,
             scratch_shapes=buffers,
@@ -562,10 +578,10 @@
 
 def joint_basis(basis, lanes):
     length = basis.shape[0]
-    joint, lane = np.divmod(np.arange(length), lanes)
-    c = lane % GROUP
-    column = (lanes * (joint + 1) + c - 8) % length
-    return np.where(((c >= 6) & (c < 10))[:, None], basis[column], np.zeros_like(basis))
+    tile, lane = np.divmod(np.arange(length // 2), lanes)
+    half, c = np.divmod(lane % GROUP, 8)
+    column = (lanes * (2 * tile + half + 1) + c - 4) % length
+    return np.where(((c >= 2) & (c < 6))[:, None], basis[column], np.zeros_like(basis[column]))
 
 
 def mode_weights(counts, modes, length):
@@ -585,8 +601,8 @@
 
 
 def ring_rows(rows):
-    place = np.arange(rows + 8)
-    return np.where(place < rows + 2, place, np.where(place < rows + 6, 0, place - rows - 8))
+    place = jnp.arange(rows + 8, dtype=jnp.int32)
+    return jnp.where(place < rows + 2, place, jnp.where(place < rows + 6, 0, place - rows - 8))
 
 
 def shards(ocean_state, thickness, wet_mask, mode_counts, row_flags):
@@ -601,17 +617,18 @@
     part = total // lon_peers
     lat_pos = lax.axis_index("lat")
     first_row = lat_pos * rows
-    table = row_table(first_row + jnp.asarray(ring_rows(rows), jnp.int32), nlat)
+    table = row_table(first_row + ring_rows(rows), nlat)
     cells = 4 * levels * full * lanes
     edge_rows = (6, levels, 2, lanes)
 
-    *block, first, last = call(
+    *block, first, last, flags, counts = call(
         load_kernel,
-        [ocean_state.shape, thickness.shape, thickness.shape, edge_rows, edge_rows],
-        [pltpu.VMEM(thickness.shape, jnp.int32)],
-        sems=6,
+        [ocean_state.shape, thickness.shape, thickness.shape, edge_rows, edge_rows]
+        + [(rows, lanes)] * 2,
+        [pltpu.VMEM(shape, jnp.int32) for shape in (thickness.shape, (1, rows), (1, rows))],
+        sems=8,
         raw=True,
-    )(ocean_state, thickness, wet_mask)
+    )(ocean_state, thickness, wet_mask, row_flags[None], mode_counts[None])
     below, above = swap_edges(last, first, "lat")
     own, terms = call(
         ready_kernel, [(6, rows, LANES), (5, levels, rows, lanes)], flops=20 * cells
@@ -636,39 +653,29 @@
         )(inner, edges, from_west, from_east, table)
 
     banded = (first_row < FBAND) | (first_row + rows > nlat - FBAND)
-    flags = jnp.broadcast_to(row_flags.astype(jnp.float32)[:, None], (rows, lanes))
-    counts = mode_counts.astype(jnp.float32)
     modes = mode_basis(nlon, MAXM)
     basis, at_joints = lax.optimization_barrier(
         (jnp.asarray(modes), jnp.asarray(joint_basis(modes, lanes)))
     )
     lon_pos = lax.axis_index("lon")
+    place = first_row + 2 * lon_pos - 2 + jnp.arange(4 * lon_peers, dtype=jnp.int32) % 8
+    joint_table = row_table(jnp.minimum(place, first_row + 2 * lon_pos + 3), nlat)
 
     def circled():
         main = 8 * levels
         sent = call(
-            send_kernel,
-            [(lon_peers, main + 24, lanes)],
-            [(lon_peers, main + 24, lanes), (3, full, lanes)],
-            sems=rows // 8,
-            sent=True,
+            send_kernel, [(lon_peers, main + 24, lanes)], [(3, full, lanes)]
         )(inner, edges)[0]
         circles = lax.all_to_all(sent, "lon", 0, 0, tiled=True)
-        place = first_row + 2 * lon_pos - 2 + jnp.minimum(jnp.arange(8, dtype=jnp.int32), 5)
-        joint_table = jnp.tile(row_table(place, nlat), (1, lon_peers, 1))
-        row_counts = jnp.tile(lax.dynamic_slice(counts, (2 * lon_pos,), (2,)), 4 * levels)
         pieces = call(
             circle_kernel,
             [(lon_peers, main + 8, lanes)],
             [
-                (6, 8 * lon_peers, lanes),
-                (7, 8 * lon_peers, lanes),
-                (8 * lon_peers, lanes),
-                (lon_peers, main + 8, lanes),
+                (6, 4 * lon_peers, lanes),
+                (7, 4 * lon_peers, lanes),
+                (4 * lon_peers, lanes),
             ],
-            sems=lon_peers // 2,
-            sent=True,
-        )(circles, joint_table, basis, at_joints, mode_weights(row_counts, MAXM, nlon))[0]
+        )(circles, joint_table, basis, at_joints, counts)[0]
         pieces = lax.all_to_all(pieces, "lon", 0, 0, tiled=True)
         return call(join_kernel, [ocean_state.shape], [ocean_state.shape], sems=4, sent=True)(
             inner, pieces, block[2], flags
@@ -681,7 +688,9 @@
 
     def filtered():
         row_counts = lax.dynamic_slice(
-            jnp.broadcast_to(counts[None], (4 * levels, rows)).reshape(total),
+            jnp.broadcast_to(
+                mode_counts.astype(jnp.float32)[None], (4 * levels, rows)
+            ).reshape(total),
             (lon_pos * part,),
             (part,),
         )

time: 40.2 us -> 36.9 us (0.918)
  blocking collectives: 11.8 us -> 26.9 us
  waiting for transfers between devices: 8.42 us -> 1.49 us
  starting transfers between devices: 9.09 us -> 2.49 us
  other arithmetic: 2.27 us -> 0.14 us
  Pallas kernels: 6.93 us -> 5.46 us
  local copies, waits for them, and re-layouts: 1.18 us -> 0.15 us
    all_to_all x0 -> x1, blocking collectives: none -> 15.3 us  [circled(): circles = lax.all_to_all(sent, 'lon', 0, 0, tiled=True)]
    all_to_all x1 -> x0, waiting for transfers between devices: 8.41 us -> none  [circled(): circles = lax.all_to_all(sent, 'lon', 0, 0, tiled=True)]
    all_to_all x1 -> x0, starting transfers between devices: 6.6 us -> none  [circled(): circles = lax.all_to_all(sent, 'lon', 0, 0, tiled=True)]
    pallas_call x6, Pallas kernels: 6.93 us -> 5.46 us  [run(): pl.pallas_call(kernel, out_shape=shapes, in_specs=[away if raw else vmem]...]
    convert_element_type x3 -> x0, other arithmetic: 1.32 us -> none  [the longest x1 0.66 us: shards(): counts = mode_counts.astype(jnp.float32)]
    ppermute x1, waiting for transfers between devices: 0.01 us -> 1.15 us  [swap_edges(): lax.ppermute(before_src, axis, up)]
    another operation x3 -> x2, other arithmetic: 0.73 us -> 0.02 us  [row_table(): table = jnp.stack([1.0 / centre, faces])]
    unnamed x6 -> x4, local copies, waits for them, and re-layouts: 0.7 us -> 0.01 us
  transfers between devices with their start and end apart: 3 -> 2, of which waited for: 1 -> 2; matrix products, arithmetic and copies ran while one was open for 7% -> 1% of each run, Pallas kernels for 1% -> 1%
where the time goes in v8:
time: 36.9 us; the launch traced here: 36.7 us
  blocking collectives  26.9 us (73%)
  Pallas kernels  5.46 us (15%)
  starting transfers between devices  2.49 us (7%)
  waiting for transfers between devices  1.49 us (4%)
    all_to_all x1, blocking collectives, circled(): circles = lax.all_to_all(sent, 'lon', 0, 0, tiled=True)  15.3 us
    all_to_all x1, blocking collectives, circled(): pieces = lax.all_to_all(pieces, 'lon', 0, 0, tiled=True)  11.5 us
    pallas_call x6, Pallas kernels, run(): pl.pallas_call(kernel, out_shape=shapes, in_specs=[away if raw else vmem]...  5.46 us
    ppermute x1, starting transfers between devices, swap_edges(): lax.ppermute(after_src, axis, down)  1.99 us
    ppermute x1, waiting for transfers between devices, swap_edges(): lax.ppermute(before_src, axis, up)  1.15 us
  transfers between devices with their start and end apart: 2, of which 2 were waited for; matrix products, arithmetic and copies ran while one was open for 1% of the time, Pallas kernels for 1%

profile of v8, /device:TPU:0, one launch (start us, length us, event | category | flops | bytes accessed | tf_op | source)
XLA Modules:
  0.0 36.7 jit_solution(16397650075093531155)
XLA Ops:
  0.0 0.0 copy-start
  0.0 0.0 copy-start.1
  0.0 1.2 %shard_map.75 = (f32[4,8,16,128]{3,2,1,0:T(8,128)S(1)}, f32[8,16,128]{2,1,0:T(8,128)S(1)}, f32[8,16,128]{2,1,0:T(8,128)S(1)}, f32[6,8,2,128]{3,2,1,0:T(2,128)S(1...) custom-call(f32[4,8,16,128]{3,2,1,0:T(8,128)} %state_any.1, ...), custom_call_target="tpu_custom_call" | custom-call | bytes 507904 | tf_op jit(solution)/shard_map/pallas_call | solution.py:550
  1.2 0.5 %collective-permute-start.2 = (f32[6,8,2,128]{3,2,1,0:T(2,128)S(1)}, f32[6,8,2,128]{3,2,1,0:T(2,128)S(1)}, u32[]{:S(2)}, u32[]{:S(2)}) collective-permute-start(f32[6,8,2,128]{3,2,1,0:T(2,128)S(1)} %get-tuple-element.78), channel_id=1, source_target_pairs={{0,1},{1,2},{2,3},{3,0},{4,5},{5,6},{6,7},{7,4},{8,9},{9,10},{10,1... | collective-permute-start | bytes 147464 | tf_op jit(solution)/shard_map/ppermute | solution.py:567
  1.7 2.0 %collective-permute-start.3 = (f32[6,8,2,128]{3,2,1,0:T(2,128)S(1)}, f32[6,8,2,128]{3,2,1,0:T(2,128)S(1)}, u32[]{:S(2)}, u32[]{:S(2)}) collective-permute-start(f32[6,8,2,128]{3,2,1,0:T(2,128)S(1)} %get-tuple-element.79), channel_id=1, source_target_pairs={{1,0},{2,1},{3,2},{0,3},{5,4},{6,5},{7,6},{4,7},{9,8},{10,9},{11,1... | collective-permute-start | bytes 147464 | tf_op jit(solution)/shard_map/ppermute | solution.py:567
  3.7 0.1 multiply_cosine_fusion.1
  3.8 0.1 multiply_cosine_fusion
  3.9 0.1 broadcast_in_dim.26.table_ref
  4.0 0.3 shard_map.76
  4.3 1.1 %collective-permute-done.2.below_ref = f32[6,8,2,128]{3,2,1,0:T(2,128)S(1)} collective-permute-done((f32[6,8,2,128]{3,2,1,0:T(2,128)S(1)}, f32[6,8,2,128]{3,2,1,0:T(2,128)S(1)}, u32[]{:S(2)}, u32[]{:S(2)}) %collective-permute-start.2) | collective-permute-done | bytes 49184 | tf_op jit(solution)/shard_map/ppermute | solution.py:567
  5.4 0.3 collective-permute-done.3.above_ref
  5.8 1.7 %shard_map.77 = (f32[3,4,8,24,128]{4,3,2,1,0:T(8,128)S(1)}, f32[6,24,128]{2,1,0:T(8,128)S(1)}, f32[6,8,8,128]{3,2,1,0:T(8,128)S(1)}) custom-call(f32[4,8,16,128]{3,2,1,0:T(8,128)S(1)} %get-tuple-element.75.state_ref, f32[8,16,128]{2,1,0:T(8,128)S(1)} %get-tuple-element.76.thick_ref, f32[8,16,128]{2,1,0:T(8,128)S(1)} %get-tuple-element.77.wet_ref, ...), custom_call_target="tpu_custom_call" | custom-call | flops 5898240 | bytes 1449984 | tf_op jit(solution)/shard_map/pallas_call | solution.py:550
  7.5 0.0 copy-done
  7.5 0.0 copy-done.1
  7.5 29.2 %conditional.1 = (f32[4,8,16,128]{3,2,1,0:T(8,128)}) conditional(s32[]{:T(128)} %convert_element_type.31, (f32[4,8,16,128]{3,2,1,0:T(8,128)S(1)}, f32[8,16,128]{2,1,0:T(8,128)S(1)}, f32[8,16,128]{2,1,0:T(8,128)S(1)}, f32[6,8,8,128]{3,2,1,0:T(8,128)S(1)}, f32[3,4,8,24,128]{4,3,2,1,0:T(8,128)S(1)}, /*index=5*/f32[6,24,128]{2,1,0:T(8,128)S(1)}, ...), branch_computations={%region_0.1_spmd, %region_1.2_spmd} | conditional | bytes 2261256 | solution.py:685
  7.6 0.1 branch_1_fun.3
  7.7 15.3 %all_to_all.8.circle_ref = f32[8,88,128]{2,1,0:T(8,128)S(1)} all-to-all(f32[8,88,128]{2,1,0:T(8,128)S(1)} %branch_1_fun.3), channel_id=1, replica_groups=mesh['lon'=8,'lat'=4] {'lon'}, dimensions={0} | all-to-all | bytes 720896 | tf_op jit(solution)/shard_map/cond/branch_1_fun/all_to_all | solution.py:669
  23.0 0.1 broadcast_in_dim.3.table_ref
  23.1 1.2 %branch_1_fun.4 = f32[8,72,128]{2,1,0:T(8,128)S(1)} custom-call(f32[8,88,128]{2,1,0:T(8,128)S(1)} %all_to_all.8.circle_ref, f32[2,32,128]{2,1,0:T(8,128)S(1)} %broadcast_in_dim.3.table_ref, bf16[1024,256]{1,0:T(8,128)(2,1)S(1)} %get-tuple-element.52.basis_ref, bf16[512,256]{1,0:T(8,128)(2,1)S(1)} %get-tuple-element.53.joint_basis_ref, ...), custom_call_target="tpu_custom_call" | custom-call | bytes 294912 | tf_op jit(solution)/shard_map/cond/branch_1_fun/pallas_call | solution.py:550
  24.2 11.5 %all_to_all.9.piece_ref = f32[8,72,128]{2,1,0:T(8,128)S(1)} all-to-all(f32[8,72,128]{2,1,0:T(8,128)S(1)} %branch_1_fun.4), channel_id=1, replica_groups=mesh['lon'=8,'lat'=4] {'lon'}, dimensions={0} | all-to-all | bytes 589824 | tf_op jit(solution)/shard_map/cond/branch_1_fun/all_to_all | solution.py:679
  35.8 0.9 %branch_1_fun.5 = f32[4,8,16,128]{3,2,1,0:T(8,128)} custom-call(f32[3,4,8,24,128]{4,3,2,1,0:T(8,128)S(1)} %get-tuple-element.49.inner_ref, f32[8,72,128]{2,1,0:T(8,128)S(1)} %all_to_all.9.piece_ref, f32[8,16,128]{2,1,0:T(8,128)S(1)} %get-tuple-element.55.wet_ref, f32[16,128]{1,0:T(8,128)S(1)} %get-tuple-element.56.flag_ref), custom_call_target="tpu_custom_call" | custom-call | bytes 262144 | tf_op jit(solution)/shard_map/cond/branch_1_fun/pallas_call | solution.py:550
  (2 shorter events, 0.0 us)
Async XLA Ops:
  0.0 7.5 %copy-start = (bf16[1024,256]{1,0:T(8,128)(2,1)S(1)}, bf16[1024,256]{1,0:T(8,128)(2,1)}, u32[]{:S(2)}) copy-start(bf16[1024,256]{1,0:T(8,128)(2,1)} %constant.77.clone) | copy-start | bytes 1572868
  0.0 7.5 %copy-start.1 = (bf16[512,256]{1,0:T(8,128)(2,1)S(1)}, bf16[512,256]{1,0:T(8,128)(2,1)}, u32[]{:S(2)}) copy-start(bf16[512,256]{1,0:T(8,128)(2,1)} %constant.78.clone) | copy-start | bytes 786436
  1.2 4.2 %collective-permute-start.2 = (f32[6,8,2,128]{3,2,1,0:T(2,128)S(1)}, f32[6,8,2,128]{3,2,1,0:T(2,128)S(1)}, u32[]{:S(2)}, u32[]{:S(2)}) collective-permute-start(f32[6,8,2,128]{3,2,1,0:T(2,128)S(1)} %get-tuple-element.78), channel_id=1, source_target_pairs={{0,1},{1,2},{2,3},{3,0},{4,5},{5,6},{6,7},{7,4},{8,9},{9,10},{10,1... | collective-permute-start | bytes 147464 | tf_op jit(solution)/shard_map/ppermute | solution.py:567
  1.7 4.0 %collective-permute-start.3 = (f32[6,8,2,128]{3,2,1,0:T(2,128)S(1)}, f32[6,8,2,128]{3,2,1,0:T(2,128)S(1)}, u32[]{:S(2)}, u32[]{:S(2)}) collective-permute-start(f32[6,8,2,128]{3,2,1,0:T(2,128)S(1)} %get-tuple-element.79), channel_id=1, source_target_pairs={{1,0},{2,1},{3,2},{0,3},{5,4},{6,5},{7,6},{4,7},{9,8},{10,9},{11,1... | collective-permute-start | bytes 147464 | tf_op jit(solution)/shard_map/ppermute | solution.py:567

commit v9 on v8

--- a/solution.py
+++ b/solution.py
@@ -1,3 +1,4 @@
+import functools
 import math
 
 import jax
@@ -100,6 +101,7 @@
 
 
 def load_kernel(
+    paired,
     state_any,
     thick_any,
     wet_any,
@@ -141,6 +143,13 @@
             x = state_ref.at[f, k] if f < 4 else (thick_ref, wet_ref)[f - 4].at[k]
             first_ref[f, k] = x[0:2]
             last_ref[f, k] = x[rows - 2 : rows]
+    if paired:
+        even = lax.axis_index("lat") % 2 == 0
+        for f in range(6):
+            for k in range(levels):
+                low, high = first_ref[f, k], last_ref[f, k]
+                first_ref[f, k] = jnp.where(even, high, low)
+                last_ref[f, k] = jnp.where(even, low, high)
 
 
 def ready_kernel(state_ref, thick_ref, wet_ref, table_ref, own_ref, term_ref):
@@ -341,30 +350,146 @@
         place(y, made)
 
 
-def send_kernel(inner_ref, own_ref, out_ref, raw_ref):
-    levels, full = inner_ref.shape[2:4]
-    rows = full - 8
-    main = 8 * levels
+def step_levels(buf_ref, term_ref):
+    levels, size = buf_ref.shape[2:4]
+
+    def step(i, _):
+        source, target = buf_ref.at[i], buf_ref.at[i + 1]
+        fields = [source[f, 0] for f in range(4)]
+        above = [jnp.zeros((size, LANES), jnp.float32)] * 4
+        for k in range(levels):
+            deeper = below = above
+            if k + 1 < levels:
+                couple = term_ref[4, k]
+                deeper = [source[f, k + 1] for f in range(4)]
+                below = [couple * (d - q) for d, q in zip(deeper, fields)]
+                vertical = [b - a for b, a in zip(below, above)]
+            else:
+                vertical = [-a for a in above]
+            terms = [term_ref[i, k] for i in (0, 1, 5, 6)]
+            fresh = advance(fields, terms, term_ref[2, k], term_ref[3, k], vertical)
+            for f in range(4):
+                target[f, k] = fresh[f]
+            fields, above = deeper, below
+        return 0
+
+    lax.fori_loop(0, 2, step, 0)
+
+
+def closed_kernel(state_ref, thick_ref, wet_ref, table_ref, own_ref, buf_ref, term_ref):
+    levels, rows, lanes = thick_ref.shape
+
+    def thick(k):
+        return thick_ref[k]
+
+    def wet(k):
+        return wet_ref[k]
+
+    for f in range(4):
+        own_ref[f] = own_columns(lambda k, f=f: state_ref[f, k], levels, lanes, rows)
+    own_ref[4] = own_columns(thick, levels, lanes, rows)
+    own_ref[5] = own_columns(wet, levels, lanes, rows)
+    row_terms(thick, wet, table_ref[0, :rows], levels, term_ref)
+    row = lax.broadcasted_iota(jnp.int32, (rows, LANES), 0)
+    face = jnp.where(row < rows - 1, table_ref[1, :rows], 0.0)
+    for k in range(levels):
+        term_ref[5, k], term_ref[6, k] = north_terms(thick(k), wet(k), face)
+        for f in range(4):
+            buf_ref[0, f, k] = state_ref[f, k]
+    step_levels(buf_ref, term_ref)
+
+
+def end_kernel(
+    state_ref,
+    thick_ref,
+    wet_ref,
+    got_ref,
+    own_ref,
+    closed_ref,
+    table_ref,
+    out_ref,
+    send_ref,
+    field_ref,
+    halo_ref,
+    buf_ref,
+    term_ref,
+    raw_ref,
+):
+    levels, rows, lanes = thick_ref.shape
+    full = rows + 8
+    top = lax.axis_index("lat") == 0
+    at_top = jnp.where(top, 1.0, 0.0)
+    at_bottom = jnp.where(top, 0.0, 1.0)
+    sub = lax.broadcasted_iota(jnp.int32, (8, LANES), 0)
+
+    def own(f, k, part):
+        return state_ref[f, k, part] if f < 4 else (thick_ref, wet_ref)[f - 4][k, part]
+
+    for f in range(6):
+        for k in range(levels):
+            halo_ref[f, k, 0:2] = got_ref[f, k] * at_top
+            halo_ref[f, k, 2:6] = jnp.zeros((4, lanes), jnp.float32)
+            halo_ref[f, k, 6:8] = got_ref[f, k] * at_bottom
+    for f in range(6):
+        for k in range(levels):
+            halo = halo_ref[f, k]
+            beyond = jnp.where(sub < 6, roll(halo, 4, 0), 0.0)
+            high = jnp.where(sub < 4, roll(own(f, k, slice(rows - 8, rows)), -4, 0), beyond)
+            low = jnp.where(sub < 2, roll(halo, 2, 0), roll(own(f, k, slice(0, 8)), 2, 0))
+            tile = jnp.where(top, high, low)
+            if f < 4:
+                buf_ref[0, f, k] = tile
+            else:
+                field_ref[f - 4, k] = tile
+
+    def thick(k):
+        return field_ref[0, k]
+
+    def wet(k):
+        return field_ref[1, k]
+
+    row_terms(thick, wet, table_ref[0], levels, term_ref)
+    for k in range(levels):
+        term_ref[5, k], term_ref[6, k] = north_terms(thick(k), wet(k), table_ref[1])
+    step_levels(buf_ref, term_ref)
     c = lane_of((full, LANES)) % GROUP
+
+    def ring(f):
+        beyond = own_columns(lambda k: halo_ref[f, k], levels, lanes, 8)
+        return jnp.concatenate([own_ref[f], beyond], axis=0)
+
     for i in range(3):
-        a, b = own_ref[2 * i], own_ref[2 * i + 1]
+        a, b = ring(2 * i), ring(2 * i + 1)
         one = jnp.where(c < 4, roll(a, -2, 1), roll(a, -4, 1))
         two = jnp.where(c < 12, roll(b, 6, 1), roll(b, 4, 1))
         both = jnp.where(c < 8, one, two)
         raw_ref[i, 0:2] = both[full - 2 : full]
         raw_ref[i, 2 : rows + 4] = both[: rows + 2]
         raw_ref[i, rows + 4 : full] = jnp.zeros((4, LANES), jnp.float32)
+    main = 8 * levels
+    last = rows // 8 - 1
     for t in range(rows // 8):
-        for k in range(levels):
-            tiles = [inner_ref[2, f, k, 8 * t : 8 * t + 8] for f in range(4)]
+        part = slice(8 * t, 8 * t + 8)
+        for k in range(levels):
+            tiles = []
+            for f in range(4):
+                x = closed_ref[2, f, k, part]
+                if t == last:
+                    fixed = jnp.where(sub >= 6, roll(buf_ref[2, f, k], 4, 0), x)
+                    x = jnp.where(top, fixed, x)
+                if t == 0:
+                    fixed = jnp.where(sub < 2, roll(buf_ref[2, f, k], -2, 0), x)
+                    x = jnp.where(top, x, fixed)
+                out_ref[f, k, part] = x
+                tiles.append(x)
 
             def place(y, tile, t=t, k=k):
-                out_ref[4 * t + y, 8 * k : 8 * k + 8] = tile
+                send_ref[4 * t + y, 8 * k : 8 * k + 8] = tile
 
             pairs_of_rows(tiles, t, place)
         for p in range(4 * t, 4 * t + 4):
             for i in range(3):
-                out_ref[p, main + 8 * i : main + 8 * i + 8] = raw_ref[i, 2 * p : 2 * p + 8]
+                send_ref[p, main + 8 * i : main + 8 * i + 8] = raw_ref[i, 2 * p : 2 * p + 8]
 
 
 def circle_kernel(
@@ -450,39 +575,38 @@
         out_ref[o + 1, main:] = here
 
 
-def join_kernel(inner_ref, piece_ref, wet_ref, flag_ref, out_ref, made_ref, sems):
+def join_kernel(state_ref, piece_ref, wet_ref, flag_ref, out_ref, made_ref, sems):
     levels, rows, lanes = wet_ref.shape
     main = 8 * levels
     lane = lane_of((8, LANES))
-
-    def edges_of(t, into):
+    edges = [{} for _ in range(rows // 8)]
+    for t, into in enumerate(edges):
         tiles = [piece_ref[4 * t + x, main : main + 8] for x in range(4)]
-        pairs_of_rows(tiles, t, into)
-
-    for t in range(rows // 8):
-        part = slice(8 * t, 8 * t + 8)
-        flag = flag_ref[part]
-        edges = {}
-        edges_of(t, edges.__setitem__)
-        for k in range(levels):
+        pairs_of_rows(tiles, t, into.__setitem__)
+    copies = []
+    for k in range(levels):
+        for t in range(rows // 8):
+            part = slice(8 * t, 8 * t + 8)
             tiles = [piece_ref[4 * t + x, 8 * k : 8 * k + 8] for x in range(4)]
-            gate = flag * wet_ref[k, part]
-
-            def place(f, smooth, k=k, gate=gate, part=part, edges=edges):
-                first = roll(edges[f], -(GROUP * k + 4), 1)
-                last = roll(edges[f], lanes - 2 - (GROUP * k + 10), 1)
+            gate = flag_ref[part] * wet_ref[k, part]
+
+            def place(f, smooth, k=k, gate=gate, part=part, edge=edges[t]):
+                first = roll(edge[f], -(GROUP * k + 4), 1)
+                last = roll(edge[f], lanes - 2 - (GROUP * k + 10), 1)
                 state = jnp.where(
-                    lane < 2,
-                    first,
-                    jnp.where(lane >= lanes - 2, last, inner_ref[2, f, k, part]),
+                    lane < 2, first, jnp.where(lane >= lanes - 2, last, state_ref[f, k, part])
                 )
                 made_ref[f, k, part] = state + gate * (smooth - state)
 
             pairs_of_rows(tiles, t, place)
-    copies = []
-    for f in range(4):
-        copies.append(pltpu.make_async_copy(made_ref.at[f], out_ref.at[f], sems.at[f]))
-        copies[-1].start()
+        if k % 2:
+            both = pl.ds(k - 1, 2)
+            copies.append(
+                pltpu.make_async_copy(
+                    made_ref.at[:, both], out_ref.at[:, both], sems.at[k // 2]
+                )
+            )
+            copies[-1].start()
     for copy in copies:
         copy.wait()
 
@@ -621,27 +745,28 @@
     cells = 4 * levels * full * lanes
     edge_rows = (6, levels, 2, lanes)
 
+    paired = rows == 2 * lon_peers and rows >= FBAND and lat_peers % 2 == 0 and levels % 2 == 0
     *block, first, last, flags, counts = call(
-        load_kernel,
+        functools.partial(load_kernel, paired),
         [ocean_state.shape, thickness.shape, thickness.shape, edge_rows, edge_rows]
         + [(rows, lanes)] * 2,
         [pltpu.VMEM(shape, jnp.int32) for shape in (thickness.shape, (1, rows), (1, rows))],
         sems=8,
         raw=True,
     )(ocean_state, thickness, wet_mask, row_flags[None], mode_counts[None])
-    below, above = swap_edges(last, first, "lat")
-    own, terms = call(
-        ready_kernel, [(6, rows, LANES), (5, levels, rows, lanes)], flops=20 * cells
-    )(*block, table)
-    below, above, own, terms = lax.optimization_barrier((below, above, own, terms))
-    inner, edges, halo = call(
-        inner_kernel,
-        [(3, 4, levels, full, lanes), (6, full, LANES), (6, levels, 8, lanes)],
-        [(5, levels, 8, lanes), (2, levels, full, lanes)],
-        flops=60 * cells,
-    )(*block, below, above, table, own, terms)
-
-    def exchanged():
+
+    def ready():
+        return call(
+            ready_kernel, [(6, rows, LANES), (5, levels, rows, lanes)], flops=20 * cells
+        )(*block, table)
+
+    def exchanged(below, above, own, terms):
+        inner, edges, halo = call(
+            inner_kernel,
+            [(3, 4, levels, full, lanes), (6, full, LANES), (6, levels, 8, lanes)],
+            [(5, levels, 8, lanes), (2, levels, full, lanes)],
+            flops=60 * cells,
+        )(*block, below, above, table, own, terms)
         first, last = call(pack_kernel, [(full, LANES)] * 2)(*block, halo)
         from_west, from_east = swap_edges(last, first, "lon")
         return call(
@@ -661,11 +786,14 @@
     place = first_row + 2 * lon_pos - 2 + jnp.arange(4 * lon_peers, dtype=jnp.int32) % 8
     joint_table = row_table(jnp.minimum(place, first_row + 2 * lon_pos + 3), nlat)
 
-    def circled():
+    def circled(got, own, closed):
         main = 8 * levels
-        sent = call(
-            send_kernel, [(lon_peers, main + 24, lanes)], [(3, full, lanes)]
-        )(inner, edges)[0]
+        tile = (levels, 8, lanes)
+        state, sent = call(
+            end_kernel,
+            [ocean_state.shape, (lon_peers, main + 24, lanes)],
+            [(2,) + tile, (6,) + tile, (3, 4) + tile, (7,) + tile, (3, full, lanes)],
+        )(*block, got, own, closed, end_table)
         circles = lax.all_to_all(sent, "lon", 0, 0, tiled=True)
         pieces = call(
             circle_kernel,
@@ -677,14 +805,33 @@
             ],
         )(circles, joint_table, basis, at_joints, counts)[0]
         pieces = lax.all_to_all(pieces, "lon", 0, 0, tiled=True)
-        return call(join_kernel, [ocean_state.shape], [ocean_state.shape], sems=4, sent=True)(
-            inner, pieces, block[2], flags
-        )[0]
-
-    if rows == 2 * lon_peers:
-        return lax.cond(banded, circled, lambda: exchanged()[1])
-
-    state, sent = exchanged()
+        return call(
+            join_kernel, [ocean_state.shape], [ocean_state.shape], sems=levels // 2, sent=True
+        )(state, pieces, block[2], flags)[0]
+
+    def between(got, *_):
+        pairs = [(i, i + 1) for i in range(1, lat_peers - 1, 2)]
+        other = lax.ppermute(last, "lat", pairs + [(j, i) for i, j in pairs])
+        even = lat_pos % 2 == 0
+        below, above = jnp.where(even, other, got), jnp.where(even, got, other)
+        return exchanged(below, above, *ready())[1]
+
+    if paired:
+        ends = jnp.where(lat_pos == 0, first_row + rows - 4, first_row - 2)
+        end_place = ends + jnp.minimum(jnp.arange(8, dtype=jnp.int32), 5)
+        end_table = row_table(end_place, nlat)
+        got = lax.ppermute(first, "lat", [(i, i ^ 1) for i in range(lat_peers)])
+        own, closed = call(
+            closed_kernel,
+            [(6, rows, LANES), (3, 4, levels, rows, lanes)],
+            [(7, levels, rows, lanes)],
+            flops=60 * cells,
+        )(*block, table)
+        got, own, closed = lax.optimization_barrier((got, own, closed))
+        return lax.cond(banded, circled, between, got, own, closed)
+
+    below, above = swap_edges(last, first, "lat")
+    state, sent = exchanged(*lax.optimization_barrier((below, above, *ready())))
 
     def filtered():
         row_counts = lax.dynamic_slice(

time: 36.9 us -> 33.8 us (0.916)
  starting transfers between devices: 2.49 us -> 0.52 us
  waiting for transfers between devices: 1.49 us -> 0.01 us
  blocking collectives: 26.9 us -> 27.5 us
  Pallas kernels: 5.46 us -> 4.92 us
    ppermute x2 -> x1, starting transfers between devices: 2.49 us -> 0.52 us  [shards(): got = lax.ppermute(first, 'lat', [(i, i ^ 1) for i in range(lat_peers)])]
    ppermute x2 -> x1, waiting for transfers between devices: 1.49 us -> 0.01 us  [shards(): got = lax.ppermute(first, 'lat', [(i, i ^ 1) for i in range(lat_peers)])]
    all_to_all x1, blocking collectives: 15.3 us -> 16 us  [circled(): circles = lax.all_to_all(sent, 'lon', 0, 0, tiled=True)]
    pallas_call x6 -> x5, Pallas kernels: 5.46 us -> 4.92 us  [run(): pl.pallas_call(kernel, out_shape=shapes, in_specs=[away if raw else vmem]...]
  transfers between devices with their start and end apart: 2 -> 1, of which waited for: 2 -> 0; matrix products, arithmetic and copies ran while one was open for 1% -> 1% of each run, Pallas kernels for 1% -> 3%
where the time goes in v9:
time: 33.8 us; the launch traced here: 33.5 us
  blocking collectives  27.5 us (81%)
  Pallas kernels  4.92 us (15%)
  starting transfers between devices  0.52 us (2%)
    all_to_all x1, blocking collectives, circled(): circles = lax.all_to_all(sent, 'lon', 0, 0, tiled=True)  16 us
    all_to_all x1, blocking collectives, circled(): pieces = lax.all_to_all(pieces, 'lon', 0, 0, tiled=True)  11.5 us
    pallas_call x5, Pallas kernels, run(): pl.pallas_call(kernel, out_shape=shapes, in_specs=[away if raw else vmem]...  4.92 us
  transfers between devices with their start and end apart: 1, of which 0 were waited for; matrix products, arithmetic and copies ran while one was open for 1% of the time, Pallas kernels for 3%

profile of v9, /device:TPU:0, one launch (start us, length us, event | category | flops | bytes accessed | tf_op | source)
XLA Modules:
  0.0 33.5 jit_solution(15252168453929968812)
XLA Ops:
  0.0 1.2 %shard_map.75 = (f32[4,8,16,128]{3,2,1,0:T(8,128)S(1)}, f32[8,16,128]{2,1,0:T(8,128)S(1)}, f32[8,16,128]{2,1,0:T(8,128)S(1)}, f32[6,8,2,128]{3,2,1,0:T(2,128)S(1...) custom-call(f32[4,8,16,128]{3,2,1,0:T(8,128)} %state_any.1, ...), custom_call_target="tpu_custom_call" | custom-call | bytes 507904 | tf_op jit(solution)/shard_map/pallas_call | solution.py:674
  1.2 0.5 %collective-permute-start.3 = (f32[6,8,2,128]{3,2,1,0:T(2,128)S(1)}, f32[6,8,2,128]{3,2,1,0:T(2,128)S(1)}, u32[]{:S(2)}, u32[]{:S(2)}) collective-permute-start(f32[6,8,2,128]{3,2,1,0:T(2,128)S(1)} %get-tuple-element.92), channel_id=1, source_target_pairs={{0,1},{1,0},{2,3},{3,2},{4,5},{5,4},{6,7},{7,6},{8,9},{9,8},{10,11... | collective-permute-start | bytes 147464 | tf_op jit(solution)/shard_map/ppermute | solution.py:823
  1.7 0.1 multiply_cosine_fusion.2
  1.8 0.1 multiply_cosine_fusion.1
  1.8 0.1 multiply_cosine_fusion
  2.0 0.1 broadcast_in_dim.33.table_ref
  2.0 0.9 %shard_map.76 = (f32[6,16,128]{2,1,0:T(8,128)S(1)}, f32[3,4,8,16,128]{4,3,2,1,0:T(8,128)S(1)}) custom-call(f32[4,8,16,128]{3,2,1,0:T(8,128)S(1)} %get-tuple-element.93.state_ref, f32[8,16,128]{2,1,0:T(8,128)S(1)} %get-tuple-element.94.thick_ref, f32[8,16,128]{2,1,0:T(8,128)S(1)} %get-tuple-element.95.wet_ref, f32[2,24,128]{2,1,0:T(8,128)S(1)} %broadcast_in_dim.33.table_ref), custom_call_target="tpu_custom_call" | custom-call | flops 5898240 | bytes 835584 | tf_op jit(solution)/shard_map/pallas_call | solution.py:674
  2.9 0.0 collective-permute-done.3
  2.9 30.6 %conditional.1 = (f32[4,8,16,128]{3,2,1,0:T(8,128)}) conditional(s32[]{:T(128)} %convert_element_type.45, (s32[]{:T(128)}, f32[6,8,2,128]{3,2,1,0:T(2,128)S(1)}, f32[6,8,2,128]{3,2,1,0:T(2,128)S(1)}, f32[4,8,16,128]{3,2,1,0:T(8,128)S(1)}, f32[8,16,128]{2,1,0:T(8,128)S(1)}, /*index=5*/f32[8,16,128]{2,1,0:T(8,128)S(1)}, ...), branch_computations={%region_0.1_spmd, %region_1.2_spmd} | conditional | flops 7888908 | bytes 5677440 | solution.py:831
  2.9 0.0 copy-start
  2.9 0.0 copy-start.1
  3.0 0.1 broadcast_in_dim.4.table_ref
  3.0 0.9 %branch_1_fun.3 = (f32[4,8,16,128]{3,2,1,0:T(8,128)S(1)}, f32[8,88,128]{2,1,0:T(8,128)S(1)}) custom-call(f32[4,8,16,128]{3,2,1,0:T(8,128)S(1)} %get-tuple-element.63.state_ref, f32[8,16,128]{2,1,0:T(8,128)S(1)} %get-tuple-element.64.thick_ref, f32[8,16,128]{2,1,0:T(8,128)S(1)} %get-tuple-element.65.wet_ref, f32[6,8,2,128]{3,2,1,0:T(2,128)S(1)} %get-tuple-element.66.got_ref, ...), custom_call_target="tpu_custom_call" | custom-call | bytes 622592 | tf_op jit(solution)/shard_map/cond/branch_1_fun/pallas_call | solution.py:674
  3.9 16.0 %all_to_all.8.circle_ref = f32[8,88,128]{2,1,0:T(8,128)S(1)} all-to-all(f32[8,88,128]{2,1,0:T(8,128)S(1)} %get-tuple-element.71), channel_id=1, replica_groups=mesh['lon'=8,'lat'=4] {'lon'}, dimensions={0} | all-to-all | bytes 720896 | tf_op jit(solution)/shard_map/cond/branch_1_fun/all_to_all | solution.py:797
  19.9 0.1 broadcast_in_dim.5.table_ref
  20.0 0.0 copy-done
  20.0 0.0 copy-done.1
  20.0 1.2 %branch_1_fun.4 = f32[8,72,128]{2,1,0:T(8,128)S(1)} custom-call(f32[8,88,128]{2,1,0:T(8,128)S(1)} %all_to_all.8.circle_ref, f32[2,32,128]{2,1,0:T(8,128)S(1)} %broadcast_in_dim.5.table_ref, bf16[1024,256]{1,0:T(8,128)(2,1)S(1)} %copy-done, bf16[512,256]{1,0:T(8,128)(2,1)S(1)} %copy-done.1, f32[16,128]{1,0:T(8,128)S(1)} %get-tuple-element.75.count_ref), custom_call_target="tpu_custom_call" | custom-call | bytes 294912 | tf_op jit(solution)/shard_map/cond/branch_1_fun/pallas_call | solution.py:674
  21.1 11.5 %all_to_all.9.piece_ref = f32[8,72,128]{2,1,0:T(8,128)S(1)} all-to-all(f32[8,72,128]{2,1,0:T(8,128)S(1)} %branch_1_fun.4), channel_id=1, replica_groups=mesh['lon'=8,'lat'=4] {'lon'}, dimensions={0} | all-to-all | bytes 589824 | tf_op jit(solution)/shard_map/cond/branch_1_fun/all_to_all | solution.py:807
  32.7 0.9 %branch_1_fun.5 = f32[4,8,16,128]{3,2,1,0:T(8,128)} custom-call(f32[4,8,16,128]{3,2,1,0:T(8,128)S(1)} %get-tuple-element.70.state_ref, f32[8,72,128]{2,1,0:T(8,128)S(1)} %all_to_all.9.piece_ref, f32[8,16,128]{2,1,0:T(8,128)S(1)} %get-tuple-element.65.wet_ref, f32[16,128]{1,0:T(8,128)S(1)} %get-tuple-element.76.flag_ref), custom_call_target="tpu_custom_call" | custom-call | bytes 262144 | tf_op jit(solution)/shard_map/cond/branch_1_fun/pallas_call | solution.py:674
  (3 shorter events, 0.0 us)
Async XLA Ops:
  1.2 1.7 %collective-permute-start.3 = (f32[6,8,2,128]{3,2,1,0:T(2,128)S(1)}, f32[6,8,2,128]{3,2,1,0:T(2,128)S(1)}, u32[]{:S(2)}, u32[]{:S(2)}) collective-permute-start(f32[6,8,2,128]{3,2,1,0:T(2,128)S(1)} %get-tuple-element.92), channel_id=1, source_target_pairs={{0,1},{1,0},{2,3},{3,2},{4,5},{5,4},{6,7},{7,6},{8,9},{9,8},{10,11... | collective-permute-start | bytes 147464 | tf_op jit(solution)/shard_map/ppermute | solution.py:823
  2.9 17.1 %copy-start = (bf16[1024,256]{1,0:T(8,128)(2,1)S(1)}, bf16[1024,256]{1,0:T(8,128)(2,1)}, u32[]{:S(2)}) copy-start(bf16[1024,256]{1,0:T(8,128)(2,1)} %get-tuple-element.73.basis_ref) | copy-start | bytes 1572868 | tf_op jit(solution)/shard_map/cond
  2.9 17.0 %copy-start.1 = (bf16[512,256]{1,0:T(8,128)(2,1)S(1)}, bf16[512,256]{1,0:T(8,128)(2,1)}, u32[]{:S(2)}) copy-start(bf16[512,256]{1,0:T(8,128)(2,1)} %get-tuple-element.74.joint_basis_ref) | copy-start | bytes 786436 | tf_op jit(solution)/shard_map/cond

commit v10 on v9

--- a/solution.py
+++ b/solution.py
@@ -100,6 +100,17 @@
             w, h, hs = w_next, h_next, hs_next
 
 
+def fill_table(ref, place, nlat):
+    place = place.astype(jnp.float32)
+    ref[0] = 1.0 / jnp.cos(lat_edge * (2.0 * (place + 0.5) / nlat - 1.0))
+    ref[1] = jnp.cos(lat_edge * (2.0 * (place + 1.0) / nlat - 1.0))
+
+
+def ring_rows(rows):
+    place = lax.broadcasted_iota(jnp.int32, (rows + 8, LANES), 0)
+    return jnp.where(place < rows + 2, place, jnp.where(place < rows + 6, 0, place - rows - 8))
+
+
 def load_kernel(
     paired,
     state_any,
@@ -114,6 +125,9 @@
     last_ref,
     flag_ref,
     count_ref,
+    table_ref,
+    end_table_ref,
+    joint_table_ref,
     raw_ref,
     raw_flag_ref,
     raw_count_ref,
@@ -126,6 +140,15 @@
     copies = [pltpu.make_async_copy(*pair, sems.at[i]) for i, pair in enumerate(moves)]
     for copy in copies:
         copy.start()
+    nlat = rows * lax.axis_size("lat")
+    lat_pos = lax.axis_index("lat")
+    first_row = lat_pos * rows
+    fill_table(table_ref, first_row + ring_rows(rows), nlat)
+    if paired:
+        six = jnp.minimum(lax.broadcasted_iota(jnp.int32, (8, LANES), 0), 5)
+        end = jnp.where(lat_pos == 0, rows - 4, -2)
+        fill_table(end_table_ref, first_row + end + six, nlat)
+        fill_table(joint_table_ref, first_row + 2 * lax.axis_index("lon") - 2 + six, nlat)
     for copy in copies[:3]:
         copy.wait()
     shape = (rows, rows)
@@ -263,8 +286,7 @@
     lax.fori_loop(0, 2, step, 0)
 
 
-def step_tile(tile_ref, h, w, levels, table_ref, term_ref):
-    inv_c, face = table_ref[0], table_ref[1]
+def step_tile(tile_ref, h, w, levels, inv_c, face, term_ref):
     lane = lane_of(h.shape)
 
     def deeper(x):
@@ -281,7 +303,7 @@
     for i, term in enumerate(terms + (scale, scale * inv_c, couple)):
         term_ref[i] = term
 
-    def step(_, __):
+    def step():
         terms = [term_ref[i] for i in range(7)]
         fields = [tile_ref[f] for f in range(4)]
         vertical = []
@@ -290,9 +312,9 @@
             vertical.append(down - shallower(down))
         for f, q in enumerate(advance(fields, terms[:4], terms[4], terms[5], vertical)):
             tile_ref[f] = q
-        return 0
-
-    lax.fori_loop(0, 2, step, 0)
+
+    step()
+    step()
 
 
 def edge_kernel(
@@ -315,7 +337,7 @@
 
     for f in range(4):
         tile_ref[f] = joined(f)
-    step_tile(tile_ref, joined(4), joined(5), levels, table_ref, term_ref)
+    step_tile(tile_ref, joined(4), joined(5), levels, table_ref[0], table_ref[1], term_ref)
     lane = lane_of((rows, LANES))
     for f in range(4):
         x = tile_ref[f, :rows]
@@ -350,7 +372,7 @@
         place(y, made)
 
 
-def step_levels(buf_ref, term_ref):
+def step_levels(buf_ref, term_ref, loop):
     levels, size = buf_ref.shape[2:4]
 
     def step(i, _):
@@ -373,7 +395,10 @@
             fields, above = deeper, below
         return 0
 
-    lax.fori_loop(0, 2, step, 0)
+    if loop:
+        lax.fori_loop(0, 2, step, 0)
+    else:
+        step(1, step(0, 0))
 
 
 def closed_kernel(state_ref, thick_ref, wet_ref, table_ref, own_ref, buf_ref, term_ref):
@@ -396,7 +421,7 @@
         term_ref[5, k], term_ref[6, k] = north_terms(thick(k), wet(k), face)
         for f in range(4):
             buf_ref[0, f, k] = state_ref[f, k]
-    step_levels(buf_ref, term_ref)
+    step_levels(buf_ref, term_ref, True)
 
 
 def end_kernel(
@@ -451,7 +476,7 @@
     row_terms(thick, wet, table_ref[0], levels, term_ref)
     for k in range(levels):
         term_ref[5, k], term_ref[6, k] = north_terms(thick(k), wet(k), table_ref[1])
-    step_levels(buf_ref, term_ref)
+    step_levels(buf_ref, term_ref, False)
     c = lane_of((full, LANES)) % GROUP
 
     def ring(f):
@@ -520,7 +545,8 @@
             for f, shift in ((2 * i, 0), (2 * i + 1, -8)):
                 middle = jnp.where(c < 12, roll(y, 4 + shift, 1), roll(z, 12 + shift, 1))
                 tile_ref[f, part] = jnp.where(c < 4, roll(x, shift - 4, 1), middle)
-    step_tile(tile_ref, tile_ref[4], tile_ref[5], levels, table_ref, term_ref)
+    inv_c, face = (jnp.concatenate([table_ref[i]] * (peers // 2), axis=0) for i in (0, 1))
+    step_tile(tile_ref, tile_ref[4], tile_ref[5], levels, inv_c, face, term_ref)
     sub = lax.broadcasted_iota(jnp.int32, (8, LANES), 0) // 2
     right = (c % 8 >= 2) & (c % 8 < 6)
     for j in range(peers // 2):
@@ -716,19 +742,6 @@
     return jnp.concatenate([weights, weights], axis=1)
 
 
-def row_table(place, nlat):
-    place = place.astype(jnp.float32)
-    centre = jnp.cos(lat_edge * (2.0 * (place + 0.5) / nlat - 1.0))
-    faces = jnp.cos(lat_edge * (2.0 * (place + 1.0) / nlat - 1.0))
-    table = jnp.stack([1.0 / centre, faces])
-    return jnp.broadcast_to(table[:, :, None], table.shape + (LANES,))
-
-
-def ring_rows(rows):
-    place = jnp.arange(rows + 8, dtype=jnp.int32)
-    return jnp.where(place < rows + 2, place, jnp.where(place < rows + 6, 0, place - rows - 8))
-
-
 def shards(ocean_state, thickness, wet_mask, mode_counts, row_flags):
     levels, rows, lanes = ocean_state.shape[1:]
     assert rows % 8 == 0 and lanes == LANES and levels * GROUP <= LANES
@@ -741,15 +754,15 @@
     part = total // lon_peers
     lat_pos = lax.axis_index("lat")
     first_row = lat_pos * rows
-    table = row_table(first_row + ring_rows(rows), nlat)
     cells = 4 * levels * full * lanes
     edge_rows = (6, levels, 2, lanes)
 
     paired = rows == 2 * lon_peers and rows >= FBAND and lat_peers % 2 == 0 and levels % 2 == 0
-    *block, first, last, flags, counts = call(
+    *block, first, last, flags, counts, table, end_table, joint_table = call(
         functools.partial(load_kernel, paired),
         [ocean_state.shape, thickness.shape, thickness.shape, edge_rows, edge_rows]
-        + [(rows, lanes)] * 2,
+        + [(rows, lanes)] * 2
+        + [(2, full, lanes), (2, 8, lanes), (2, 8, lanes)],
         [pltpu.VMEM(shape, jnp.int32) for shape in (thickness.shape, (1, rows), (1, rows))],
         sems=8,
         raw=True,
@@ -783,8 +796,6 @@
         (jnp.asarray(modes), jnp.asarray(joint_basis(modes, lanes)))
     )
     lon_pos = lax.axis_index("lon")
-    place = first_row + 2 * lon_pos - 2 + jnp.arange(4 * lon_peers, dtype=jnp.int32) % 8
-    joint_table = row_table(jnp.minimum(place, first_row + 2 * lon_pos + 3), nlat)
 
     def circled(got, own, closed):
         main = 8 * levels
@@ -817,9 +828,6 @@
         return exchanged(below, above, *ready())[1]
 
     if paired:
-        ends = jnp.where(lat_pos == 0, first_row + rows - 4, first_row - 2)
-        end_place = ends + jnp.minimum(jnp.arange(8, dtype=jnp.int32), 5)
-        end_table = row_table(end_place, nlat)
         got = lax.ppermute(first, "lat", [(i, i ^ 1) for i in range(lat_peers)])
         own, closed = call(
             closed_kernel,

time: 33.8 us -> 33.1 us (0.979)
  Pallas kernels: 4.92 us -> 4.43 us
    pallas_call x5, Pallas kernels: 4.92 us -> 4.43 us  [run(): pl.pallas_call(kernel, out_shape=shapes, in_specs=[away if raw else vmem]...]
  transfers between devices with their start and end apart: 1 -> 1, of which waited for: 0 -> 0; matrix products, arithmetic and copies ran while one was open for 1% -> 0% of each run, Pallas kernels for 3% -> 3%
where the time goes in v10:
time: 33.1 us; the launch traced here: 32.9 us
  blocking collectives  27.8 us (84%)
  Pallas kernels  4.43 us (13%)
  starting transfers between devices  0.52 us (2%)
    all_to_all x1, blocking collectives, circled(): circles = lax.all_to_all(sent, 'lon', 0, 0, tiled=True)  16.3 us
    all_to_all x1, blocking collectives, circled(): pieces = lax.all_to_all(pieces, 'lon', 0, 0, tiled=True)  11.5 us
    pallas_call x5, Pallas kernels, run(): pl.pallas_call(kernel, out_shape=shapes, in_specs=[away if raw else vmem]...  4.43 us
  transfers between devices with their start and end apart: 1, of which 0 were waited for; matrix products, arithmetic and copies ran while one was open for 0% of the time, Pallas kernels for 3%

profile of v10, /device:TPU:0, one launch (start us, length us, event | category | flops | bytes accessed | tf_op | source)
XLA Modules:
  0.0 32.9 jit_solution(18204540337872292104)
XLA Ops:
  0.0 1.2 %shard_map.75 = (f32[4,8,16,128]{3,2,1,0:T(8,128)S(1)}, f32[8,16,128]{2,1,0:T(8,128)S(1)}, f32[8,16,128]{2,1,0:T(8,128)S(1)}, f32[6,8,2,128]{3,2,1,0:T(2,128)S(1...) custom-call(f32[4,8,16,128]{3,2,1,0:T(8,128)} %state_any.1, ...), custom_call_target="tpu_custom_call" | custom-call | bytes 548864 | tf_op jit(solution)/shard_map/pallas_call | solution.py:700
  1.2 0.5 %collective-permute-start.3 = (f32[6,8,2,128]{3,2,1,0:T(2,128)S(1)}, f32[6,8,2,128]{3,2,1,0:T(2,128)S(1)}, u32[]{:S(2)}, u32[]{:S(2)}) collective-permute-start(f32[6,8,2,128]{3,2,1,0:T(2,128)S(1)} %get-tuple-element.93), channel_id=1, source_target_pairs={{0,1},{1,0},{2,3},{3,2},{4,5},{5,4},{6,7},{7,6},{8,9},{9,8},{10,11... | collective-permute-start | bytes 147464 | tf_op jit(solution)/shard_map/ppermute | solution.py:831
  1.7 0.9 %shard_map.76 = (f32[6,16,128]{2,1,0:T(8,128)S(1)}, f32[3,4,8,16,128]{4,3,2,1,0:T(8,128)S(1)}) custom-call(f32[4,8,16,128]{3,2,1,0:T(8,128)S(1)} %get-tuple-element.94.state_ref, f32[8,16,128]{2,1,0:T(8,128)S(1)} %get-tuple-element.95.thick_ref, f32[8,16,128]{2,1,0:T(8,128)S(1)} %get-tuple-element.96.wet_ref, f32[2,24,128]{2,1,0:T(8,128)S(1)} %get-tuple-element.97.table_ref), custom_call_target="tpu_custom_call" | custom-call | flops 5898240 | bytes 835584 | tf_op jit(solution)/shard_map/pallas_call | solution.py:700
  2.6 0.0 collective-permute-done.3
  2.6 30.3 %conditional.1 = (f32[4,8,16,128]{3,2,1,0:T(8,128)}) conditional(s32[]{:T(128)} %convert_element_type.3, (s32[]{:T(128)}, f32[6,8,2,128]{3,2,1,0:T(2,128)S(1)}, f32[6,8,2,128]{3,2,1,0:T(2,128)S(1)}, f32[4,8,16,128]{3,2,1,0:T(8,128)S(1)}, f32[8,16,128]{2,1,0:T(8,128)S(1)}, /*index=5*/f32[8,16,128]{2,1,0:T(8,128)S(1)}, ...), branch_computations={%region_0.1_spmd, %region_1.2_spmd} | conditional | flops 7888908 | bytes 5636160 | solution.py:839
  2.6 0.0 copy-start
  2.6 0.0 copy-start.1
  2.6 0.6 %branch_1_fun.3 = (f32[4,8,16,128]{3,2,1,0:T(8,128)S(1)}, f32[8,88,128]{2,1,0:T(8,128)S(1)}) custom-call(f32[4,8,16,128]{3,2,1,0:T(8,128)S(1)} %get-tuple-element.61.state_ref, f32[8,16,128]{2,1,0:T(8,128)S(1)} %get-tuple-element.62.thick_ref, f32[8,16,128]{2,1,0:T(8,128)S(1)} %get-tuple-element.63.wet_ref, f32[6,8,2,128]{3,2,1,0:T(2,128)S(1)} %get-tuple-element.64.got_ref, ...), custom_call_target="tpu_custom_call" | custom-call | bytes 622592 | tf_op jit(solution)/shard_map/cond/branch_1_fun/pallas_call | solution.py:700
  3.2 16.3 %all_to_all.8.circle_ref = f32[8,88,128]{2,1,0:T(8,128)S(1)} all-to-all(f32[8,88,128]{2,1,0:T(8,128)S(1)} %get-tuple-element.69), channel_id=1, replica_groups=mesh['lon'=8,'lat'=4] {'lon'}, dimensions={0} | all-to-all | bytes 720896 | tf_op jit(solution)/shard_map/cond/branch_1_fun/all_to_all | solution.py:808
  19.5 0.0 copy-done
  19.5 0.0 copy-done.1
  19.5 0.9 %branch_1_fun.4 = f32[8,72,128]{2,1,0:T(8,128)S(1)} custom-call(f32[8,88,128]{2,1,0:T(8,128)S(1)} %all_to_all.8.circle_ref, f32[2,8,128]{2,1,0:T(8,128)S(1)} %get-tuple-element.70.table_ref, bf16[1024,256]{1,0:T(8,128)(2,1)S(1)} %copy-done, bf16[512,256]{1,0:T(8,128)(2,1)S(1)} %copy-done.1, f32[16,128]{1,0:T(8,128)S(1)} %get-tuple-element.73.count_ref), custom_call_target="tpu_custom_call" | custom-call | bytes 294912 | tf_op jit(solution)/shard_map/cond/branch_1_fun/pallas_call | solution.py:700
  20.5 11.5 %all_to_all.9.piece_ref = f32[8,72,128]{2,1,0:T(8,128)S(1)} all-to-all(f32[8,72,128]{2,1,0:T(8,128)S(1)} %branch_1_fun.4), channel_id=1, replica_groups=mesh['lon'=8,'lat'=4] {'lon'}, dimensions={0} | all-to-all | bytes 589824 | tf_op jit(solution)/shard_map/cond/branch_1_fun/all_to_all | solution.py:818
  32.0 0.9 %branch_1_fun.5 = f32[4,8,16,128]{3,2,1,0:T(8,128)} custom-call(f32[4,8,16,128]{3,2,1,0:T(8,128)S(1)} %get-tuple-element.68.state_ref, f32[8,72,128]{2,1,0:T(8,128)S(1)} %all_to_all.9.piece_ref, f32[8,16,128]{2,1,0:T(8,128)S(1)} %get-tuple-element.63.wet_ref, f32[16,128]{1,0:T(8,128)S(1)} %get-tuple-element.74.flag_ref), custom_call_target="tpu_custom_call" | custom-call | bytes 262144 | tf_op jit(solution)/shard_map/cond/branch_1_fun/pallas_call | solution.py:700
Async XLA Ops:
  1.2 1.4 %collective-permute-start.3 = (f32[6,8,2,128]{3,2,1,0:T(2,128)S(1)}, f32[6,8,2,128]{3,2,1,0:T(2,128)S(1)}, u32[]{:S(2)}, u32[]{:S(2)}) collective-permute-start(f32[6,8,2,128]{3,2,1,0:T(2,128)S(1)} %get-tuple-element.93), channel_id=1, source_target_pairs={{0,1},{1,0},{2,3},{3,2},{4,5},{5,4},{6,7},{7,6},{8,9},{9,8},{10,11... | collective-permute-start | bytes 147464 | tf_op jit(solution)/shard_map/ppermute | solution.py:831
  2.6 17.0 %copy-start = (bf16[1024,256]{1,0:T(8,128)(2,1)S(1)}, bf16[1024,256]{1,0:T(8,128)(2,1)}, u32[]{:S(2)}) copy-start(bf16[1024,256]{1,0:T(8,128)(2,1)} %get-tuple-element.71.basis_ref) | copy-start | bytes 1572868 | tf_op jit(solution)/shard_map/cond
  2.6 16.9 %copy-start.1 = (bf16[512,256]{1,0:T(8,128)(2,1)S(1)}, bf16[512,256]{1,0:T(8,128)(2,1)}, u32[]{:S(2)}) copy-start(bf16[512,256]{1,0:T(8,128)(2,1)} %get-tuple-element.72.joint_basis_ref) | copy-start | bytes 786436 | tf_op jit(solution)/shard_map/cond

commit v11 on v10

--- a/solution.py
+++ b/solution.py
@@ -13,6 +13,7 @@
 FBAND = 16
 MAXM = 64
 LANES = 128
+DEGREE = LANES // 2
 GROUP = 16
 
 
@@ -363,6 +364,11 @@
     return lax.dot_general(a, b, (dims, ((), ())), preferred_element_type=jnp.float32)
 
 
+def unpack(x):
+    left = lane_of(x.shape) < DEGREE
+    return jnp.concatenate([jnp.where(left, x, 0.0), jnp.where(left, 0.0, x)], axis=0)
+
+
 def pairs_of_rows(tiles, t, place):
     sub = lax.broadcasted_iota(jnp.int32, tiles[0].shape, 0) // 2
     for y in range(4):
@@ -432,6 +438,7 @@
     own_ref,
     closed_ref,
     table_ref,
+    sums_ref,
     out_ref,
     send_ref,
     field_ref,
@@ -439,6 +446,7 @@
     buf_ref,
     term_ref,
     raw_ref,
+    main_ref,
 ):
     levels, rows, lanes = thick_ref.shape
     full = rows + 8
@@ -492,6 +500,7 @@
         raw_ref[i, 2 : rows + 4] = both[: rows + 2]
         raw_ref[i, rows + 4 : full] = jnp.zeros((4, LANES), jnp.float32)
     main = 8 * levels
+    half = main // 2
     last = rows // 8 - 1
     for t in range(rows // 8):
         part = slice(8 * t, 8 * t + 8)
@@ -509,12 +518,20 @@
                 tiles.append(x)
 
             def place(y, tile, t=t, k=k):
-                send_ref[4 * t + y, 8 * k : 8 * k + 8] = tile
+                at = main * (4 * t + y) + 8 * k
+                main_ref[at : at + 8] = tile
 
             pairs_of_rows(tiles, t, place)
         for p in range(4 * t, 4 * t + 4):
             for i in range(3):
-                send_ref[p, main + 8 * i : main + 8 * i + 8] = raw_ref[i, 2 * p : 2 * p + 8]
+                send_ref[p, half + 8 * i : half + 8 * i + 8] = raw_ref[i, 2 * p : 2 * p + 8]
+    x = jnp.concatenate(split(main_ref[...]), axis=1)
+    x = product(x, jnp.concatenate([sums_ref[...]] * 2, axis=0), ((1,), (0,)))
+    x = x + roll(x, DEGREE, 1)
+    left = lane_of((half, LANES)) < DEGREE
+    for p in range(send_ref.shape[0]):
+        at = main * p
+        send_ref[p, :half] = jnp.where(left, x[at : at + half], x[at + half : at + main])
 
 
 def circle_kernel(
@@ -531,7 +548,8 @@
     peers = circle_ref.shape[0]
     modes = basis_ref.shape[1] // 2
     length = basis_ref.shape[0]
-    main = circle_ref.shape[1] - 24
+    half = circle_ref.shape[1] - 24
+    main = 2 * half
     levels = main // 8
     lanes = LANES
     lane = lane_of((8, LANES))
@@ -540,7 +558,7 @@
         part = slice(4 * j, 4 * j + 8)
         for i in range(3):
             x, y, z = (
-                circle_ref[(j + d) % peers, main + 8 * i : main + 8 * i + 8] for d in range(3)
+                circle_ref[(j + d) % peers, half + 8 * i : half + 8 * i + 8] for d in range(3)
             )
             for f, shift in ((2 * i, 0), (2 * i + 1, -8)):
                 middle = jnp.where(c < 12, roll(y, 4 + shift, 1), roll(z, 12 + shift, 1))
@@ -557,11 +575,10 @@
         joint_ref[8 * j : 8 * j + 8] = jnp.where(right, made, 0.0)
     lane_main = lane_of((main, LANES))
     row_main = lax.broadcasted_iota(jnp.int32, (main, LANES), 0)
-    inside = (lane_main >= 2) & (lane_main < lanes - 2)
     at_level = lane_main // GROUP == row_main // 8
 
     def block(o):
-        return jnp.where(inside, circle_ref[o, :main], 0.0)
+        return unpack(circle_ref[o, :half])
 
     def joint(j):
         x = joint_ref[8 * j : 8 * j + 8]
@@ -591,29 +608,40 @@
     for o in range(0, peers, 2):
         x = product(y, basis_ref[lanes * o : lanes * (o + 2)], ((1,), (1,)))
         x = x[:main] + x[main:]
-        out_ref[o, :main] = x[:, :lanes]
-        out_ref[o + 1, :main] = x[:, lanes:]
+        left = lane_of((half, LANES)) < DEGREE
+        out_ref[o, :half] = jnp.where(left, x[:half, :lanes], x[half:, :lanes])
+        out_ref[o + 1, :half] = jnp.where(left, x[:half, lanes:], x[half:, lanes:])
         before = (4 * o - 8) % (4 * peers)
         here = joint_ref[4 * o : 4 * o + 8]
-        out_ref[o, main:] = jnp.where(
+        out_ref[o, half:] = jnp.where(
             c < 8, roll(joint_ref[before : before + 8], -8, 1), roll(here, 8, 1)
         )
-        out_ref[o + 1, main:] = here
-
-
-def join_kernel(state_ref, piece_ref, wet_ref, flag_ref, out_ref, made_ref, sems):
+        out_ref[o + 1, half:] = here
+
+
+def join_kernel(
+    state_ref, piece_ref, wet_ref, flag_ref, columns_ref, out_ref, made_ref, smooth_ref, sems
+):
     levels, rows, lanes = wet_ref.shape
     main = 8 * levels
+    half = main // 2
     lane = lane_of((8, LANES))
+    x = jnp.concatenate(
+        [unpack(piece_ref[p, :half]) for p in range(piece_ref.shape[0])], axis=0
+    )
+    x = jnp.concatenate(split(x), axis=1)
+    x = product(x, jnp.concatenate([columns_ref[...]] * 2, axis=0), ((1,), (0,)))
+    smooth_ref[...] = x[:, :lanes] + x[:, lanes:]
     edges = [{} for _ in range(rows // 8)]
     for t, into in enumerate(edges):
-        tiles = [piece_ref[4 * t + x, main : main + 8] for x in range(4)]
+        tiles = [piece_ref[4 * t + x, half : half + 8] for x in range(4)]
         pairs_of_rows(tiles, t, into.__setitem__)
     copies = []
     for k in range(levels):
         for t in range(rows // 8):
             part = slice(8 * t, 8 * t + 8)
-            tiles = [piece_ref[4 * t + x, 8 * k : 8 * k + 8] for x in range(4)]
+            starts = [main * (4 * t + x) + 8 * k for x in range(4)]
+            tiles = [smooth_ref[at : at + 8] for at in starts]
             gate = flag_ref[part] * wet_ref[k, part]
 
             def place(f, smooth, k=k, gate=gate, part=part, edge=edges[t]):
@@ -726,6 +754,31 @@
     return np.concatenate([high, low], axis=1)
 
 
+def two_parts(x):
+    x = x.astype(np.float32)
+    high = x.astype(ml_dtypes.bfloat16)
+    return np.concatenate([high, (x - high.astype(np.float32)).astype(ml_dtypes.bfloat16)], axis=1)
+
+
+def polynomials(lanes):
+    x = (2.0 * np.arange(lanes) + 1.0 - lanes) / lanes
+    return np.cos(np.arange(DEGREE)[None, :] * np.arccos(x)[:, None])
+
+
+def block_coefficients(length, lanes, modes):
+    nodes = 4 * DEGREE
+    turn = (np.arange(nodes) + 0.5) * math.pi / nodes
+    at_nodes = np.cos(np.arange(DEGREE)[:, None] * turn[None, :])
+    at_nodes *= np.where(np.arange(DEGREE) == 0, 1.0, 2.0)[:, None] / nodes
+    parts = []
+    for block in range(length // lanes):
+        place = (np.cos(turn) * lanes + lanes - 1.0) / 2.0 + lanes * block
+        angle = np.arange(modes)[None, :] * place[:, None] * (2.0 * math.pi / length)
+        values = np.concatenate([np.cos(angle), np.sin(angle)], axis=1)
+        parts.append((at_nodes[:, :, None] * values[None]).sum(axis=1))
+    return np.stack(parts)
+
+
 def joint_basis(basis, lanes):
     length = basis.shape[0]
     tile, lane = np.divmod(np.arange(length // 2), lanes)
@@ -758,6 +811,7 @@
     edge_rows = (6, levels, 2, lanes)
 
     paired = rows == 2 * lon_peers and rows >= FBAND and lat_peers % 2 == 0 and levels % 2 == 0
+    paired = paired and math.pi * (MAXM - 1) * lanes / nlon <= DEGREE / 2.5
     *block, first, last, flags, counts, table, end_table, joint_table = call(
         functools.partial(load_kernel, paired),
         [ocean_state.shape, thickness.shape, thickness.shape, edge_rows, edge_rows]
@@ -792,33 +846,49 @@
 
     banded = (first_row < FBAND) | (first_row + rows > nlat - FBAND)
     modes = mode_basis(nlon, MAXM)
-    basis, at_joints = lax.optimization_barrier(
-        (jnp.asarray(modes), jnp.asarray(joint_basis(modes, lanes)))
-    )
+    tables = [modes]
+    if paired:
+        coefficients = block_coefficients(nlon, lanes, MAXM)
+        coefficients = np.concatenate([coefficients] * 2, axis=1).reshape(nlon, 2 * MAXM)
+        columns = polynomials(lanes)
+        inside = (np.arange(lanes) >= 2) & (np.arange(lanes) < lanes - 2)
+        tables = [
+            two_parts(coefficients),
+            joint_basis(modes, lanes),
+            two_parts(columns * inside[:, None]),
+            two_parts(np.concatenate([columns.T] * 2, axis=0)),
+        ]
+    tables = lax.optimization_barrier([jnp.asarray(table) for table in tables])
     lon_pos = lax.axis_index("lon")
 
     def circled(got, own, closed):
-        main = 8 * levels
+        half = 4 * levels
         tile = (levels, 8, lanes)
+        to_modes, at_joints, to_sums, to_columns = tables
         state, sent = call(
             end_kernel,
-            [ocean_state.shape, (lon_peers, main + 24, lanes)],
-            [(2,) + tile, (6,) + tile, (3, 4) + tile, (7,) + tile, (3, full, lanes)],
-        )(*block, got, own, closed, end_table)
+            [ocean_state.shape, (lon_peers, half + 24, lanes)],
+            [(2,) + tile, (6,) + tile, (3, 4) + tile, (7,) + tile, (3, full, lanes)]
+            + [(total, lanes)],
+        )(*block, got, own, closed, end_table, to_sums)
         circles = lax.all_to_all(sent, "lon", 0, 0, tiled=True)
         pieces = call(
             circle_kernel,
-            [(lon_peers, main + 8, lanes)],
+            [(lon_peers, half + 8, lanes)],
             [
                 (6, 4 * lon_peers, lanes),
                 (7, 4 * lon_peers, lanes),
                 (4 * lon_peers, lanes),
             ],
-        )(circles, joint_table, basis, at_joints, counts)[0]
+        )(circles, joint_table, to_modes, at_joints, counts)[0]
         pieces = lax.all_to_all(pieces, "lon", 0, 0, tiled=True)
         return call(
-            join_kernel, [ocean_state.shape], [ocean_state.shape], sems=levels // 2, sent=True
-        )(state, pieces, block[2], flags)[0]
+            join_kernel,
+            [ocean_state.shape],
+            [ocean_state.shape, (total, lanes)],
+            sems=levels // 2,
+            sent=True,
+        )(state, pieces, block[2], flags, to_columns)[0]
 
     def between(got, *_):
         pairs = [(i, i + 1) for i in range(1, lat_peers - 1, 2)]
@@ -854,7 +924,7 @@
         )
         smooth = call(
             filter_kernel, [circles.shape], [circles.shape], sems=lon_peers // 2, sent=True
-        )(circles, basis, mode_weights(row_counts, MAXM, nlon))[0]
+        )(circles, tables[0], mode_weights(row_counts, MAXM, nlon))[0]
         smooth = lax.all_to_all(smooth, "lon", 0, 0, tiled=True).reshape(state.shape)
         return call(blend_kernel, [state.shape], [state.shape], sems=4, sent=True)(
             state, smooth, block[2], flags

time: 33.1 us -> 31.8 us (0.961)
  blocking collectives: 27.8 us -> 25.3 us
  Pallas kernels: 4.43 us -> 5.53 us
    all_to_all x1, blocking collectives: 11.5 us -> 10.3 us  [circled(): pieces = lax.all_to_all(pieces, 'lon', 0, 0, tiled=True)]
    all_to_all x1, blocking collectives: 16.3 us -> 15.1 us  [circled(): circles = lax.all_to_all(sent, 'lon', 0, 0, tiled=True)]
    pallas_call x5, Pallas kernels: 4.43 us -> 5.53 us  [run(): pl.pallas_call(kernel, out_shape=shapes, in_specs=[away if raw else vmem]...]
where the time goes in v11:
time: 31.8 us; the launch traced here: 31.5 us
  blocking collectives  25.3 us (80%)
  Pallas kernels  5.53 us (17%)
  starting transfers between devices  0.52 us (2%)
    all_to_all x1, blocking collectives, circled(): circles = lax.all_to_all(sent, 'lon', 0, 0, tiled=True)  15.1 us
    all_to_all x1, blocking collectives, circled(): pieces = lax.all_to_all(pieces, 'lon', 0, 0, tiled=True)  10.3 us
    pallas_call x5, Pallas kernels, run(): pl.pallas_call(kernel, out_shape=shapes, in_specs=[away if raw else vmem]...  5.53 us
  transfers between devices with their start and end apart: 1, of which 0 were waited for; matrix products, arithmetic and copies ran while one was open for 0% of the time, Pallas kernels for 3%

profile of v11, /device:TPU:0, one launch (start us, length us, event | category | flops | bytes accessed | tf_op | source)
XLA Modules:
  0.0 31.5 jit_solution(1078775505875861624)
XLA Ops:
  0.0 1.2 %shard_map.93 = (f32[4,8,16,128]{3,2,1,0:T(8,128)S(1)}, f32[8,16,128]{2,1,0:T(8,128)S(1)}, f32[8,16,128]{2,1,0:T(8,128)S(1)}, f32[6,8,2,128]{3,2,1,0:T(2,128)S(1...) custom-call(f32[4,8,16,128]{3,2,1,0:T(8,128)} %state_any.1, ...), custom_call_target="tpu_custom_call" | custom-call | bytes 548864 | tf_op jit(solution)/shard_map/pallas_call | solution.py:728
  1.2 0.5 %collective-permute-start.3 = (f32[6,8,2,128]{3,2,1,0:T(2,128)S(1)}, f32[6,8,2,128]{3,2,1,0:T(2,128)S(1)}, u32[]{:S(2)}, u32[]{:S(2)}) collective-permute-start(f32[6,8,2,128]{3,2,1,0:T(2,128)S(1)} %get-tuple-element.101), channel_id=1, source_target_pairs={{0,1},{1,0},{2,3},{3,2},{4,5},{5,4},{6,7},{7,6},{8,9},{9,8},{10,11... | collective-permute-start | bytes 147464 | tf_op jit(solution)/shard_map/ppermute | solution.py:901
  1.7 0.9 %shard_map.94 = (f32[6,16,128]{2,1,0:T(8,128)S(1)}, f32[3,4,8,16,128]{4,3,2,1,0:T(8,128)S(1)}) custom-call(f32[4,8,16,128]{3,2,1,0:T(8,128)S(1)} %get-tuple-element.102.state_ref, f32[8,16,128]{2,1,0:T(8,128)S(1)} %get-tuple-element.103.thick_ref, f32[8,16,128]{2,1,0:T(8,128)S(1)} %get-tuple-element.104.wet_ref, f32[2,24,128]{2,1,0:T(8,128)S(1)} %get-tuple-element.105.table_ref), custom_call_target="tpu_custom_call" | custom-call | flops 5898240 | bytes 835584 | tf_op jit(solution)/shard_map/pallas_call | solution.py:728
  2.6 0.0 collective-permute-done.3
  2.6 28.9 %conditional.1 = (f32[4,8,16,128]{3,2,1,0:T(8,128)}) conditional(s32[]{:T(128)} %convert_element_type.3, (s32[]{:T(128)}, f32[6,8,2,128]{3,2,1,0:T(2,128)S(1)}, f32[6,8,2,128]{3,2,1,0:T(2,128)S(1)}, f32[4,8,16,128]{3,2,1,0:T(8,128)S(1)}, f32[8,16,128]{2,1,0:T(8,128)S(1)}, /*index=5*/f32[8,16,128]{2,1,0:T(8,128)S(1)}, ...), branch_computations={%region_0.1_spmd, %region_1.2_spmd} | conditional | flops 7888908 | bytes 5111900 | solution.py:909
  2.6 0.0 copy-start
  2.6 0.0 copy-start.1
  2.6 1.6 %branch_1_fun.3 = (f32[4,8,16,128]{3,2,1,0:T(8,128)S(1)}, f32[8,56,128]{2,1,0:T(8,128)S(1)}) custom-call(f32[4,8,16,128]{3,2,1,0:T(8,128)S(1)} %get-tuple-element.65.state_ref, f32[8,16,128]{2,1,0:T(8,128)S(1)} %get-tuple-element.66.thick_ref, f32[8,16,128]{2,1,0:T(8,128)S(1)} %get-tuple-element.67.wet_ref, f32[6,8,2,128]{3,2,1,0:T(2,128)S(1)} %get-tuple-element.68.got_ref, ...), custom_call_target="tpu_custom_call" | custom-call | bytes 491520 | tf_op jit(solution)/shard_map/cond/branch_1_fun/pallas_call | solution.py:728
  4.2 0.0 copy-start.2
  4.3 15.1 %all_to_all.8.circle_ref = f32[8,56,128]{2,1,0:T(8,128)S(1)} all-to-all(f32[8,56,128]{2,1,0:T(8,128)S(1)} %get-tuple-element.74), channel_id=1, replica_groups=mesh['lon'=8,'lat'=4] {'lon'}, dimensions={0} | all-to-all | bytes 458752 | tf_op jit(solution)/shard_map/cond/branch_1_fun/all_to_all | solution.py:874
  19.3 0.0 copy-done
  19.3 0.0 copy-done.1
  19.3 0.9 %branch_1_fun.4 = f32[8,40,128]{2,1,0:T(8,128)S(1)} custom-call(f32[8,56,128]{2,1,0:T(8,128)S(1)} %all_to_all.8.circle_ref, f32[2,8,128]{2,1,0:T(8,128)S(1)} %get-tuple-element.75.table_ref, bf16[1024,256]{1,0:T(8,128)(2,1)S(1)} %copy-done, bf16[512,256]{1,0:T(8,128)(2,1)S(1)} %copy-done.1, f32[16,128]{1,0:T(8,128)S(1)} %get-tuple-element.78.count_ref), custom_call_target="tpu_custom_call" | custom-call | bytes 163840 | tf_op jit(solution)/shard_map/cond/branch_1_fun/pallas_call | solution.py:728
  20.3 10.3 %all_to_all.9.piece_ref = f32[8,40,128]{2,1,0:T(8,128)S(1)} all-to-all(f32[8,40,128]{2,1,0:T(8,128)S(1)} %branch_1_fun.4), channel_id=1, replica_groups=mesh['lon'=8,'lat'=4] {'lon'}, dimensions={0} | all-to-all | bytes 327680 | tf_op jit(solution)/shard_map/cond/branch_1_fun/all_to_all | solution.py:884
  30.5 0.0 copy-done.2
  30.5 1.0 %branch_1_fun.5 = f32[4,8,16,128]{3,2,1,0:T(8,128)} custom-call(f32[4,8,16,128]{3,2,1,0:T(8,128)S(1)} %get-tuple-element.73.state_ref, f32[8,40,128]{2,1,0:T(8,128)S(1)} %all_to_all.9.piece_ref, f32[8,16,128]{2,1,0:T(8,128)S(1)} %get-tuple-element.67.wet_ref, f32[16,128]{1,0:T(8,128)S(1)} %get-tuple-element.79.flag_ref, bf16[128,256]{1,0:T(8,128)(2,1)S(1)} %copy-done.2), custom_call_target="tpu_custom_call" | custom-call | bytes 262144 | tf_op jit(solution)/shard_map/cond/branch_1_fun/pallas_call | solution.py:728
Async XLA Ops:
  1.2 1.4 %collective-permute-start.3 = (f32[6,8,2,128]{3,2,1,0:T(2,128)S(1)}, f32[6,8,2,128]{3,2,1,0:T(2,128)S(1)}, u32[]{:S(2)}, u32[]{:S(2)}) collective-permute-start(f32[6,8,2,128]{3,2,1,0:T(2,128)S(1)} %get-tuple-element.101), channel_id=1, source_target_pairs={{0,1},{1,0},{2,3},{3,2},{4,5},{5,4},{6,7},{7,6},{8,9},{9,8},{10,11... | collective-permute-start | bytes 147464 | tf_op jit(solution)/shard_map/ppermute | solution.py:901
  2.6 16.8 %copy-start = (bf16[1024,256]{1,0:T(8,128)(2,1)S(1)}, bf16[1024,256]{1,0:T(8,128)(2,1)}, u32[]{:S(2)}) copy-start(bf16[1024,256]{1,0:T(8,128)(2,1)} %get-tuple-element.76.basis_ref) | copy-start | bytes 1572868 | tf_op jit(solution)/shard_map/cond
  2.6 16.7 %copy-start.1 = (bf16[512,256]{1,0:T(8,128)(2,1)S(1)}, bf16[512,256]{1,0:T(8,128)(2,1)}, u32[]{:S(2)}) copy-start(bf16[512,256]{1,0:T(8,128)(2,1)} %get-tuple-element.77.joint_basis_ref) | copy-start | bytes 786436 | tf_op jit(solution)/shard_map/cond
  4.2 26.3 %copy-start.2 = (bf16[128,256]{1,0:T(8,128)(2,1)S(1)}, bf16[128,256]{1,0:T(8,128)(2,1)}, u32[]{:S(2)}) copy-start(bf16[128,256]{1,0:T(8,128)(2,1)} %get-tuple-element.80.columns_ref) | copy-start | bytes 196612 | tf_op jit(solution)/shard_map/cond

commit v12 on v11

--- a/solution.py
+++ b/solution.py
@@ -119,6 +119,7 @@
     wet_any,
     flag_any,
     count_any,
+    sums_any,
     state_ref,
     thick_ref,
     wet_ref,
@@ -129,6 +130,7 @@
     table_ref,
     end_table_ref,
     joint_table_ref,
+    sums_ref,
     raw_ref,
     raw_flag_ref,
     raw_count_ref,
@@ -136,7 +138,7 @@
 ):
     levels, rows = thick_ref.shape[:2]
     moves = [(flag_any, raw_flag_ref), (count_any, raw_count_ref), (wet_any, raw_ref)]
-    moves += [(thick_any, thick_ref)]
+    moves += [(thick_any, thick_ref), (sums_any, sums_ref)]
     moves += [(state_any.at[f], state_ref.at[f]) for f in range(4)]
     copies = [pltpu.make_async_copy(*pair, sems.at[i]) for i, pair in enumerate(moves)]
     for copy in copies:
@@ -711,7 +713,7 @@
     vmem = pl.BlockSpec(memory_space=pltpu.VMEM)
     away = pl.BlockSpec(memory_space=pl.ANY)
     specs = [vmem] * len(outs)
-    shapes = [jax.ShapeDtypeStruct(s, jnp.float32) for s in outs]
+    shapes = [jax.ShapeDtypeStruct(s, jnp.float32) if isinstance(s, tuple) else s for s in outs]
     if sent:
         specs[-1] = away
         shapes[-1] = pltpu.HBM(outs[-1], jnp.float32)
@@ -719,7 +721,9 @@
     if sems:
         buffers.append(pltpu.SemaphoreType.DMA((sems,)))
     cost = pl.CostEstimate(
-        flops=flops, transcendentals=0, bytes_accessed=4 * sum(map(math.prod, outs))
+        flops=flops,
+        transcendentals=0,
+        bytes_accessed=4 * sum(math.prod(s.shape) for s in shapes),
     )
 
     def run(*args):
@@ -812,15 +816,19 @@
 
     paired = rows == 2 * lon_peers and rows >= FBAND and lat_peers % 2 == 0 and levels % 2 == 0
     paired = paired and math.pi * (MAXM - 1) * lanes / nlon <= DEGREE / 2.5
-    *block, first, last, flags, counts, table, end_table, joint_table = call(
+    columns = polynomials(lanes)
+    inside = (np.arange(lanes) >= 2) & (np.arange(lanes) < lanes - 2)
+    sums = jnp.asarray(two_parts(columns * inside[:, None]))
+    *block, first, last, flags, counts, table, end_table, joint_table, to_sums = call(
         functools.partial(load_kernel, paired),
         [ocean_state.shape, thickness.shape, thickness.shape, edge_rows, edge_rows]
         + [(rows, lanes)] * 2
-        + [(2, full, lanes), (2, 8, lanes), (2, 8, lanes)],
+        + [(2, full, lanes), (2, 8, lanes), (2, 8, lanes)]
+        + [jax.ShapeDtypeStruct(sums.shape, sums.dtype)],
         [pltpu.VMEM(shape, jnp.int32) for shape in (thickness.shape, (1, rows), (1, rows))],
-        sems=8,
+        sems=9,
         raw=True,
-    )(ocean_state, thickness, wet_mask, row_flags[None], mode_counts[None])
+    )(ocean_state, thickness, wet_mask, row_flags[None], mode_counts[None], sums)
 
     def ready():
         return call(
@@ -850,12 +858,9 @@
     if paired:
         coefficients = block_coefficients(nlon, lanes, MAXM)
         coefficients = np.concatenate([coefficients] * 2, axis=1).reshape(nlon, 2 * MAXM)
-        columns = polynomials(lanes)
-        inside = (np.arange(lanes) >= 2) & (np.arange(lanes) < lanes - 2)
         tables = [
             two_parts(coefficients),
             joint_basis(modes, lanes),
-            two_parts(columns * inside[:, None]),
             two_parts(np.concatenate([columns.T] * 2, axis=0)),
         ]
     tables = lax.optimization_barrier([jnp.asarray(table) for table in tables])
@@ -864,7 +869,7 @@
     def circled(got, own, closed):
         half = 4 * levels
         tile = (levels, 8, lanes)
-        to_modes, at_joints, to_sums, to_columns = tables
+        to_modes, at_joints, to_columns = tables
         state, sent = call(
             end_kernel,
             [ocean_state.shape, (lon_peers, half + 24, lanes)],

time: 31.8 us -> 30.8 us (0.969)
  Pallas kernels: 5.53 us -> 4.74 us
    pallas_call x5, Pallas kernels: 5.53 us -> 4.74 us  [run(): pl.pallas_call(kernel, out_shape=shapes, in_specs=[away if raw else vmem]...]
where the time goes in v12:
time: 30.8 us; the launch traced here: 30.6 us
  blocking collectives  25.2 us (82%)
  Pallas kernels  4.74 us (15%)
  starting transfers between devices  0.52 us (2%)
    all_to_all x1, blocking collectives, circled(): circles = lax.all_to_all(sent, 'lon', 0, 0, tiled=True)  15.1 us
    all_to_all x1, blocking collectives, circled(): pieces = lax.all_to_all(pieces, 'lon', 0, 0, tiled=True)  10.1 us
    pallas_call x5, Pallas kernels, run(): pl.pallas_call(kernel, out_shape=shapes, in_specs=[away if raw else vmem]...  4.74 us
  transfers between devices with their start and end apart: 1, of which 0 were waited for; matrix products, arithmetic and copies ran while one was open for 0% of the time, Pallas kernels for 3%

profile of v12, /device:TPU:0, one launch (start us, length us, event | category | flops | bytes accessed | tf_op | source)
XLA Modules:
  0.0 30.6 jit_solution(11019835485121037330)
XLA Ops:
  0.0 1.2 %shard_map.93 = (f32[4,8,16,128]{3,2,1,0:T(8,128)S(1)}, f32[8,16,128]{2,1,0:T(8,128)S(1)}, f32[8,16,128]{2,1,0:T(8,128)S(1)}, f32[6,8,2,128]{3,2,1,0:T(2,128)S(1...) custom-call(f32[4,8,16,128]{3,2,1,0:T(8,128)} %state_any.1, ...), custom_call_target="tpu_custom_call" | custom-call | bytes 614400 | tf_op jit(solution)/shard_map/pallas_call | solution.py:732
  1.2 0.5 %collective-permute-start.3 = (f32[6,8,2,128]{3,2,1,0:T(2,128)S(1)}, f32[6,8,2,128]{3,2,1,0:T(2,128)S(1)}, u32[]{:S(2)}, u32[]{:S(2)}) collective-permute-start(f32[6,8,2,128]{3,2,1,0:T(2,128)S(1)} %get-tuple-element.101), channel_id=1, source_target_pairs={{0,1},{1,0},{2,3},{3,2},{4,5},{5,4},{6,7},{7,6},{8,9},{9,8},{10,11... | collective-permute-start | bytes 147464 | tf_op jit(solution)/shard_map/ppermute | solution.py:906
  1.7 0.9 %shard_map.94 = (f32[6,16,128]{2,1,0:T(8,128)S(1)}, f32[3,4,8,16,128]{4,3,2,1,0:T(8,128)S(1)}) custom-call(f32[4,8,16,128]{3,2,1,0:T(8,128)S(1)} %get-tuple-element.102.state_ref, f32[8,16,128]{2,1,0:T(8,128)S(1)} %get-tuple-element.103.thick_ref, f32[8,16,128]{2,1,0:T(8,128)S(1)} %get-tuple-element.104.wet_ref, f32[2,24,128]{2,1,0:T(8,128)S(1)} %get-tuple-element.105.table_ref), custom_call_target="tpu_custom_call" | custom-call | flops 5898240 | bytes 835584 | tf_op jit(solution)/shard_map/pallas_call | solution.py:732
  2.6 0.0 collective-permute-done.3
  2.6 28.0 %conditional.1 = (f32[4,8,16,128]{3,2,1,0:T(8,128)}) conditional(s32[]{:T(128)} %convert_element_type.3, (s32[]{:T(128)}, f32[6,8,2,128]{3,2,1,0:T(2,128)S(1)}, f32[6,8,2,128]{3,2,1,0:T(2,128)S(1)}, f32[4,8,16,128]{3,2,1,0:T(8,128)S(1)}, f32[8,16,128]{2,1,0:T(8,128)S(1)}, /*index=5*/f32[8,16,128]{2,1,0:T(8,128)S(1)}, ...), branch_computations={%region_0.1_spmd, %region_1.2_spmd} | conditional | flops 7888908 | bytes 5111900 | solution.py:914
  2.6 0.0 copy-start
  2.6 0.0 copy-start.1
  2.6 0.8 %branch_1_fun.3 = (f32[4,8,16,128]{3,2,1,0:T(8,128)S(1)}, f32[8,56,128]{2,1,0:T(8,128)S(1)}) custom-call(f32[4,8,16,128]{3,2,1,0:T(8,128)S(1)} %get-tuple-element.65.state_ref, f32[8,16,128]{2,1,0:T(8,128)S(1)} %get-tuple-element.66.thick_ref, f32[8,16,128]{2,1,0:T(8,128)S(1)} %get-tuple-element.67.wet_ref, f32[6,8,2,128]{3,2,1,0:T(2,128)S(1)} %get-tuple-element.68.got_ref, ...), custom_call_target="tpu_custom_call" | custom-call | bytes 491520 | tf_op jit(solution)/shard_map/cond/branch_1_fun/pallas_call | solution.py:732
  3.4 0.0 copy-start.2
  3.5 15.1 %all_to_all.8.circle_ref = f32[8,56,128]{2,1,0:T(8,128)S(1)} all-to-all(f32[8,56,128]{2,1,0:T(8,128)S(1)} %get-tuple-element.74), channel_id=1, replica_groups=mesh['lon'=8,'lat'=4] {'lon'}, dimensions={0} | all-to-all | bytes 458752 | tf_op jit(solution)/shard_map/cond/branch_1_fun/all_to_all | solution.py:879
  18.5 0.0 copy-done
  18.5 0.0 copy-done.1
  18.5 0.9 %branch_1_fun.4 = f32[8,40,128]{2,1,0:T(8,128)S(1)} custom-call(f32[8,56,128]{2,1,0:T(8,128)S(1)} %all_to_all.8.circle_ref, f32[2,8,128]{2,1,0:T(8,128)S(1)} %get-tuple-element.75.table_ref, bf16[1024,256]{1,0:T(8,128)(2,1)S(1)} %copy-done, bf16[512,256]{1,0:T(8,128)(2,1)S(1)} %copy-done.1, f32[16,128]{1,0:T(8,128)S(1)} %get-tuple-element.78.count_ref), custom_call_target="tpu_custom_call" | custom-call | bytes 163840 | tf_op jit(solution)/shard_map/cond/branch_1_fun/pallas_call | solution.py:732
  19.5 10.1 %all_to_all.9.piece_ref = f32[8,40,128]{2,1,0:T(8,128)S(1)} all-to-all(f32[8,40,128]{2,1,0:T(8,128)S(1)} %branch_1_fun.4), channel_id=1, replica_groups=mesh['lon'=8,'lat'=4] {'lon'}, dimensions={0} | all-to-all | bytes 327680 | tf_op jit(solution)/shard_map/cond/branch_1_fun/all_to_all | solution.py:889
  29.6 0.0 copy-done.2
  29.6 1.0 %branch_1_fun.5 = f32[4,8,16,128]{3,2,1,0:T(8,128)} custom-call(f32[4,8,16,128]{3,2,1,0:T(8,128)S(1)} %get-tuple-element.73.state_ref, f32[8,40,128]{2,1,0:T(8,128)S(1)} %all_to_all.9.piece_ref, f32[8,16,128]{2,1,0:T(8,128)S(1)} %get-tuple-element.67.wet_ref, f32[16,128]{1,0:T(8,128)S(1)} %get-tuple-element.79.flag_ref, bf16[128,256]{1,0:T(8,128)(2,1)S(1)} %copy-done.2), custom_call_target="tpu_custom_call" | custom-call | bytes 262144 | tf_op jit(solution)/shard_map/cond/branch_1_fun/pallas_call | solution.py:732
Async XLA Ops:
  1.2 1.4 %collective-permute-start.3 = (f32[6,8,2,128]{3,2,1,0:T(2,128)S(1)}, f32[6,8,2,128]{3,2,1,0:T(2,128)S(1)}, u32[]{:S(2)}, u32[]{:S(2)}) collective-permute-start(f32[6,8,2,128]{3,2,1,0:T(2,128)S(1)} %get-tuple-element.101), channel_id=1, source_target_pairs={{0,1},{1,0},{2,3},{3,2},{4,5},{5,4},{6,7},{7,6},{8,9},{9,8},{10,11... | collective-permute-start | bytes 147464 | tf_op jit(solution)/shard_map/ppermute | solution.py:906
  2.6 15.9 %copy-start = (bf16[1024,256]{1,0:T(8,128)(2,1)S(1)}, bf16[1024,256]{1,0:T(8,128)(2,1)}, u32[]{:S(2)}) copy-start(bf16[1024,256]{1,0:T(8,128)(2,1)} %get-tuple-element.76.basis_ref) | copy-start | bytes 1572868 | tf_op jit(solution)/shard_map/cond
  2.6 15.9 %copy-start.1 = (bf16[512,256]{1,0:T(8,128)(2,1)S(1)}, bf16[512,256]{1,0:T(8,128)(2,1)}, u32[]{:S(2)}) copy-start(bf16[512,256]{1,0:T(8,128)(2,1)} %get-tuple-element.77.joint_basis_ref) | copy-start | bytes 786436 | tf_op jit(solution)/shard_map/cond
  3.4 26.1 %copy-start.2 = (bf16[128,256]{1,0:T(8,128)(2,1)S(1)}, bf16[128,256]{1,0:T(8,128)(2,1)}, u32[]{:S(2)}) copy-start(bf16[128,256]{1,0:T(8,128)(2,1)} %get-tuple-element.80.columns_ref) | copy-start | bytes 196612 | tf_op jit(solution)/shard_map/cond

commit v13 on v12

--- a/solution.py
+++ b/solution.py
@@ -13,7 +13,8 @@
 FBAND = 16
 MAXM = 64
 LANES = 128
-DEGREE = LANES // 2
+SUMS = 32
+PACKED = LANES // SUMS
 GROUP = 16
 
 
@@ -367,8 +368,17 @@
 
 
 def unpack(x):
-    left = lane_of(x.shape) < DEGREE
-    return jnp.concatenate([jnp.where(left, x, 0.0), jnp.where(left, 0.0, x)], axis=0)
+    part = lane_of(x.shape) // SUMS
+    return jnp.concatenate([jnp.where(part == g, x, 0.0) for g in range(PACKED)], axis=0)
+
+
+def pack(x):
+    size = x.shape[0] // PACKED
+    made = x[:size]
+    part = lane_of(made.shape) // SUMS
+    for g in range(1, PACKED):
+        made = jnp.where(part == g, x[size * g : size * (g + 1)], made)
+    return made
 
 
 def pairs_of_rows(tiles, t, place):
@@ -502,7 +512,7 @@
         raw_ref[i, 2 : rows + 4] = both[: rows + 2]
         raw_ref[i, rows + 4 : full] = jnp.zeros((4, LANES), jnp.float32)
     main = 8 * levels
-    half = main // 2
+    few = main // PACKED
     last = rows // 8 - 1
     for t in range(rows // 8):
         part = slice(8 * t, 8 * t + 8)
@@ -526,14 +536,12 @@
             pairs_of_rows(tiles, t, place)
         for p in range(4 * t, 4 * t + 4):
             for i in range(3):
-                send_ref[p, half + 8 * i : half + 8 * i + 8] = raw_ref[i, 2 * p : 2 * p + 8]
+                send_ref[p, few + 8 * i : few + 8 * i + 8] = raw_ref[i, 2 * p : 2 * p + 8]
     x = jnp.concatenate(split(main_ref[...]), axis=1)
     x = product(x, jnp.concatenate([sums_ref[...]] * 2, axis=0), ((1,), (0,)))
-    x = x + roll(x, DEGREE, 1)
-    left = lane_of((half, LANES)) < DEGREE
+    x = x + roll(x, SUMS, 1)
     for p in range(send_ref.shape[0]):
-        at = main * p
-        send_ref[p, :half] = jnp.where(left, x[at : at + half], x[at + half : at + main])
+        send_ref[p, :few] = pack(x[main * p : main * (p + 1)])
 
 
 def circle_kernel(
@@ -550,8 +558,8 @@
     peers = circle_ref.shape[0]
     modes = basis_ref.shape[1] // 2
     length = basis_ref.shape[0]
-    half = circle_ref.shape[1] - 24
-    main = 2 * half
+    few = circle_ref.shape[1] - 24
+    main = PACKED * few
     levels = main // 8
     lanes = LANES
     lane = lane_of((8, LANES))
@@ -560,7 +568,7 @@
         part = slice(4 * j, 4 * j + 8)
         for i in range(3):
             x, y, z = (
-                circle_ref[(j + d) % peers, half + 8 * i : half + 8 * i + 8] for d in range(3)
+                circle_ref[(j + d) % peers, few + 8 * i : few + 8 * i + 8] for d in range(3)
             )
             for f, shift in ((2 * i, 0), (2 * i + 1, -8)):
                 middle = jnp.where(c < 12, roll(y, 4 + shift, 1), roll(z, 12 + shift, 1))
@@ -580,7 +588,7 @@
     at_level = lane_main // GROUP == row_main // 8
 
     def block(o):
-        return unpack(circle_ref[o, :half])
+        return unpack(circle_ref[o, :few])
 
     def joint(j):
         x = joint_ref[8 * j : 8 * j + 8]
@@ -610,15 +618,14 @@
     for o in range(0, peers, 2):
         x = product(y, basis_ref[lanes * o : lanes * (o + 2)], ((1,), (1,)))
         x = x[:main] + x[main:]
-        left = lane_of((half, LANES)) < DEGREE
-        out_ref[o, :half] = jnp.where(left, x[:half, :lanes], x[half:, :lanes])
-        out_ref[o + 1, :half] = jnp.where(left, x[:half, lanes:], x[half:, lanes:])
+        out_ref[o, :few] = pack(x[:, :lanes])
+        out_ref[o + 1, :few] = pack(x[:, lanes:])
         before = (4 * o - 8) % (4 * peers)
         here = joint_ref[4 * o : 4 * o + 8]
-        out_ref[o, half:] = jnp.where(
+        out_ref[o, few:] = jnp.where(
             c < 8, roll(joint_ref[before : before + 8], -8, 1), roll(here, 8, 1)
         )
-        out_ref[o + 1, half:] = here
+        out_ref[o + 1, few:] = here
 
 
 def join_kernel(
@@ -626,17 +633,17 @@
 ):
     levels, rows, lanes = wet_ref.shape
     main = 8 * levels
-    half = main // 2
+    few = main // PACKED
     lane = lane_of((8, LANES))
     x = jnp.concatenate(
-        [unpack(piece_ref[p, :half]) for p in range(piece_ref.shape[0])], axis=0
+        [unpack(piece_ref[p, :few]) for p in range(piece_ref.shape[0])], axis=0
     )
     x = jnp.concatenate(split(x), axis=1)
     x = product(x, jnp.concatenate([columns_ref[...]] * 2, axis=0), ((1,), (0,)))
     smooth_ref[...] = x[:, :lanes] + x[:, lanes:]
     edges = [{} for _ in range(rows // 8)]
     for t, into in enumerate(edges):
-        tiles = [piece_ref[4 * t + x, half : half + 8] for x in range(4)]
+        tiles = [piece_ref[4 * t + x, few : few + 8] for x in range(4)]
         pairs_of_rows(tiles, t, into.__setitem__)
     copies = []
     for k in range(levels):
@@ -764,23 +771,28 @@
     return np.concatenate([high, (x - high.astype(np.float32)).astype(ml_dtypes.bfloat16)], axis=1)
 
 
-def polynomials(lanes):
-    x = (2.0 * np.arange(lanes) + 1.0 - lanes) / lanes
-    return np.cos(np.arange(DEGREE)[None, :] * np.arccos(x)[:, None])
-
-
-def block_coefficients(length, lanes, modes):
-    nodes = 4 * DEGREE
-    turn = (np.arange(nodes) + 0.5) * math.pi / nodes
-    at_nodes = np.cos(np.arange(DEGREE)[:, None] * turn[None, :])
-    at_nodes *= np.where(np.arange(DEGREE) == 0, 1.0, 2.0)[:, None] / nodes
-    parts = []
-    for block in range(length // lanes):
-        place = (np.cos(turn) * lanes + lanes - 1.0) / 2.0 + lanes * block
-        angle = np.arange(modes)[None, :] * place[:, None] * (2.0 * math.pi / length)
-        values = np.concatenate([np.cos(angle), np.sin(angle)], axis=1)
-        parts.append((at_nodes[:, :, None] * values[None]).sum(axis=1))
-    return np.stack(parts)
+def on_grid(x):
+    return np.round(x * 2.0**32) / 2.0**32
+
+
+def sequences(length, lanes, modes):
+    at = np.arange(lanes)
+    band = 2.0 * math.pi * (modes - 0.5) / length
+    along = ((lanes - 1 - 2.0 * at) / 2.0) ** 2 * math.cos(band)
+    beside = at[1:] * (lanes - at[1:]) / 2.0
+    matrix = np.diag(along) + np.diag(beside, 1) + np.diag(beside, -1)
+    most = np.linalg.eigh(matrix)[1][:, ::-1][:, :SUMS]
+    order = np.where(np.arange(SUMS)[None, :] % 2 == 0, 1.0, at[:, None] - (lanes - 1) / 2.0)
+    return on_grid(most * np.sign((most * order).sum(axis=0))[None, :])
+
+
+def block_coefficients(length, lanes, modes, columns):
+    turns = np.arange(modes)[None, :] * np.arange(length)[:, None] % length
+    angle = turns * (2.0 * math.pi / length)
+    wave = np.concatenate([np.cos(angle), np.sin(angle)], axis=1).reshape(-1, lanes, 2 * modes)
+    made = on_grid(np.einsum("in,oim->onm", columns, wave, optimize=False))
+    rest = wave - np.einsum("in,onm->oim", columns, made, optimize=False)
+    return made, np.abs(rest).max()
 
 
 def joint_basis(basis, lanes):
@@ -815,10 +827,12 @@
     edge_rows = (6, levels, 2, lanes)
 
     paired = rows == 2 * lon_peers and rows >= FBAND and lat_peers % 2 == 0 and levels % 2 == 0
-    paired = paired and math.pi * (MAXM - 1) * lanes / nlon <= DEGREE / 2.5
-    columns = polynomials(lanes)
+    columns = sequences(nlon, lanes, MAXM)
+    if paired:
+        coefficients, rest = block_coefficients(nlon, lanes, MAXM, columns)
+        paired = bool(rest < 1e-8)
     inside = (np.arange(lanes) >= 2) & (np.arange(lanes) < lanes - 2)
-    sums = jnp.asarray(two_parts(columns * inside[:, None]))
+    sums = jnp.asarray(np.tile(two_parts(columns * inside[:, None]), (1, PACKED // 2)))
     *block, first, last, flags, counts, table, end_table, joint_table, to_sums = call(
         functools.partial(load_kernel, paired),
         [ocean_state.shape, thickness.shape, thickness.shape, edge_rows, edge_rows]
@@ -856,30 +870,29 @@
     modes = mode_basis(nlon, MAXM)
     tables = [modes]
     if paired:
-        coefficients = block_coefficients(nlon, lanes, MAXM)
-        coefficients = np.concatenate([coefficients] * 2, axis=1).reshape(nlon, 2 * MAXM)
+        coefficients = np.concatenate([coefficients] * PACKED, axis=1).reshape(nlon, 2 * MAXM)
         tables = [
             two_parts(coefficients),
             joint_basis(modes, lanes),
-            two_parts(np.concatenate([columns.T] * 2, axis=0)),
+            two_parts(np.concatenate([columns.T] * PACKED, axis=0)),
         ]
     tables = lax.optimization_barrier([jnp.asarray(table) for table in tables])
     lon_pos = lax.axis_index("lon")
 
     def circled(got, own, closed):
-        half = 4 * levels
+        few = 8 * levels // PACKED
         tile = (levels, 8, lanes)
         to_modes, at_joints, to_columns = tables
         state, sent = call(
             end_kernel,
-            [ocean_state.shape, (lon_peers, half + 24, lanes)],
+            [ocean_state.shape, (lon_peers, few + 24, lanes)],
             [(2,) + tile, (6,) + tile, (3, 4) + tile, (7,) + tile, (3, full, lanes)]
             + [(total, lanes)],
         )(*block, got, own, closed, end_table, to_sums)
         circles = lax.all_to_all(sent, "lon", 0, 0, tiled=True)
         pieces = call(
             circle_kernel,
-            [(lon_peers, half + 8, lanes)],
+            [(lon_peers, few + 8, lanes)],
             [
                 (6, 4 * lon_peers, lanes),
                 (7, 4 * lon_peers, lanes),

time: 30.8 us -> 29.7 us (0.964)
  blocking collectives: 25.2 us -> 24.1 us
    all_to_all x1, blocking collectives: 10.1 us -> 9.51 us  [circled(): pieces = lax.all_to_all(pieces, 'lon', 0, 0, tiled=True)]
    all_to_all x1, blocking collectives: 15.1 us -> 14.6 us  [circled(): circles = lax.all_to_all(sent, 'lon', 0, 0, tiled=True)]
where the time goes in v13:
time: 29.7 us; the launch traced here: 29.5 us
  blocking collectives  24.1 us (81%)
  Pallas kernels  4.73 us (16%)
  starting transfers between devices  0.52 us (2%)
    all_to_all x1, blocking collectives, circled(): circles = lax.all_to_all(sent, 'lon', 0, 0, tiled=True)  14.6 us
    all_to_all x1, blocking collectives, circled(): pieces = lax.all_to_all(pieces, 'lon', 0, 0, tiled=True)  9.51 us
    pallas_call x5, Pallas kernels, run(): pl.pallas_call(kernel, out_shape=shapes, in_specs=[away if raw else vmem]...  4.73 us
  transfers between devices with their start and end apart: 1, of which 0 were waited for; matrix products, arithmetic and copies ran while one was open for 0% of the time, Pallas kernels for 3%

profile of v13, /device:TPU:0, one launch (start us, length us, event | category | flops | bytes accessed | tf_op | source)
XLA Modules:
  0.0 29.5 jit_solution(7933150602148316348)
XLA Ops:
  0.0 1.2 %shard_map.93 = (f32[4,8,16,128]{3,2,1,0:T(8,128)S(1)}, f32[8,16,128]{2,1,0:T(8,128)S(1)}, f32[8,16,128]{2,1,0:T(8,128)S(1)}, f32[6,8,2,128]{3,2,1,0:T(2,128)S(1...) custom-call(f32[4,8,16,128]{3,2,1,0:T(8,128)} %state_any.1, ...), custom_call_target="tpu_custom_call" | custom-call | bytes 614400 | tf_op jit(solution)/shard_map/pallas_call | solution.py:739
  1.2 0.5 %collective-permute-start.3 = (f32[6,8,2,128]{3,2,1,0:T(2,128)S(1)}, f32[6,8,2,128]{3,2,1,0:T(2,128)S(1)}, u32[]{:S(2)}, u32[]{:S(2)}) collective-permute-start(f32[6,8,2,128]{3,2,1,0:T(2,128)S(1)} %get-tuple-element.101), channel_id=1, source_target_pairs={{0,1},{1,0},{2,3},{3,2},{4,5},{5,4},{6,7},{7,6},{8,9},{9,8},{10,11... | collective-permute-start | bytes 147464 | tf_op jit(solution)/shard_map/ppermute | solution.py:919
  1.7 0.9 %shard_map.94 = (f32[6,16,128]{2,1,0:T(8,128)S(1)}, f32[3,4,8,16,128]{4,3,2,1,0:T(8,128)S(1)}) custom-call(f32[4,8,16,128]{3,2,1,0:T(8,128)S(1)} %get-tuple-element.102.state_ref, f32[8,16,128]{2,1,0:T(8,128)S(1)} %get-tuple-element.103.thick_ref, f32[8,16,128]{2,1,0:T(8,128)S(1)} %get-tuple-element.104.wet_ref, f32[2,24,128]{2,1,0:T(8,128)S(1)} %get-tuple-element.105.table_ref), custom_call_target="tpu_custom_call" | custom-call | flops 5898240 | bytes 835584 | tf_op jit(solution)/shard_map/pallas_call | solution.py:739
  2.6 0.0 collective-permute-done.3
  2.6 26.9 %conditional.1 = (f32[4,8,16,128]{3,2,1,0:T(8,128)}) conditional(s32[]{:T(128)} %convert_element_type.3, (s32[]{:T(128)}, f32[6,8,2,128]{3,2,1,0:T(2,128)S(1)}, f32[6,8,2,128]{3,2,1,0:T(2,128)S(1)}, f32[4,8,16,128]{3,2,1,0:T(8,128)S(1)}, f32[8,16,128]{2,1,0:T(8,128)S(1)}, /*index=5*/f32[8,16,128]{2,1,0:T(8,128)S(1)}, ...), branch_computations={%region_0.1_spmd, %region_1.2_spmd} | conditional | flops 7888908 | bytes 4718684 | solution.py:927
  2.6 0.0 copy-start
  2.6 0.0 copy-start.1
  2.6 0.0 copy-start.2
  2.6 0.8 %branch_1_fun.3 = (f32[4,8,16,128]{3,2,1,0:T(8,128)S(1)}, f32[8,40,128]{2,1,0:T(8,128)S(1)}) custom-call(f32[4,8,16,128]{3,2,1,0:T(8,128)S(1)} %get-tuple-element.65.state_ref, f32[8,16,128]{2,1,0:T(8,128)S(1)} %get-tuple-element.66.thick_ref, f32[8,16,128]{2,1,0:T(8,128)S(1)} %get-tuple-element.67.wet_ref, f32[6,8,2,128]{3,2,1,0:T(2,128)S(1)} %get-tuple-element.68.got_ref, ...), custom_call_target="tpu_custom_call" | custom-call | bytes 425984 | tf_op jit(solution)/shard_map/cond/branch_1_fun/pallas_call | solution.py:739
  3.5 14.6 %all_to_all.8.circle_ref = f32[8,40,128]{2,1,0:T(8,128)S(1)} all-to-all(f32[8,40,128]{2,1,0:T(8,128)S(1)} %get-tuple-element.74), channel_id=1, replica_groups=mesh['lon'=8,'lat'=4] {'lon'}, dimensions={0} | all-to-all | bytes 327680 | tf_op jit(solution)/shard_map/cond/branch_1_fun/all_to_all | solution.py:892
  18.1 0.0 copy-done
  18.1 0.0 copy-done.1
  18.1 0.9 %branch_1_fun.4 = f32[8,24,128]{2,1,0:T(8,128)S(1)} custom-call(f32[8,40,128]{2,1,0:T(8,128)S(1)} %all_to_all.8.circle_ref, f32[2,8,128]{2,1,0:T(8,128)S(1)} %get-tuple-element.75.table_ref, bf16[1024,256]{1,0:T(8,128)(2,1)S(1)} %copy-done, bf16[512,256]{1,0:T(8,128)(2,1)S(1)} %copy-done.1, f32[16,128]{1,0:T(8,128)S(1)} %get-tuple-element.78.count_ref), custom_call_target="tpu_custom_call" | custom-call | bytes 98304 | tf_op jit(solution)/shard_map/cond/branch_1_fun/pallas_call | solution.py:739
  19.0 9.5 %all_to_all.9.piece_ref = f32[8,24,128]{2,1,0:T(8,128)S(1)} all-to-all(f32[8,24,128]{2,1,0:T(8,128)S(1)} %branch_1_fun.4), channel_id=1, replica_groups=mesh['lon'=8,'lat'=4] {'lon'}, dimensions={0} | all-to-all | bytes 196608 | tf_op jit(solution)/shard_map/cond/branch_1_fun/all_to_all | solution.py:902
  28.5 0.0 copy-done.2
  28.5 1.0 %branch_1_fun.5 = f32[4,8,16,128]{3,2,1,0:T(8,128)} custom-call(f32[4,8,16,128]{3,2,1,0:T(8,128)S(1)} %get-tuple-element.73.state_ref, f32[8,24,128]{2,1,0:T(8,128)S(1)} %all_to_all.9.piece_ref, f32[8,16,128]{2,1,0:T(8,128)S(1)} %get-tuple-element.67.wet_ref, f32[16,128]{1,0:T(8,128)S(1)} %get-tuple-element.79.flag_ref, bf16[128,256]{1,0:T(8,128)(2,1)S(1)} %copy-done.2), custom_call_target="tpu_custom_call" | custom-call | bytes 262144 | tf_op jit(solution)/shard_map/cond/branch_1_fun/pallas_call | solution.py:739
Async XLA Ops:
  1.2 1.4 %collective-permute-start.3 = (f32[6,8,2,128]{3,2,1,0:T(2,128)S(1)}, f32[6,8,2,128]{3,2,1,0:T(2,128)S(1)}, u32[]{:S(2)}, u32[]{:S(2)}) collective-permute-start(f32[6,8,2,128]{3,2,1,0:T(2,128)S(1)} %get-tuple-element.101), channel_id=1, source_target_pairs={{0,1},{1,0},{2,3},{3,2},{4,5},{5,4},{6,7},{7,6},{8,9},{9,8},{10,11... | collective-permute-start | bytes 147464 | tf_op jit(solution)/shard_map/ppermute | solution.py:919
  2.6 15.5 %copy-start = (bf16[1024,256]{1,0:T(8,128)(2,1)S(1)}, bf16[1024,256]{1,0:T(8,128)(2,1)}, u32[]{:S(2)}) copy-start(bf16[1024,256]{1,0:T(8,128)(2,1)} %get-tuple-element.76.basis_ref) | copy-start | bytes 1572868 | tf_op jit(solution)/shard_map/cond
  2.6 15.5 %copy-start.1 = (bf16[512,256]{1,0:T(8,128)(2,1)S(1)}, bf16[512,256]{1,0:T(8,128)(2,1)}, u32[]{:S(2)}) copy-start(bf16[512,256]{1,0:T(8,128)(2,1)} %get-tuple-element.77.joint_basis_ref) | copy-start | bytes 786436 | tf_op jit(solution)/shard_map/cond
  2.6 25.9 %copy-start.2 = (bf16[128,256]{1,0:T(8,128)(2,1)S(1)}, bf16[128,256]{1,0:T(8,128)(2,1)}, u32[]{:S(2)}) copy-start(bf16[128,256]{1,0:T(8,128)(2,1)} %get-tuple-element.80.columns_ref) | copy-start | bytes 196612 | tf_op jit(solution)/shard_map/cond

commit v14 on v13

--- a/solution.py
+++ b/solution.py
@@ -372,6 +372,14 @@
     return jnp.concatenate([jnp.where(part == g, x, 0.0) for g in range(PACKED)], axis=0)
 
 
+def turned(tiles, place):
+    part = lane_of(tiles[0].shape) // SUMS
+    made = roll(tiles[0], -SUMS * place, 1)
+    for d in range(1, PACKED):
+        made = jnp.where(part == d, roll(tiles[d], SUMS * (d - place), 1), made)
+    return made
+
+
 def pack(x):
     size = x.shape[0] // PACKED
     made = x[:size]
@@ -557,7 +565,7 @@
 ):
     peers = circle_ref.shape[0]
     modes = basis_ref.shape[1] // 2
-    length = basis_ref.shape[0]
+    length = peers * LANES
     few = circle_ref.shape[1] - 24
     main = PACKED * few
     levels = main // 8
@@ -588,7 +596,10 @@
     at_level = lane_main // GROUP == row_main // 8
 
     def block(o):
-        return unpack(circle_ref[o, :few])
+        return jnp.concatenate(
+            [turned([circle_ref[PACKED * o + d, :few] for d in range(PACKED)], g) for g in range(PACKED)],
+            axis=0,
+        )
 
     def joint(j):
         x = joint_ref[8 * j : 8 * j + 8]
@@ -596,7 +607,7 @@
 
     total = jnp.zeros((2 * main, 2 * modes), jnp.float32)
     for source, basis, count in (
-        (block, basis_ref, peers),
+        (block, basis_ref, peers // PACKED),
         (joint, joint_basis_ref, peers // 2),
     ):
         for o in range(0, count, 2):
@@ -615,11 +626,13 @@
     weight = jnp.where(order < limit, jnp.where(order == 0.0, 1.0 / length, 2.0 / length), 0.0)
     total = (total[:, :modes] + total[:, modes:]) * weight
     y = jnp.concatenate([jnp.concatenate([p, p], axis=1) for p in split(total)], axis=0)
+    x = product(y, basis_ref[...], ((1,), (1,)))
+    x = x[:main] + x[main:]
+    for o in range(peers):
+        at = lanes * (o // PACKED)
+        tiles = [x[few * g : few * (g + 1), at : at + lanes] for g in range(PACKED)]
+        out_ref[o, :few] = turned(tiles, o % PACKED)
     for o in range(0, peers, 2):
-        x = product(y, basis_ref[lanes * o : lanes * (o + 2)], ((1,), (1,)))
-        x = x[:main] + x[main:]
-        out_ref[o, :few] = pack(x[:, :lanes])
-        out_ref[o + 1, :few] = pack(x[:, lanes:])
         before = (4 * o - 8) % (4 * peers)
         here = joint_ref[4 * o : 4 * o + 8]
         out_ref[o, few:] = jnp.where(
@@ -826,7 +839,7 @@
     cells = 4 * levels * full * lanes
     edge_rows = (6, levels, 2, lanes)
 
-    paired = rows == 2 * lon_peers and rows >= FBAND and lat_peers % 2 == 0 and levels % 2 == 0
+    paired = rows == 2 * lon_peers and lon_peers % (2 * PACKED) == 0 and rows >= FBAND and lat_peers % 2 == 0 and levels % 2 == 0
     columns = sequences(nlon, lanes, MAXM)
     if paired:
         coefficients, rest = block_coefficients(nlon, lanes, MAXM, columns)
@@ -870,7 +883,7 @@
     modes = mode_basis(nlon, MAXM)
     tables = [modes]
     if paired:
-        coefficients = np.concatenate([coefficients] * PACKED, axis=1).reshape(nlon, 2 * MAXM)
+        coefficients = coefficients.reshape(SUMS * lon_peers, 2 * MAXM)
         tables = [
             two_parts(coefficients),
             joint_basis(modes, lanes),

time: 29.7 us -> 29.8 us (level)
  no operation moved by 1% of the time
where the time goes in v14:
time: 29.8 us; the launch traced here: 29.5 us
  blocking collectives  24.1 us (81%)
  Pallas kernels  4.76 us (16%)
  starting transfers between devices  0.52 us (2%)
    all_to_all x1, blocking collectives, circled(): circles = lax.all_to_all(sent, 'lon', 0, 0, tiled=True)  14.6 us
    all_to_all x1, blocking collectives, circled(): pieces = lax.all_to_all(pieces, 'lon', 0, 0, tiled=True)  9.51 us
    pallas_call x5, Pallas kernels, run(): pl.pallas_call(kernel, out_shape=shapes, in_specs=[away if raw else vmem]...  4.76 us
  transfers between devices with their start and end apart: 1, of which 0 were waited for; matrix products, arithmetic and copies ran while one was open for 0% of the time, Pallas kernels for 3%

profile of v14, /device:TPU:0, one launch (start us, length us, event | category | flops | bytes accessed | tf_op | source)
XLA Modules:
  0.0 29.5 jit_solution(12253871880807341660)
XLA Ops:
  0.0 1.2 %shard_map.93 = (f32[4,8,16,128]{3,2,1,0:T(8,128)S(1)}, f32[8,16,128]{2,1,0:T(8,128)S(1)}, f32[8,16,128]{2,1,0:T(8,128)S(1)}, f32[6,8,2,128]{3,2,1,0:T(2,128)S(1...) custom-call(f32[4,8,16,128]{3,2,1,0:T(8,128)} %state_any.1, ...), custom_call_target="tpu_custom_call" | custom-call | bytes 614400 | tf_op jit(solution)/shard_map/pallas_call | solution.py:752
  1.2 0.5 %collective-permute-start.3 = (f32[6,8,2,128]{3,2,1,0:T(2,128)S(1)}, f32[6,8,2,128]{3,2,1,0:T(2,128)S(1)}, u32[]{:S(2)}, u32[]{:S(2)}) collective-permute-start(f32[6,8,2,128]{3,2,1,0:T(2,128)S(1)} %get-tuple-element.101), channel_id=1, source_target_pairs={{0,1},{1,0},{2,3},{3,2},{4,5},{5,4},{6,7},{7,6},{8,9},{9,8},{10,11... | collective-permute-start | bytes 147464 | tf_op jit(solution)/shard_map/ppermute | solution.py:932
  1.7 0.9 %shard_map.94 = (f32[6,16,128]{2,1,0:T(8,128)S(1)}, f32[3,4,8,16,128]{4,3,2,1,0:T(8,128)S(1)}) custom-call(f32[4,8,16,128]{3,2,1,0:T(8,128)S(1)} %get-tuple-element.102.state_ref, f32[8,16,128]{2,1,0:T(8,128)S(1)} %get-tuple-element.103.thick_ref, f32[8,16,128]{2,1,0:T(8,128)S(1)} %get-tuple-element.104.wet_ref, f32[2,24,128]{2,1,0:T(8,128)S(1)} %get-tuple-element.105.table_ref), custom_call_target="tpu_custom_call" | custom-call | flops 5898240 | bytes 835584 | tf_op jit(solution)/shard_map/pallas_call | solution.py:752
  2.6 0.0 collective-permute-done.3
  2.6 26.9 %conditional.1 = (f32[4,8,16,128]{3,2,1,0:T(8,128)}) conditional(s32[]{:T(128)} %convert_element_type.3, (s32[]{:T(128)}, f32[6,8,2,128]{3,2,1,0:T(2,128)S(1)}, f32[6,8,2,128]{3,2,1,0:T(2,128)S(1)}, f32[4,8,16,128]{3,2,1,0:T(8,128)S(1)}, f32[8,16,128]{2,1,0:T(8,128)S(1)}, /*index=5*/f32[8,16,128]{2,1,0:T(8,128)S(1)}, ...), branch_computations={%region_0.1_spmd, %region_1.2_spmd} | conditional | flops 7888908 | bytes 3145820 | solution.py:940
  2.6 0.0 copy-start
  2.6 0.0 copy-start.1
  2.6 0.0 copy-start.2
  2.6 0.8 %branch_1_fun.3 = (f32[4,8,16,128]{3,2,1,0:T(8,128)S(1)}, f32[8,40,128]{2,1,0:T(8,128)S(1)}) custom-call(f32[4,8,16,128]{3,2,1,0:T(8,128)S(1)} %get-tuple-element.65.state_ref, f32[8,16,128]{2,1,0:T(8,128)S(1)} %get-tuple-element.66.thick_ref, f32[8,16,128]{2,1,0:T(8,128)S(1)} %get-tuple-element.67.wet_ref, f32[6,8,2,128]{3,2,1,0:T(2,128)S(1)} %get-tuple-element.68.got_ref, ...), custom_call_target="tpu_custom_call" | custom-call | bytes 425984 | tf_op jit(solution)/shard_map/cond/branch_1_fun/pallas_call | solution.py:752
  3.5 14.6 %all_to_all.8.circle_ref = f32[8,40,128]{2,1,0:T(8,128)S(1)} all-to-all(f32[8,40,128]{2,1,0:T(8,128)S(1)} %get-tuple-element.74), channel_id=1, replica_groups=mesh['lon'=8,'lat'=4] {'lon'}, dimensions={0} | all-to-all | bytes 327680 | tf_op jit(solution)/shard_map/cond/branch_1_fun/all_to_all | solution.py:905
  18.1 0.0 copy-done
  18.1 0.0 copy-done.1
  18.1 0.9 %branch_1_fun.4 = f32[8,24,128]{2,1,0:T(8,128)S(1)} custom-call(f32[8,40,128]{2,1,0:T(8,128)S(1)} %all_to_all.8.circle_ref, f32[2,8,128]{2,1,0:T(8,128)S(1)} %get-tuple-element.75.table_ref, bf16[256,256]{1,0:T(8,128)(2,1)S(1)} %copy-done.1, bf16[512,256]{1,0:T(8,128)(2,1)S(1)} %copy-done, f32[16,128]{1,0:T(8,128)S(1)} %get-tuple-element.78.count_ref), custom_call_target="tpu_custom_call" | custom-call | bytes 98304 | tf_op jit(solution)/shard_map/cond/branch_1_fun/pallas_call | solution.py:752
  19.0 9.5 %all_to_all.9.piece_ref = f32[8,24,128]{2,1,0:T(8,128)S(1)} all-to-all(f32[8,24,128]{2,1,0:T(8,128)S(1)} %branch_1_fun.4), channel_id=1, replica_groups=mesh['lon'=8,'lat'=4] {'lon'}, dimensions={0} | all-to-all | bytes 196608 | tf_op jit(solution)/shard_map/cond/branch_1_fun/all_to_all | solution.py:915
  28.6 0.0 copy-done.2
  28.6 1.0 %branch_1_fun.5 = f32[4,8,16,128]{3,2,1,0:T(8,128)} custom-call(f32[4,8,16,128]{3,2,1,0:T(8,128)S(1)} %get-tuple-element.73.state_ref, f32[8,24,128]{2,1,0:T(8,128)S(1)} %all_to_all.9.piece_ref, f32[8,16,128]{2,1,0:T(8,128)S(1)} %get-tuple-element.67.wet_ref, f32[16,128]{1,0:T(8,128)S(1)} %get-tuple-element.79.flag_ref, bf16[128,256]{1,0:T(8,128)(2,1)S(1)} %copy-done.2), custom_call_target="tpu_custom_call" | custom-call | bytes 262144 | tf_op jit(solution)/shard_map/cond/branch_1_fun/pallas_call | solution.py:752
Async XLA Ops:
  1.2 1.4 %collective-permute-start.3 = (f32[6,8,2,128]{3,2,1,0:T(2,128)S(1)}, f32[6,8,2,128]{3,2,1,0:T(2,128)S(1)}, u32[]{:S(2)}, u32[]{:S(2)}) collective-permute-start(f32[6,8,2,128]{3,2,1,0:T(2,128)S(1)} %get-tuple-element.101), channel_id=1, source_target_pairs={{0,1},{1,0},{2,3},{3,2},{4,5},{5,4},{6,7},{7,6},{8,9},{9,8},{10,11... | collective-permute-start | bytes 147464 | tf_op jit(solution)/shard_map/ppermute | solution.py:932
  2.6 15.5 %copy-start = (bf16[512,256]{1,0:T(8,128)(2,1)S(1)}, bf16[512,256]{1,0:T(8,128)(2,1)}, u32[]{:S(2)}) copy-start(bf16[512,256]{1,0:T(8,128)(2,1)} %get-tuple-element.77.joint_basis_ref) | copy-start | bytes 786436 | tf_op jit(solution)/shard_map/cond
  2.6 15.5 %copy-start.1 = (bf16[256,256]{1,0:T(8,128)(2,1)S(1)}, bf16[256,256]{1,0:T(8,128)(2,1)}, u32[]{:S(2)}) copy-start(bf16[256,256]{1,0:T(8,128)(2,1)} %get-tuple-element.76.basis_ref) | copy-start | bytes 393220 | tf_op jit(solution)/shard_map/cond
  2.6 25.9 %copy-start.2 = (bf16[128,256]{1,0:T(8,128)(2,1)S(1)}, bf16[128,256]{1,0:T(8,128)(2,1)}, u32[]{:S(2)}) copy-start(bf16[128,256]{1,0:T(8,128)(2,1)} %get-tuple-element.80.columns_ref) | copy-start | bytes 196612 | tf_op jit(solution)/shard_map/cond

commit v15 on v13

--- a/solution.py
+++ b/solution.py
@@ -163,20 +163,19 @@
         ref[...] = jnp.broadcast_to(value, (rows, LANES))
     for k in range(levels):
         wet_ref[k] = raw_ref[k].astype(jnp.float32)
-    for copy in copies[3:]:
-        copy.wait()
-    for f in range(6):
+    even = lax.axis_index("lat") % 2 == 0
+    copies[3].wait()
+    copies[4].wait()
+    for f in (4, 5, 0, 1, 2, 3):
+        if f < 4:
+            copies[5 + f].wait()
         for k in range(levels):
             x = state_ref.at[f, k] if f < 4 else (thick_ref, wet_ref)[f - 4].at[k]
-            first_ref[f, k] = x[0:2]
-            last_ref[f, k] = x[rows - 2 : rows]
-    if paired:
-        even = lax.axis_index("lat") % 2 == 0
-        for f in range(6):
-            for k in range(levels):
-                low, high = first_ref[f, k], last_ref[f, k]
-                first_ref[f, k] = jnp.where(even, high, low)
-                last_ref[f, k] = jnp.where(even, low, high)
+            low, high = x[0:2], x[rows - 2 : rows]
+            if paired:
+                low, high = jnp.where(even, high, low), jnp.where(even, low, high)
+            first_ref[f, k] = low
+            last_ref[f, k] = high
 
 
 def ready_kernel(state_ref, thick_ref, wet_ref, table_ref, own_ref, term_ref):

time: 29.7 us -> 29.7 us (level)
  no operation moved by 1% of the time
where the time goes in v15:
time: 29.7 us; the launch traced here: 29.4 us
  blocking collectives  24.1 us (81%)
  Pallas kernels  4.67 us (16%)
  starting transfers between devices  0.52 us (2%)
    all_to_all x1, blocking collectives, circled(): circles = lax.all_to_all(sent, 'lon', 0, 0, tiled=True)  14.6 us
    all_to_all x1, blocking collectives, circled(): pieces = lax.all_to_all(pieces, 'lon', 0, 0, tiled=True)  9.51 us
    pallas_call x5, Pallas kernels, run(): pl.pallas_call(kernel, out_shape=shapes, in_specs=[away if raw else vmem]...  4.67 us
  transfers between devices with their start and end apart: 1, of which 0 were waited for; matrix products, arithmetic and copies ran while one was open for 0% of the time, Pallas kernels for 3%

profile of v15, /device:TPU:0, one launch (start us, length us, event | category | flops | bytes accessed | tf_op | source)
XLA Modules:
  0.0 29.4 jit_solution(11089973675928701672)
XLA Ops:
  0.0 1.1 %shard_map.93 = (f32[4,8,16,128]{3,2,1,0:T(8,128)S(1)}, f32[8,16,128]{2,1,0:T(8,128)S(1)}, f32[8,16,128]{2,1,0:T(8,128)S(1)}, f32[6,8,2,128]{3,2,1,0:T(2,128)S(1...) custom-call(f32[4,8,16,128]{3,2,1,0:T(8,128)} %state_any.1, ...), custom_call_target="tpu_custom_call" | custom-call | bytes 614400 | tf_op jit(solution)/shard_map/pallas_call | solution.py:738
  1.1 0.5 %collective-permute-start.3 = (f32[6,8,2,128]{3,2,1,0:T(2,128)S(1)}, f32[6,8,2,128]{3,2,1,0:T(2,128)S(1)}, u32[]{:S(2)}, u32[]{:S(2)}) collective-permute-start(f32[6,8,2,128]{3,2,1,0:T(2,128)S(1)} %get-tuple-element.101), channel_id=1, source_target_pairs={{0,1},{1,0},{2,3},{3,2},{4,5},{5,4},{6,7},{7,6},{8,9},{9,8},{10,11... | collective-permute-start | bytes 147464 | tf_op jit(solution)/shard_map/ppermute | solution.py:918
  1.7 0.9 %shard_map.94 = (f32[6,16,128]{2,1,0:T(8,128)S(1)}, f32[3,4,8,16,128]{4,3,2,1,0:T(8,128)S(1)}) custom-call(f32[4,8,16,128]{3,2,1,0:T(8,128)S(1)} %get-tuple-element.102.state_ref, f32[8,16,128]{2,1,0:T(8,128)S(1)} %get-tuple-element.103.thick_ref, f32[8,16,128]{2,1,0:T(8,128)S(1)} %get-tuple-element.104.wet_ref, f32[2,24,128]{2,1,0:T(8,128)S(1)} %get-tuple-element.105.table_ref), custom_call_target="tpu_custom_call" | custom-call | flops 5898240 | bytes 835584 | tf_op jit(solution)/shard_map/pallas_call | solution.py:738
  2.5 0.0 collective-permute-done.3
  2.5 26.9 %conditional.1 = (f32[4,8,16,128]{3,2,1,0:T(8,128)}) conditional(s32[]{:T(128)} %convert_element_type.3, (s32[]{:T(128)}, f32[6,8,2,128]{3,2,1,0:T(2,128)S(1)}, f32[6,8,2,128]{3,2,1,0:T(2,128)S(1)}, f32[4,8,16,128]{3,2,1,0:T(8,128)S(1)}, f32[8,16,128]{2,1,0:T(8,128)S(1)}, /*index=5*/f32[8,16,128]{2,1,0:T(8,128)S(1)}, ...), branch_computations={%region_0.1_spmd, %region_1.2_spmd} | conditional | flops 7888908 | bytes 4718684 | solution.py:926
  2.5 0.0 copy-start
  2.6 0.0 copy-start.1
  2.6 0.0 copy-start.2
  2.6 0.8 %branch_1_fun.3 = (f32[4,8,16,128]{3,2,1,0:T(8,128)S(1)}, f32[8,40,128]{2,1,0:T(8,128)S(1)}) custom-call(f32[4,8,16,128]{3,2,1,0:T(8,128)S(1)} %get-tuple-element.65.state_ref, f32[8,16,128]{2,1,0:T(8,128)S(1)} %get-tuple-element.66.thick_ref, f32[8,16,128]{2,1,0:T(8,128)S(1)} %get-tuple-element.67.wet_ref, f32[6,8,2,128]{3,2,1,0:T(2,128)S(1)} %get-tuple-element.68.got_ref, ...), custom_call_target="tpu_custom_call" | custom-call | bytes 425984 | tf_op jit(solution)/shard_map/cond/branch_1_fun/pallas_call | solution.py:738
  3.4 14.6 %all_to_all.8.circle_ref = f32[8,40,128]{2,1,0:T(8,128)S(1)} all-to-all(f32[8,40,128]{2,1,0:T(8,128)S(1)} %get-tuple-element.74), channel_id=1, replica_groups=mesh['lon'=8,'lat'=4] {'lon'}, dimensions={0} | all-to-all | bytes 327680 | tf_op jit(solution)/shard_map/cond/branch_1_fun/all_to_all | solution.py:891
  18.0 0.0 copy-done
  18.0 0.0 copy-done.1
  18.0 0.9 %branch_1_fun.4 = f32[8,24,128]{2,1,0:T(8,128)S(1)} custom-call(f32[8,40,128]{2,1,0:T(8,128)S(1)} %all_to_all.8.circle_ref, f32[2,8,128]{2,1,0:T(8,128)S(1)} %get-tuple-element.75.table_ref, bf16[1024,256]{1,0:T(8,128)(2,1)S(1)} %copy-done, bf16[512,256]{1,0:T(8,128)(2,1)S(1)} %copy-done.1, f32[16,128]{1,0:T(8,128)S(1)} %get-tuple-element.78.count_ref), custom_call_target="tpu_custom_call" | custom-call | bytes 98304 | tf_op jit(solution)/shard_map/cond/branch_1_fun/pallas_call | solution.py:738
  19.0 9.5 %all_to_all.9.piece_ref = f32[8,24,128]{2,1,0:T(8,128)S(1)} all-to-all(f32[8,24,128]{2,1,0:T(8,128)S(1)} %branch_1_fun.4), channel_id=1, replica_groups=mesh['lon'=8,'lat'=4] {'lon'}, dimensions={0} | all-to-all | bytes 196608 | tf_op jit(solution)/shard_map/cond/branch_1_fun/all_to_all | solution.py:901
  28.5 0.0 copy-done.2
  28.5 1.0 %branch_1_fun.5 = f32[4,8,16,128]{3,2,1,0:T(8,128)} custom-call(f32[4,8,16,128]{3,2,1,0:T(8,128)S(1)} %get-tuple-element.73.state_ref, f32[8,24,128]{2,1,0:T(8,128)S(1)} %all_to_all.9.piece_ref, f32[8,16,128]{2,1,0:T(8,128)S(1)} %get-tuple-element.67.wet_ref, f32[16,128]{1,0:T(8,128)S(1)} %get-tuple-element.79.flag_ref, bf16[128,256]{1,0:T(8,128)(2,1)S(1)} %copy-done.2), custom_call_target="tpu_custom_call" | custom-call | bytes 262144 | tf_op jit(solution)/shard_map/cond/branch_1_fun/pallas_call | solution.py:738
Async XLA Ops:
  1.1 1.4 %collective-permute-start.3 = (f32[6,8,2,128]{3,2,1,0:T(2,128)S(1)}, f32[6,8,2,128]{3,2,1,0:T(2,128)S(1)}, u32[]{:S(2)}, u32[]{:S(2)}) collective-permute-start(f32[6,8,2,128]{3,2,1,0:T(2,128)S(1)} %get-tuple-element.101), channel_id=1, source_target_pairs={{0,1},{1,0},{2,3},{3,2},{4,5},{5,4},{6,7},{7,6},{8,9},{9,8},{10,11... | collective-permute-start | bytes 147464 | tf_op jit(solution)/shard_map/ppermute | solution.py:918
  2.5 15.5 %copy-start = (bf16[1024,256]{1,0:T(8,128)(2,1)S(1)}, bf16[1024,256]{1,0:T(8,128)(2,1)}, u32[]{:S(2)}) copy-start(bf16[1024,256]{1,0:T(8,128)(2,1)} %get-tuple-element.76.basis_ref) | copy-start | bytes 1572868 | tf_op jit(solution)/shard_map/cond
  2.6 15.5 %copy-start.1 = (bf16[512,256]{1,0:T(8,128)(2,1)S(1)}, bf16[512,256]{1,0:T(8,128)(2,1)}, u32[]{:S(2)}) copy-start(bf16[512,256]{1,0:T(8,128)(2,1)} %get-tuple-element.77.joint_basis_ref) | copy-start | bytes 786436 | tf_op jit(solution)/shard_map/cond
  2.6 25.9 %copy-start.2 = (bf16[128,256]{1,0:T(8,128)(2,1)S(1)}, bf16[128,256]{1,0:T(8,128)(2,1)}, u32[]{:S(2)}) copy-start(bf16[128,256]{1,0:T(8,128)(2,1)} %get-tuple-element.80.columns_ref) | copy-start | bytes 196612 | tf_op jit(solution)/shard_map/cond

commit v16 on v15

--- a/solution.py
+++ b/solution.py
@@ -389,6 +389,13 @@
         place(y, made)
 
 
+def side_by_side(a, b):
+    c = lane_of(a.shape) % GROUP
+    one = jnp.where(c < 4, roll(a, -2, 1), roll(a, -4, 1))
+    two = jnp.where(c < 12, roll(b, 6, 1), roll(b, 4, 1))
+    return jnp.where(c < 8, one, two)
+
+
 def step_levels(buf_ref, term_ref, loop):
     levels, size = buf_ref.shape[2:4]
 
@@ -427,10 +434,12 @@
     def wet(k):
         return wet_ref[k]
 
-    for f in range(4):
-        own_ref[f] = own_columns(lambda k, f=f: state_ref[f, k], levels, lanes, rows)
-    own_ref[4] = own_columns(thick, levels, lanes, rows)
-    own_ref[5] = own_columns(wet, levels, lanes, rows)
+    tiles = [
+        own_columns(lambda k, f=f: state_ref[f, k], levels, lanes, rows) for f in range(4)
+    ]
+    tiles += [own_columns(load, levels, lanes, rows) for load in (thick, wet)]
+    for i in range(3):
+        own_ref[i] = side_by_side(tiles[2 * i], tiles[2 * i + 1])
     row_terms(thick, wet, table_ref[0, :rows], levels, term_ref)
     row = lax.broadcasted_iota(jnp.int32, (rows, LANES), 0)
     face = jnp.where(row < rows - 1, table_ref[1, :rows], 0.0)
@@ -477,8 +486,8 @@
     for f in range(6):
         for k in range(levels):
             halo = halo_ref[f, k]
-            beyond = jnp.where(sub < 6, roll(halo, 4, 0), 0.0)
-            high = jnp.where(sub < 4, roll(own(f, k, slice(rows - 8, rows)), -4, 0), beyond)
+            past = jnp.where(sub < 6, roll(halo, 4, 0), 0.0)
+            high = jnp.where(sub < 4, roll(own(f, k, slice(rows - 8, rows)), -4, 0), past)
             low = jnp.where(sub < 2, roll(halo, 2, 0), roll(own(f, k, slice(0, 8)), 2, 0))
             tile = jnp.where(top, high, low)
             if f < 4:
@@ -496,20 +505,15 @@
     for k in range(levels):
         term_ref[5, k], term_ref[6, k] = north_terms(thick(k), wet(k), table_ref[1])
     step_levels(buf_ref, term_ref, False)
-    c = lane_of((full, LANES)) % GROUP
-
-    def ring(f):
-        beyond = own_columns(lambda k: halo_ref[f, k], levels, lanes, 8)
-        return jnp.concatenate([own_ref[f], beyond], axis=0)
+
+    def beyond(f):
+        return own_columns(lambda k: halo_ref[f, k], levels, lanes, 8)
 
     for i in range(3):
-        a, b = ring(2 * i), ring(2 * i + 1)
-        one = jnp.where(c < 4, roll(a, -2, 1), roll(a, -4, 1))
-        two = jnp.where(c < 12, roll(b, 6, 1), roll(b, 4, 1))
-        both = jnp.where(c < 8, one, two)
-        raw_ref[i, 0:2] = both[full - 2 : full]
-        raw_ref[i, 2 : rows + 4] = both[: rows + 2]
-        raw_ref[i, rows + 4 : full] = jnp.zeros((4, LANES), jnp.float32)
+        outer = side_by_side(beyond(2 * i), beyond(2 * i + 1))
+        raw_ref[i, 0:2] = outer[6:8]
+        raw_ref[i, 2 : rows + 2] = own_ref[i]
+        raw_ref[i, rows + 2 : full] = outer[0:6]
     main = 8 * levels
     few = main // PACKED
     last = rows // 8 - 1
@@ -918,7 +922,7 @@
         got = lax.ppermute(first, "lat", [(i, i ^ 1) for i in range(lat_peers)])
         own, closed = call(
             closed_kernel,
-            [(6, rows, LANES), (3, 4, levels, rows, lanes)],
+            [(3, rows, LANES), (3, 4, levels, rows, lanes)],
             [(7, levels, rows, lanes)],
             flops=60 * cells,
         )(*block, table)

time: 29.7 us -> 29.7 us (level)
  no operation moved by 1% of the time
where the time goes in v16:
time: 29.7 us; the launch traced here: 29.4 us
  blocking collectives  24.1 us (81%)
  Pallas kernels  4.71 us (16%)
  starting transfers between devices  0.52 us (2%)
    all_to_all x1, blocking collectives, circled(): circles = lax.all_to_all(sent, 'lon', 0, 0, tiled=True)  14.6 us
    all_to_all x1, blocking collectives, circled(): pieces = lax.all_to_all(pieces, 'lon', 0, 0, tiled=True)  9.51 us
    pallas_call x5, Pallas kernels, run(): pl.pallas_call(kernel, out_shape=shapes, in_specs=[away if raw else vmem]...  4.71 us
  transfers between devices with their start and end apart: 1, of which 0 were waited for; matrix products, arithmetic and copies ran while one was open for 0% of the time, Pallas kernels for 3%

profile of v16, /device:TPU:0, one launch (start us, length us, event | category | flops | bytes accessed | tf_op | source)
XLA Modules:
  0.0 29.4 jit_solution(11756106433637559094)
XLA Ops:
  0.0 1.1 %shard_map.93 = (f32[4,8,16,128]{3,2,1,0:T(8,128)S(1)}, f32[8,16,128]{2,1,0:T(8,128)S(1)}, f32[8,16,128]{2,1,0:T(8,128)S(1)}, f32[6,8,2,128]{3,2,1,0:T(2,128)S(1...) custom-call(f32[4,8,16,128]{3,2,1,0:T(8,128)} %state_any.1, ...), custom_call_target="tpu_custom_call" | custom-call | bytes 614400 | tf_op jit(solution)/shard_map/pallas_call | solution.py:742
  1.1 0.5 %collective-permute-start.3 = (f32[6,8,2,128]{3,2,1,0:T(2,128)S(1)}, f32[6,8,2,128]{3,2,1,0:T(2,128)S(1)}, u32[]{:S(2)}, u32[]{:S(2)}) collective-permute-start(f32[6,8,2,128]{3,2,1,0:T(2,128)S(1)} %get-tuple-element.101), channel_id=1, source_target_pairs={{0,1},{1,0},{2,3},{3,2},{4,5},{5,4},{6,7},{7,6},{8,9},{9,8},{10,11... | collective-permute-start | bytes 147464 | tf_op jit(solution)/shard_map/ppermute | solution.py:922
  1.7 0.9 %shard_map.94 = (f32[3,16,128]{2,1,0:T(8,128)S(1)}, f32[3,4,8,16,128]{4,3,2,1,0:T(8,128)S(1)}) custom-call(f32[4,8,16,128]{3,2,1,0:T(8,128)S(1)} %get-tuple-element.102.state_ref, f32[8,16,128]{2,1,0:T(8,128)S(1)} %get-tuple-element.103.thick_ref, f32[8,16,128]{2,1,0:T(8,128)S(1)} %get-tuple-element.104.wet_ref, f32[2,24,128]{2,1,0:T(8,128)S(1)} %get-tuple-element.105.table_ref), custom_call_target="tpu_custom_call" | custom-call | flops 5898240 | bytes 811008 | tf_op jit(solution)/shard_map/pallas_call | solution.py:742
  2.6 0.0 collective-permute-done.3
  2.6 26.9 %conditional.1 = (f32[4,8,16,128]{3,2,1,0:T(8,128)}) conditional(s32[]{:T(128)} %convert_element_type.3, (s32[]{:T(128)}, f32[6,8,2,128]{3,2,1,0:T(2,128)S(1)}, f32[6,8,2,128]{3,2,1,0:T(2,128)S(1)}, f32[4,8,16,128]{3,2,1,0:T(8,128)S(1)}, f32[8,16,128]{2,1,0:T(8,128)S(1)}, /*index=5*/f32[8,16,128]{2,1,0:T(8,128)S(1)}, ...), branch_computations={%region_0.1_spmd, %region_1.2_spmd} | conditional | flops 7888908 | bytes 4718684 | solution.py:930
  2.6 0.0 copy-start
  2.6 0.0 copy-start.1
  2.6 0.0 copy-start.2
  2.6 0.8 %branch_1_fun.3 = (f32[4,8,16,128]{3,2,1,0:T(8,128)S(1)}, f32[8,40,128]{2,1,0:T(8,128)S(1)}) custom-call(f32[4,8,16,128]{3,2,1,0:T(8,128)S(1)} %get-tuple-element.65.state_ref, f32[8,16,128]{2,1,0:T(8,128)S(1)} %get-tuple-element.66.thick_ref, f32[8,16,128]{2,1,0:T(8,128)S(1)} %get-tuple-element.67.wet_ref, f32[6,8,2,128]{3,2,1,0:T(2,128)S(1)} %get-tuple-element.68.got_ref, ...), custom_call_target="tpu_custom_call" | custom-call | bytes 425984 | tf_op jit(solution)/shard_map/cond/branch_1_fun/pallas_call | solution.py:742
  3.4 14.6 %all_to_all.8.circle_ref = f32[8,40,128]{2,1,0:T(8,128)S(1)} all-to-all(f32[8,40,128]{2,1,0:T(8,128)S(1)} %get-tuple-element.74), channel_id=1, replica_groups=mesh['lon'=8,'lat'=4] {'lon'}, dimensions={0} | all-to-all | bytes 327680 | tf_op jit(solution)/shard_map/cond/branch_1_fun/all_to_all | solution.py:895
  18.0 0.0 copy-done
  18.0 0.0 copy-done.1
  18.0 0.9 %branch_1_fun.4 = f32[8,24,128]{2,1,0:T(8,128)S(1)} custom-call(f32[8,40,128]{2,1,0:T(8,128)S(1)} %all_to_all.8.circle_ref, f32[2,8,128]{2,1,0:T(8,128)S(1)} %get-tuple-element.75.table_ref, bf16[1024,256]{1,0:T(8,128)(2,1)S(1)} %copy-done, bf16[512,256]{1,0:T(8,128)(2,1)S(1)} %copy-done.1, f32[16,128]{1,0:T(8,128)S(1)} %get-tuple-element.78.count_ref), custom_call_target="tpu_custom_call" | custom-call | bytes 98304 | tf_op jit(solution)/shard_map/cond/branch_1_fun/pallas_call | solution.py:742
  19.0 9.5 %all_to_all.9.piece_ref = f32[8,24,128]{2,1,0:T(8,128)S(1)} all-to-all(f32[8,24,128]{2,1,0:T(8,128)S(1)} %branch_1_fun.4), channel_id=1, replica_groups=mesh['lon'=8,'lat'=4] {'lon'}, dimensions={0} | all-to-all | bytes 196608 | tf_op jit(solution)/shard_map/cond/branch_1_fun/all_to_all | solution.py:905
  28.5 0.0 copy-done.2
  28.5 1.0 %branch_1_fun.5 = f32[4,8,16,128]{3,2,1,0:T(8,128)} custom-call(f32[4,8,16,128]{3,2,1,0:T(8,128)S(1)} %get-tuple-element.73.state_ref, f32[8,24,128]{2,1,0:T(8,128)S(1)} %all_to_all.9.piece_ref, f32[8,16,128]{2,1,0:T(8,128)S(1)} %get-tuple-element.67.wet_ref, f32[16,128]{1,0:T(8,128)S(1)} %get-tuple-element.79.flag_ref, bf16[128,256]{1,0:T(8,128)(2,1)S(1)} %copy-done.2), custom_call_target="tpu_custom_call" | custom-call | bytes 262144 | tf_op jit(solution)/shard_map/cond/branch_1_fun/pallas_call | solution.py:742
Async XLA Ops:
  1.1 1.4 %collective-permute-start.3 = (f32[6,8,2,128]{3,2,1,0:T(2,128)S(1)}, f32[6,8,2,128]{3,2,1,0:T(2,128)S(1)}, u32[]{:S(2)}, u32[]{:S(2)}) collective-permute-start(f32[6,8,2,128]{3,2,1,0:T(2,128)S(1)} %get-tuple-element.101), channel_id=1, source_target_pairs={{0,1},{1,0},{2,3},{3,2},{4,5},{5,4},{6,7},{7,6},{8,9},{9,8},{10,11... | collective-permute-start | bytes 147464 | tf_op jit(solution)/shard_map/ppermute | solution.py:922
  2.6 15.4 %copy-start = (bf16[1024,256]{1,0:T(8,128)(2,1)S(1)}, bf16[1024,256]{1,0:T(8,128)(2,1)}, u32[]{:S(2)}) copy-start(bf16[1024,256]{1,0:T(8,128)(2,1)} %get-tuple-element.76.basis_ref) | copy-start | bytes 1572868 | tf_op jit(solution)/shard_map/cond
  2.6 15.4 %copy-start.1 = (bf16[512,256]{1,0:T(8,128)(2,1)S(1)}, bf16[512,256]{1,0:T(8,128)(2,1)}, u32[]{:S(2)}) copy-start(bf16[512,256]{1,0:T(8,128)(2,1)} %get-tuple-element.77.joint_basis_ref) | copy-start | bytes 786436 | tf_op jit(solution)/shard_map/cond
  2.6 25.8 %copy-start.2 = (bf16[128,256]{1,0:T(8,128)(2,1)S(1)}, bf16[128,256]{1,0:T(8,128)(2,1)}, u32[]{:S(2)}) copy-start(bf16[128,256]{1,0:T(8,128)(2,1)} %get-tuple-element.80.columns_ref) | copy-start | bytes 196612 | tf_op jit(solution)/shard_map/cond

commit v17 on v16

--- a/solution.py
+++ b/solution.py
@@ -98,7 +98,7 @@
         if k + 1 < levels:
             w_next, h_next = wet(k + 1), thick(k + 1)
             hs_next = jnp.where(w_next > 0, h_next, 1.0)
-            term_ref[4, k] = w * w_next * vertical_mix / (0.5 * (hs + hs_next))
+            term_ref[4, k] = w * w_next * (2.0 * vertical_mix) / (hs + hs_next)
             w, h, hs = w_next, h_next, hs_next
 
 
@@ -300,7 +300,7 @@
 
     hs = jnp.where(w > 0, h, 1.0)
     scale = time_step * w / hs
-    couple = w * deeper(w) * vertical_mix / (0.5 * (hs + deeper(hs)))
+    couple = w * deeper(w) * (2.0 * vertical_mix) / (hs + deeper(hs))
     couple = jnp.where(lane < GROUP * (levels - 1), couple, 0.0)
     terms = east_terms(h, w, inv_c) + north_terms(h, w, face)
     for i, term in enumerate(terms + (scale, scale * inv_c, couple)):

time: 29.7 us -> 29.7 us (level)
  no operation moved by 1% of the time
where the time goes in v17:
time: 29.7 us; the launch traced here: 29.4 us
  blocking collectives  24.1 us (81%)
  Pallas kernels  4.71 us (16%)
  starting transfers between devices  0.52 us (2%)
    all_to_all x1, blocking collectives, circled(): circles = lax.all_to_all(sent, 'lon', 0, 0, tiled=True)  14.6 us
    all_to_all x1, blocking collectives, circled(): pieces = lax.all_to_all(pieces, 'lon', 0, 0, tiled=True)  9.51 us
    pallas_call x5, Pallas kernels, run(): pl.pallas_call(kernel, out_shape=shapes, in_specs=[away if raw else vmem]...  4.71 us
  transfers between devices with their start and end apart: 1, of which 0 were waited for; matrix products, arithmetic and copies ran while one was open for 0% of the time, Pallas kernels for 3%

profile of v17, /device:TPU:0, one launch (start us, length us, event | category | flops | bytes accessed | tf_op | source)
XLA Modules:
  0.0 29.4 jit_solution(16421538489201988134)
XLA Ops:
  0.0 1.1 %shard_map.93 = (f32[4,8,16,128]{3,2,1,0:T(8,128)S(1)}, f32[8,16,128]{2,1,0:T(8,128)S(1)}, f32[8,16,128]{2,1,0:T(8,128)S(1)}, f32[6,8,2,128]{3,2,1,0:T(2,128)S(1...) custom-call(f32[4,8,16,128]{3,2,1,0:T(8,128)} %state_any.1, ...), custom_call_target="tpu_custom_call" | custom-call | bytes 614400 | tf_op jit(solution)/shard_map/pallas_call | solution.py:742
  1.1 0.5 %collective-permute-start.3 = (f32[6,8,2,128]{3,2,1,0:T(2,128)S(1)}, f32[6,8,2,128]{3,2,1,0:T(2,128)S(1)}, u32[]{:S(2)}, u32[]{:S(2)}) collective-permute-start(f32[6,8,2,128]{3,2,1,0:T(2,128)S(1)} %get-tuple-element.101), channel_id=1, source_target_pairs={{0,1},{1,0},{2,3},{3,2},{4,5},{5,4},{6,7},{7,6},{8,9},{9,8},{10,11... | collective-permute-start | bytes 147464 | tf_op jit(solution)/shard_map/ppermute | solution.py:922
  1.7 0.9 %shard_map.94 = (f32[3,16,128]{2,1,0:T(8,128)S(1)}, f32[3,4,8,16,128]{4,3,2,1,0:T(8,128)S(1)}) custom-call(f32[4,8,16,128]{3,2,1,0:T(8,128)S(1)} %get-tuple-element.102.state_ref, f32[8,16,128]{2,1,0:T(8,128)S(1)} %get-tuple-element.103.thick_ref, f32[8,16,128]{2,1,0:T(8,128)S(1)} %get-tuple-element.104.wet_ref, f32[2,24,128]{2,1,0:T(8,128)S(1)} %get-tuple-element.105.table_ref), custom_call_target="tpu_custom_call" | custom-call | flops 5898240 | bytes 811008 | tf_op jit(solution)/shard_map/pallas_call | solution.py:742
  2.6 0.0 collective-permute-done.3
  2.6 26.9 %conditional.1 = (f32[4,8,16,128]{3,2,1,0:T(8,128)}) conditional(s32[]{:T(128)} %convert_element_type.3, (s32[]{:T(128)}, f32[6,8,2,128]{3,2,1,0:T(2,128)S(1)}, f32[6,8,2,128]{3,2,1,0:T(2,128)S(1)}, f32[4,8,16,128]{3,2,1,0:T(8,128)S(1)}, f32[8,16,128]{2,1,0:T(8,128)S(1)}, /*index=5*/f32[8,16,128]{2,1,0:T(8,128)S(1)}, ...), branch_computations={%region_0.1_spmd, %region_1.2_spmd} | conditional | flops 7888908 | bytes 4718684 | solution.py:930
  2.6 0.0 copy-start
  2.6 0.0 copy-start.1
  2.6 0.0 copy-start.2
  2.6 0.8 %branch_1_fun.3 = (f32[4,8,16,128]{3,2,1,0:T(8,128)S(1)}, f32[8,40,128]{2,1,0:T(8,128)S(1)}) custom-call(f32[4,8,16,128]{3,2,1,0:T(8,128)S(1)} %get-tuple-element.65.state_ref, f32[8,16,128]{2,1,0:T(8,128)S(1)} %get-tuple-element.66.thick_ref, f32[8,16,128]{2,1,0:T(8,128)S(1)} %get-tuple-element.67.wet_ref, f32[6,8,2,128]{3,2,1,0:T(2,128)S(1)} %get-tuple-element.68.got_ref, ...), custom_call_target="tpu_custom_call" | custom-call | bytes 425984 | tf_op jit(solution)/shard_map/cond/branch_1_fun/pallas_call | solution.py:742
  3.4 14.6 %all_to_all.8.circle_ref = f32[8,40,128]{2,1,0:T(8,128)S(1)} all-to-all(f32[8,40,128]{2,1,0:T(8,128)S(1)} %get-tuple-element.74), channel_id=1, replica_groups=mesh['lon'=8,'lat'=4] {'lon'}, dimensions={0} | all-to-all | bytes 327680 | tf_op jit(solution)/shard_map/cond/branch_1_fun/all_to_all | solution.py:895
  18.0 0.0 copy-done
  18.0 0.0 copy-done.1
  18.0 0.9 %branch_1_fun.4 = f32[8,24,128]{2,1,0:T(8,128)S(1)} custom-call(f32[8,40,128]{2,1,0:T(8,128)S(1)} %all_to_all.8.circle_ref, f32[2,8,128]{2,1,0:T(8,128)S(1)} %get-tuple-element.75.table_ref, bf16[1024,256]{1,0:T(8,128)(2,1)S(1)} %copy-done, bf16[512,256]{1,0:T(8,128)(2,1)S(1)} %copy-done.1, f32[16,128]{1,0:T(8,128)S(1)} %get-tuple-element.78.count_ref), custom_call_target="tpu_custom_call" | custom-call | bytes 98304 | tf_op jit(solution)/shard_map/cond/branch_1_fun/pallas_call | solution.py:742
  19.0 9.5 %all_to_all.9.piece_ref = f32[8,24,128]{2,1,0:T(8,128)S(1)} all-to-all(f32[8,24,128]{2,1,0:T(8,128)S(1)} %branch_1_fun.4), channel_id=1, replica_groups=mesh['lon'=8,'lat'=4] {'lon'}, dimensions={0} | all-to-all | bytes 196608 | tf_op jit(solution)/shard_map/cond/branch_1_fun/all_to_all | solution.py:905
  28.5 0.0 copy-done.2
  28.5 1.0 %branch_1_fun.5 = f32[4,8,16,128]{3,2,1,0:T(8,128)} custom-call(f32[4,8,16,128]{3,2,1,0:T(8,128)S(1)} %get-tuple-element.73.state_ref, f32[8,24,128]{2,1,0:T(8,128)S(1)} %all_to_all.9.piece_ref, f32[8,16,128]{2,1,0:T(8,128)S(1)} %get-tuple-element.67.wet_ref, f32[16,128]{1,0:T(8,128)S(1)} %get-tuple-element.79.flag_ref, bf16[128,256]{1,0:T(8,128)(2,1)S(1)} %copy-done.2), custom_call_target="tpu_custom_call" | custom-call | bytes 262144 | tf_op jit(solution)/shard_map/cond/branch_1_fun/pallas_call | solution.py:742
Async XLA Ops:
  1.1 1.4 %collective-permute-start.3 = (f32[6,8,2,128]{3,2,1,0:T(2,128)S(1)}, f32[6,8,2,128]{3,2,1,0:T(2,128)S(1)}, u32[]{:S(2)}, u32[]{:S(2)}) collective-permute-start(f32[6,8,2,128]{3,2,1,0:T(2,128)S(1)} %get-tuple-element.101), channel_id=1, source_target_pairs={{0,1},{1,0},{2,3},{3,2},{4,5},{5,4},{6,7},{7,6},{8,9},{9,8},{10,11... | collective-permute-start | bytes 147464 | tf_op jit(solution)/shard_map/ppermute | solution.py:922
  2.6 15.4 %copy-start = (bf16[1024,256]{1,0:T(8,128)(2,1)S(1)}, bf16[1024,256]{1,0:T(8,128)(2,1)}, u32[]{:S(2)}) copy-start(bf16[1024,256]{1,0:T(8,128)(2,1)} %get-tuple-element.76.basis_ref) | copy-start | bytes 1572868 | tf_op jit(solution)/shard_map/cond
  2.6 15.4 %copy-start.1 = (bf16[512,256]{1,0:T(8,128)(2,1)S(1)}, bf16[512,256]{1,0:T(8,128)(2,1)}, u32[]{:S(2)}) copy-start(bf16[512,256]{1,0:T(8,128)(2,1)} %get-tuple-element.77.joint_basis_ref) | copy-start | bytes 786436 | tf_op jit(solution)/shard_map/cond
  2.6 25.9 %copy-start.2 = (bf16[128,256]{1,0:T(8,128)(2,1)S(1)}, bf16[128,256]{1,0:T(8,128)(2,1)}, u32[]{:S(2)}) copy-start(bf16[128,256]{1,0:T(8,128)(2,1)} %get-tuple-element.80.columns_ref) | copy-start | bytes 196612 | tf_op jit(solution)/shard_map/cond
